TPU v7x, 32 devices: a whole 2x2x4 slice. The times are simulated.
32 devices in a mesh: frames: 8 (over y, x, core), coils: 4 (over z).
Axes of the slice: x: 2, y: 2, z: 4, core: 2. Of those that a mesh axis runs over, the one named last changes fastest.
Arguments:
- kdata: bfloat16 [32, 32, 2, 13, 256], P('frames', 'coils'), may hold values from -6 to 6
- angles: int32 [32, 13], P('frames'), may hold values from 0 to 15
- kernels: bfloat16 [2, 16, 256, 128], replicated, may hold values from 0 to 1.5, as said below
- seg_bounds: int32 [2], replicated, may hold values from 64 to 191, as said below
- sensitivity: bfloat16 [32, 2, 128, 128], P('coils'), may hold values from -1 to 1
- ref_center: float32 [32, 2], P('coils'), may hold values from -24 to 24
- projection: float32 [3, 32], P(None, 'coils'), may hold values from -1 to 1
- init_coef: float32 [3], replicated, may hold values from -6 to 6
Outputs:
- image: float32 [32, 2, 128, 128], P('frames', None, 'coils')
- field_coef: float32 [32, 3], P('frames')
Inputs may be any that keep to these rules, and one draw needn't show every extreme that they name: `kernels`: entries are not negative. `seg_bounds`: strictly increasing; bound j lies within 21 of j * 85, counting j from 1.
All inputs are finite; a program needn't handle non-finite values.
Results may differ from a plain program's by a relative error of at most 0.0059.
Values sent between devices are 32-bit elements; how exact they have to be, the bound alone decides.
No kernel may reach another device: no remote copies, remote signals or barrier semaphores. Data moves between devices by JAX's collectives and lax.ppermute only.
A program may use at most 64 MiB of HBM per device.

v0:
```python
import math

import jax
import jax.numpy as jnp
from jax import lax
from jax.sharding import PartitionSpec as P


def from_behind(block, axis, distance):
    devices = range(lax.axis_size(axis))
    route = [(i - distance, i) for i in devices if i - distance in devices]
    return lax.ppermute(block, axis, route)


def entering(array, axis, combine, identity):
    devices, position = (lax.axis_size(axis), lax.axis_index(axis))
    everything = lax.all_gather(array, axis)
    start = jnp.broadcast_to(jnp.asarray(identity, array.dtype), array.shape)

    def turn(k, before):
        reached = k < position
        new = combine(before, everything[k])
        return jnp.where(reached, new, before)

    return lax.fori_loop(0, devices, turn, start)


def dft_tables(grid_side):
    offsets = jnp.arange(grid_side, dtype=jnp.int32) - grid_side // 2
    wrapped = jnp.mod(offsets[:, None] * offsets[None, :], grid_side).astype(jnp.float32)
    phase_arg = 2.0 * math.pi / grid_side * wrapped
    cosine = (jnp.cos(phase_arg) / grid_side).astype(jnp.bfloat16)
    sine = (jnp.sin(phase_arg) / grid_side).astype(jnp.bfloat16)
    right_table = jnp.stack([jnp.stack([cosine, sine]), jnp.stack([-sine, cosine])])
    left_table = jnp.stack([jnp.stack([cosine, -sine]), jnp.stack([sine, cosine])])
    return (right_table, left_table)


def segment_times(seg_bounds, readout):
    seg_edges = jnp.concatenate(
        [jnp.zeros((1,), jnp.int32), seg_bounds, jnp.full((1,), readout, jnp.int32)]
    )
    centers = (seg_edges[:-1] + seg_edges[1:] - 1).astype(jnp.float32) / (2.0 * readout)
    return (seg_edges, centers)


def window_width(readout, seg_count):
    spacing = readout // seg_count
    jitter = readout // (4 * seg_count)
    needed = max(spacing + 2 * jitter, readout - (seg_count - 1) * spacing + jitter)
    return min(readout, (needed + 127) // 128 * 128)


def modulate(partials, field_coef, seg_times, grid_side):
    row_count = partials.shape[-2]
    half_side = grid_side // 2
    row_pos = (jnp.arange(row_count, dtype=jnp.int32) - half_side).astype(jnp.float32) / half_side
    col_pos = (jnp.arange(grid_side, dtype=jnp.int32) - half_side).astype(jnp.float32) / half_side
    field_map = (
        field_coef[:, 0, None, None]
        + field_coef[:, 1, None, None] * row_pos[None, :, None]
        + field_coef[:, 2, None, None] * col_pos[None, None, :]
    )
    turned = field_map[:, None] * seg_times[None, :, None, None]
    cos_turn = jnp.cos(turned)
    sin_turn = jnp.sin(turned)
    real_part = jnp.sum(cos_turn * partials[:, :, 0] - sin_turn * partials[:, :, 1], axis=1)
    imag_part = jnp.sum(sin_turn * partials[:, :, 0] + cos_turn * partials[:, :, 1], axis=1)
    return jnp.stack([real_part, imag_part], axis=1)


def frame_images(
    frame_data, frame_angles, kernels, sensitivity, seg_edges, right_table, left_table
):
    readout = frame_data.shape[3]
    seg_count = seg_edges.shape[0] - 1
    width = window_width(readout, seg_count)
    weights_x = kernels[0][frame_angles]
    weights_y = kernels[1][frame_angles]
    weighted = frame_data[:, :, :, :, None] * weights_y[None, None]
    sens_real = sensitivity[:, 0].astype(jnp.float32)
    sens_imag = sensitivity[:, 1].astype(jnp.float32)
    results = []
    for segment in range(seg_count):
        start = jnp.minimum(seg_edges[segment], readout - width)
        window_index = start + jnp.arange(width, dtype=jnp.int32)
        inside = (window_index >= seg_edges[segment]) & (window_index < seg_edges[segment + 1])
        part_x = lax.dynamic_slice_in_dim(weights_x, start, width, 1)
        part_w = lax.dynamic_slice_in_dim(weighted, start, width, 3)
        masked_x = jnp.where(inside[None, :, None], part_x, jnp.zeros((), jnp.bfloat16))
        gridded = jnp.einsum(
            "srx,cpsry->xcpy", masked_x, part_w, preferred_element_type=jnp.float32
        ).astype(jnp.bfloat16)
        half_image = jnp.einsum(
            "xcpg,pqgy->xcqy", gridded, right_table, preferred_element_type=jnp.float32
        ).astype(jnp.bfloat16)
        coil_image = jnp.einsum(
            "qpzx,xcpy->cqzy", left_table, half_image, preferred_element_type=jnp.float32
        )
        combined_real = jnp.sum(sens_real * coil_image[:, 0] + sens_imag * coil_image[:, 1], axis=0)
        combined_imag = jnp.sum(sens_real * coil_image[:, 1] - sens_imag * coil_image[:, 0], axis=0)
        results.append(jnp.stack([combined_real, combined_imag]))
    return jnp.stack(results)


def add_terms(earlier, later):
    return earlier + later


def local(kdata, angles, kernels, seg_bounds, sensitivity, ref_center, projection, init_coef):
    readout = kdata.shape[4]
    grid_side = kernels.shape[3]
    center = jnp.sum(kdata[..., readout // 2].astype(jnp.float32), axis=3)
    arrived = from_behind(center[-1], "frames", 1)
    first_prev = jnp.where(lax.axis_index("frames") == 0, ref_center, arrived)
    previous = jnp.concatenate([first_prev[None], center[:-1]], axis=0)
    cross_term = previous[..., 0] * center[..., 1] - previous[..., 1] * center[..., 0]
    energy = jnp.sum(previous * previous, -1) + jnp.sum(center * center, -1) + 1.0
    drift_signal = 2.0 * cross_term / energy
    partial_step = jnp.dot(drift_signal, projection.T, precision=lax.Precision.HIGHEST)
    starting = jnp.zeros((partial_step.shape[1],), jnp.float32)
    increment = lax.psum(partial_step, "coils")
    before = entering(jnp.sum(increment, axis=0), "frames", add_terms, starting)
    field_coef = init_coef[None, :] + (before[None, :] + jnp.cumsum(increment, axis=0))
    seg_edges, seg_times = segment_times(seg_bounds, readout)
    right_table, left_table = dft_tables(grid_side)

    def per_frame(inputs):
        frame_data, frame_angles = inputs
        return frame_images(
            frame_data, frame_angles, kernels, sensitivity, seg_edges, right_table, left_table
        )

    partials = lax.map(per_frame, (kdata, angles))
    image = lax.psum_scatter(
        modulate(partials, field_coef, seg_times, grid_side),
        "coils",
        scatter_dimension=2,
        tiled=True,
    )
    return (image, field_coef)


def solution(mesh):
    placed = (
        P("frames", "coils", None, None, None),
        P("frames", None),
        P(),
        P(),
        P("coils", None, None, None),
        P("coils", None),
        P(None, "coils"),
        P(),
    )
    return jax.shard_map(
        local,
        mesh=mesh,
        in_specs=placed,
        out_specs=(P("frames", None, "coils", None), P("frames", None)),
        check_vma=False,
    )
```

profile of v0, /device:TPU:0, one launch (start us, length us, event | category | flops | bytes accessed | tf_op | source)
XLA Modules:
  0.0 237.6 jit_solution(6088395792456412168)
XLA Ops:
  8.6 2.4 %collective-permute-start = (f32[8,2]{0,1:T(2,128)S(1)}, f32[8,2]{0,1:T(2,128)S(1)}, u32[]{:S(2)}, u32[]{:S(2)}) collective-permute-start(f32[8,2]{0,1:T(2,128)S(1)} %bitcast.288), channel_id=1, source_target_pairs={{0,4},{4,8},{8,12},{12,16},{16,20},{20,24},{24,28},{1,5},{5,9},{9,... | collective-permute-start | bytes 200 | tf_op jit(solution)/shard_map/ppermute | solution.py:12
  11.0 1.3 fusion.135
  14.5 2.1 copy.94
  16.5 141.6 %while.26 = (s32[]{:T(128)}, f32[4,3,2,128,128]{3,4,2,1,0:T(8,128)}, bf16[8,2,128,128]{2,3,1,0:T(8,128)(2,1)}, s32[2]{0:T(128)}, bf16[2,16,256,128]{3,2,1,0:T(8,...) while((s32[]{:T(128)}, ...), condition=%wide.region_15.16_spmd, body=%wide.region_8.15_spmd.sunk | while | flops 3435186176 | bytes 59162972 | solution.py:134
  17.2 1.4 fusion.179
  21.5 1.7 slice_bitcast_fusion.7
  24.6 9.4 %broadcast_multiply_fusion.3 = bf16[8,2,13,256,128]{4,3,2,1,0:T(8,128)(2,1)} fusion(bf16[13,256,128]{2,1,0:T(8,128)(2,1)S(1)} %gather_fusion, bf16[8,2,13,256]{3,2,1,0:T(8,128)(2,1)S(1)} %bitcast.279), kind=kLoop, calls=%fused_computation.8.clone.1 | loop fusion | flops 6815744 | bytes 14589952 | tf_op jit(solution)/shard_map/while/body/eval_jaxpr/mul | solution.py:80
  34.0 4.4 %fusion.182 = bf16[128,8,2,128,1]{3,0,2,4,1:T(8,128)(2,1)S(1)} fusion(bf16[8,2,13,256,128]{4,3,2,1,0:T(8,128)(2,1)} %broadcast_multiply_fusion.3, bf16[13,256,128]{2,1,0:T(8,128)(2,1)S(1)} %gather_fusion.1, pred[128]{0:T(512)(128)(4,1)S(1)} %iota_compare_fusion.2, bf16[2,2,128,128]{3,2,0,1:T(8,128)(2,1)S(1)} %get-tuple-element.567), kind=kOutput, calls=%fused_computation.28.clone.1 | convolution fusion | flops 1007370240 | bytes 7897600 | tf_op jit(solution)/shard_map/while/body/eval_jaxpr/xcpg,pqgy->xcqy/dot_general | solution.py:94
  38.4 5.5 %fusion.181 = bf16[128,8,2,128,1]{3,0,2,4,1:T(8,128)(2,1)S(1)} fusion(bf16[8,2,13,256,128]{4,3,2,1,0:T(8,128)(2,1)} %broadcast_multiply_fusion.3, s32[]{:T(128)} %get-tuple-element.572, bf16[13,256,128]{2,1,0:T(8,128)(2,1)S(1)} %gather_fusion.1, pred[128]{0:T(512)(128)(4,1)S(1)} %get-tuple-element.521, ...), kind=kOutput, calls=%fused_computation.26.clone.1 | convolution fusion | flops 1007370240 | bytes 7898624 | tf_op jit(solution)/shard_map/while/body/eval_jaxpr/xcpg,pqgy->xcqy/dot_general | solution.py:94
  43.9 5.7 %fusion.180 = bf16[128,8,2,128,1]{3,0,2,4,1:T(8,128)(2,1)S(1)} fusion(bf16[8,2,13,256,128]{4,3,2,1,0:T(8,128)(2,1)} %broadcast_multiply_fusion.3, s32[]{:T(128)} %get-tuple-element.570, bf16[13,256,128]{2,1,0:T(8,128)(2,1)S(1)} %gather_fusion.1, pred[128]{0:T(512)(128)(4,1)S(1)} %get-tuple-element.520, ...), kind=kOutput, calls=%fused_computation.27.clone.1 | convolution fusion | flops 1007370240 | bytes 7898624 | tf_op jit(solution)/shard_map/while/body/eval_jaxpr/xcpg,pqgy->xcqy/dot_general | solution.py:94
  52.6 1.4 fusion.179
  56.9 1.7 slice_bitcast_fusion.7
  60.0 9.4 %broadcast_multiply_fusion.3 = bf16[8,2,13,256,128]{4,3,2,1,0:T(8,128)(2,1)} fusion(bf16[13,256,128]{2,1,0:T(8,128)(2,1)S(1)} %gather_fusion, bf16[8,2,13,256]{3,2,1,0:T(8,128)(2,1)S(1)} %bitcast.279), kind=kLoop, calls=%fused_computation.8.clone.1 | loop fusion | flops 6815744 | bytes 14589952 | tf_op jit(solution)/shard_map/while/body/eval_jaxpr/mul | solution.py:80
  69.4 4.4 %fusion.182 = bf16[128,8,2,128,1]{3,0,2,4,1:T(8,128)(2,1)S(1)} fusion(bf16[8,2,13,256,128]{4,3,2,1,0:T(8,128)(2,1)} %broadcast_multiply_fusion.3, bf16[13,256,128]{2,1,0:T(8,128)(2,1)S(1)} %gather_fusion.1, pred[128]{0:T(512)(128)(4,1)S(1)} %iota_compare_fusion.2, bf16[2,2,128,128]{3,2,0,1:T(8,128)(2,1)S(1)} %get-tuple-element.567), kind=kOutput, calls=%fused_computation.28.clone.1 | convolution fusion | flops 1007370240 | bytes 7897600 | tf_op jit(solution)/shard_map/while/body/eval_jaxpr/xcpg,pqgy->xcqy/dot_general | solution.py:94
  73.8 5.5 %fusion.181 = bf16[128,8,2,128,1]{3,0,2,4,1:T(8,128)(2,1)S(1)} fusion(bf16[8,2,13,256,128]{4,3,2,1,0:T(8,128)(2,1)} %broadcast_multiply_fusion.3, s32[]{:T(128)} %get-tuple-element.572, bf16[13,256,128]{2,1,0:T(8,128)(2,1)S(1)} %gather_fusion.1, pred[128]{0:T(512)(128)(4,1)S(1)} %get-tuple-element.521, ...), kind=kOutput, calls=%fused_computation.26.clone.1 | convolution fusion | flops 1007370240 | bytes 7898624 | tf_op jit(solution)/shard_map/while/body/eval_jaxpr/xcpg,pqgy->xcqy/dot_general | solution.py:94
  79.3 5.7 %fusion.180 = bf16[128,8,2,128,1]{3,0,2,4,1:T(8,128)(2,1)S(1)} fusion(bf16[8,2,13,256,128]{4,3,2,1,0:T(8,128)(2,1)} %broadcast_multiply_fusion.3, s32[]{:T(128)} %get-tuple-element.570, bf16[13,256,128]{2,1,0:T(8,128)(2,1)S(1)} %gather_fusion.1, pred[128]{0:T(512)(128)(4,1)S(1)} %get-tuple-element.520, ...), kind=kOutput, calls=%fused_computation.27.clone.1 | convolution fusion | flops 1007370240 | bytes 7898624 | tf_op jit(solution)/shard_map/while/body/eval_jaxpr/xcpg,pqgy->xcqy/dot_general | solution.py:94
  88.0 1.4 fusion.179
  92.3 1.7 slice_bitcast_fusion.7
  95.4 9.4 %broadcast_multiply_fusion.3 = bf16[8,2,13,256,128]{4,3,2,1,0:T(8,128)(2,1)} fusion(bf16[13,256,128]{2,1,0:T(8,128)(2,1)S(1)} %gather_fusion, bf16[8,2,13,256]{3,2,1,0:T(8,128)(2,1)S(1)} %bitcast.279), kind=kLoop, calls=%fused_computation.8.clone.1 | loop fusion | flops 6815744 | bytes 14589952 | tf_op jit(solution)/shard_map/while/body/eval_jaxpr/mul | solution.py:80
  104.8 4.4 %fusion.182 = bf16[128,8,2,128,1]{3,0,2,4,1:T(8,128)(2,1)S(1)} fusion(bf16[8,2,13,256,128]{4,3,2,1,0:T(8,128)(2,1)} %broadcast_multiply_fusion.3, bf16[13,256,128]{2,1,0:T(8,128)(2,1)S(1)} %gather_fusion.1, pred[128]{0:T(512)(128)(4,1)S(1)} %iota_compare_fusion.2, bf16[2,2,128,128]{3,2,0,1:T(8,128)(2,1)S(1)} %get-tuple-element.567), kind=kOutput, calls=%fused_computation.28.clone.1 | convolution fusion | flops 1007370240 | bytes 7897600 | tf_op jit(solution)/shard_map/while/body/eval_jaxpr/xcpg,pqgy->xcqy/dot_general | solution.py:94
  109.2 5.5 %fusion.181 = bf16[128,8,2,128,1]{3,0,2,4,1:T(8,128)(2,1)S(1)} fusion(bf16[8,2,13,256,128]{4,3,2,1,0:T(8,128)(2,1)} %broadcast_multiply_fusion.3, s32[]{:T(128)} %get-tuple-element.572, bf16[13,256,128]{2,1,0:T(8,128)(2,1)S(1)} %gather_fusion.1, pred[128]{0:T(512)(128)(4,1)S(1)} %get-tuple-element.521, ...), kind=kOutput, calls=%fused_computation.26.clone.1 | convolution fusion | flops 1007370240 | bytes 7898624 | tf_op jit(solution)/shard_map/while/body/eval_jaxpr/xcpg,pqgy->xcqy/dot_general | solution.py:94
  114.7 5.7 %fusion.180 = bf16[128,8,2,128,1]{3,0,2,4,1:T(8,128)(2,1)S(1)} fusion(bf16[8,2,13,256,128]{4,3,2,1,0:T(8,128)(2,1)} %broadcast_multiply_fusion.3, s32[]{:T(128)} %get-tuple-element.570, bf16[13,256,128]{2,1,0:T(8,128)(2,1)S(1)} %gather_fusion.1, pred[128]{0:T(512)(128)(4,1)S(1)} %get-tuple-element.520, ...), kind=kOutput, calls=%fused_computation.27.clone.1 | convolution fusion | flops 1007370240 | bytes 7898624 | tf_op jit(solution)/shard_map/while/body/eval_jaxpr/xcpg,pqgy->xcqy/dot_general | solution.py:94
  123.4 1.4 fusion.179
  127.7 1.7 slice_bitcast_fusion.7
  130.8 9.4 %broadcast_multiply_fusion.3 = bf16[8,2,13,256,128]{4,3,2,1,0:T(8,128)(2,1)} fusion(bf16[13,256,128]{2,1,0:T(8,128)(2,1)S(1)} %gather_fusion, bf16[8,2,13,256]{3,2,1,0:T(8,128)(2,1)S(1)} %bitcast.279), kind=kLoop, calls=%fused_computation.8.clone.1 | loop fusion | flops 6815744 | bytes 14589952 | tf_op jit(solution)/shard_map/while/body/eval_jaxpr/mul | solution.py:80
  140.2 4.4 %fusion.182 = bf16[128,8,2,128,1]{3,0,2,4,1:T(8,128)(2,1)S(1)} fusion(bf16[8,2,13,256,128]{4,3,2,1,0:T(8,128)(2,1)} %broadcast_multiply_fusion.3, bf16[13,256,128]{2,1,0:T(8,128)(2,1)S(1)} %gather_fusion.1, pred[128]{0:T(512)(128)(4,1)S(1)} %iota_compare_fusion.2, bf16[2,2,128,128]{3,2,0,1:T(8,128)(2,1)S(1)} %get-tuple-element.567), kind=kOutput, calls=%fused_computation.28.clone.1 | convolution fusion | flops 1007370240 | bytes 7897600 | tf_op jit(solution)/shard_map/while/body/eval_jaxpr/xcpg,pqgy->xcqy/dot_general | solution.py:94
  144.5 5.5 %fusion.181 = bf16[128,8,2,128,1]{3,0,2,4,1:T(8,128)(2,1)S(1)} fusion(bf16[8,2,13,256,128]{4,3,2,1,0:T(8,128)(2,1)} %broadcast_multiply_fusion.3, s32[]{:T(128)} %get-tuple-element.572, bf16[13,256,128]{2,1,0:T(8,128)(2,1)S(1)} %gather_fusion.1, pred[128]{0:T(512)(128)(4,1)S(1)} %get-tuple-element.521, ...), kind=kOutput, calls=%fused_computation.26.clone.1 | convolution fusion | flops 1007370240 | bytes 7898624 | tf_op jit(solution)/shard_map/while/body/eval_jaxpr/xcpg,pqgy->xcqy/dot_general | solution.py:94
  150.1 5.7 %fusion.180 = bf16[128,8,2,128,1]{3,0,2,4,1:T(8,128)(2,1)S(1)} fusion(bf16[8,2,13,256,128]{4,3,2,1,0:T(8,128)(2,1)} %broadcast_multiply_fusion.3, s32[]{:T(128)} %get-tuple-element.570, bf16[13,256,128]{2,1,0:T(8,128)(2,1)S(1)} %gather_fusion.1, pred[128]{0:T(512)(128)(4,1)S(1)} %get-tuple-element.520, ...), kind=kOutput, calls=%fused_computation.27.clone.1 | convolution fusion | flops 1007370240 | bytes 7898624 | tf_op jit(solution)/shard_map/while/body/eval_jaxpr/xcpg,pqgy->xcqy/dot_general | solution.py:94
  160.7 12.8 %psum.7 = f32[4,3]{0,1:T(4,128)S(1)} all-reduce(f32[4,3]{0,1:T(4,128)S(1)} %fusion.128), channel_id=1, replica_groups=mesh['frames'=8,'coils'=4] {'coils'}, use_global_device_ids=true, to_apply=%region_3.4 | all-reduce | flops 12 | bytes 96 | tf_op jit(solution)/shard_map/psum | solution.py:122
  174.0 11.8 %all-reduce = f32[24]{0:T(128)S(1)} all-reduce(f32[24]{0:T(128)S(1)} %dynamic-update-slice), channel_id=2, replica_groups=mesh['frames'=8,'coils'=4] {'frames'}, use_global_device_ids=true, to_apply=%add | all-reduce | flops 24 | bytes 192
  186.5 4.6 %fusion.108 = (f32[4,128,128]{1,2,0:T(8,128)S(1)}, f32[4,128,128]{1,2,0:T(8,128)S(1)}) fusion(f32[4,3,2,128,128]{3,4,2,1,0:T(8,128)} %get-tuple-element.210, f32[3]{0:T(128)S(1)} %fusion.132, f32[4,128,128]{1,2,0:T(8,128)S(1)} %broadcast_add_fusion), kind=kLoop, calls=%fused_computation.105 | loop fusion | flops 1638400 | bytes 2359308 | tf_op jit(solution)/shard_map/reduce_sum | solution.py:67
  194.2 35.0 %all-reduce.4.cloned.1.call-done = f32[4,2,128,128]{3,0,1,2:T(4,128)} async-done(((f32[4,2,128,128]{3,0,1,2:T(4,128)}), f32[4,2,128,128]{3,0,1,2:T(4,128)}) %all-reduce.4.cloned.1.call-update) | async-done | bytes 524304
  (129 shorter events, 38.3 us)
Async XLA Ops:
  7.2 152.7 %copy-start = (f32[3,8]{1,0:T(4,128)S(1)}, f32[3,8]{1,0:T(4,128)}, u32[]{:S(2)}) copy-start(f32[3,8]{1,0:T(4,128)} %param.18) | copy-start | bytes 292
  7.2 222.0 %all-reduce.4.cloned.1.call-start = ((), (), s32[]{:S(2)}) async-start(), calls=%async_computation | async-start | bytes 1048576
  8.6 151.0 %collective-permute-start = (f32[8,2]{0,1:T(2,128)S(1)}, f32[8,2]{0,1:T(2,128)S(1)}, u32[]{:S(2)}, u32[]{:S(2)}) collective-permute-start(f32[8,2]{0,1:T(2,128)S(1)} %bitcast.288), channel_id=1, source_target_pairs={{0,4},{4,8},{8,12},{12,16},{16,20},{20,24},{24,28},{1,5},{5,9},{9,... | collective-permute-start | bytes 200 | tf_op jit(solution)/shard_map/ppermute | solution.py:12
  16.5 142.4 %copy-start.5 = (u32[32]{0:T(128)S(1)}, u32[32]{0:T(128)}, u32[]{:S(2)}) copy-start(u32[32]{0:T(128)} %constant.129) | copy-start | bytes 388
  16.5 143.0 %copy-start.2 = (f32[8,2]{0,1:T(2,128)S(1)}, f32[8,2]{0,1:T(2,128)}, u32[]{:S(2)}) copy-start(f32[8,2]{0,1:T(2,128)} %param.17) | copy-start | bytes 196
  16.5 169.7 %copy-start.3 = (f32[3]{0:T(128)S(1)}, f32[3]{0:T(128)}, u32[]{:S(2)}) copy-start(f32[3]{0:T(128)} %param.19) | copy-start | bytes 40
  16.5 175.7 %copy-start.4 = (u32[32]{0:T(128)S(1)}, u32[32]{0:T(128)}, u32[]{:S(2)}) copy-start(u32[32]{0:T(128)} %constant.135) | copy-start | bytes 388
  43.9 6.8 %copy-start.1 = (bf16[8,2,128,128]{2,3,1,0:T(8,128)(2,1)S(1)}, bf16[8,2,128,128]{2,3,1,0:T(8,128)(2,1)}, u32[]{:S(2)}) copy-start(bf16[8,2,128,128]{2,3,1,0:T(8,128)(2,1)} %get-tuple-element.562) | copy-start | bytes 1572868 | tf_op jit(solution)/shard_map/while
  79.3 6.7 %copy-start.1 = (bf16[8,2,128,128]{2,3,1,0:T(8,128)(2,1)S(1)}, bf16[8,2,128,128]{2,3,1,0:T(8,128)(2,1)}, u32[]{:S(2)}) copy-start(bf16[8,2,128,128]{2,3,1,0:T(8,128)(2,1)} %get-tuple-element.562) | copy-start | bytes 1572868 | tf_op jit(solution)/shard_map/while
  114.7 6.8 %copy-start.1 = (bf16[8,2,128,128]{2,3,1,0:T(8,128)(2,1)S(1)}, bf16[8,2,128,128]{2,3,1,0:T(8,128)(2,1)}, u32[]{:S(2)}) copy-start(bf16[8,2,128,128]{2,3,1,0:T(8,128)(2,1)} %get-tuple-element.562) | copy-start | bytes 1572868 | tf_op jit(solution)/shard_map/while
  150.1 6.7 %copy-start.1 = (bf16[8,2,128,128]{2,3,1,0:T(8,128)(2,1)S(1)}, bf16[8,2,128,128]{2,3,1,0:T(8,128)(2,1)}, u32[]{:S(2)}) copy-start(bf16[8,2,128,128]{2,3,1,0:T(8,128)(2,1)} %get-tuple-element.562) | copy-start | bytes 1572868 | tf_op jit(solution)/shard_map/while
Sparse Core Ops, SparseCore 0:
  192.4 36.7 all-reduce.3
where the time goes:
time: 239 us; the launch traced here: 238 us
  matrix products  66.5 us (28%)
  other arithmetic  61.2 us (26%)
  waiting for transfers between devices  35 us (15%)
  local copies, waits for them, and re-layouts  30.3 us (13%)
  blocking collectives  24.6 us (10%)
  between operations  16.9 us (7%)
  starting transfers between devices  2.42 us (1%)
    dot_general x12, matrix products, frame_images(): jnp.einsum('xcpg,pqgy->xcqy', gridded, right_table, preferred_element_typ...  62.2 us
    mul x4, other arithmetic, frame_images(): weighted = frame_data[:, :, :, :, None] * weights_y[None, None]  37.5 us
    unnamed x2, waiting for transfers between devices  35 us
    psum x1, blocking collectives, local(): increment = lax.psum(partial_step, 'coils')  12.8 us
    unnamed x1, blocking collectives  11.8 us
    slice x5, local copies, waits for them, and re-layouts, frame_images(): seg_edges[segment + 1]  6.89 us
    squeeze x4, local copies, waits for them, and re-layouts, frame_images(): weights_x = kernels[0][frame_angles]  6.72 us
    and x4, other arithmetic, frame_images(): (window_index >= seg_edges[segment]) & (window_index < seg_edges[segment...  5.01 us
  transfers between devices with their start and end apart: 2, of which 1 were waited for; matrix products, arithmetic and copies ran while one was open for 62% of the time, Pallas kernels for 0%

commit v1 on v0

v1 whole, which is shorter than its diff:
```python
import functools
import math

import jax
import jax.numpy as jnp
import ml_dtypes
import numpy as np
from jax import lax
from jax.experimental import pallas as pl
from jax.experimental.pallas import tpu as pltpu
from jax.sharding import PartitionSpec as P

BF16 = jnp.bfloat16
F32 = jnp.float32


def dft_tables(side):
    offsets = np.arange(side) - side // 2
    wrapped = np.mod(offsets[:, None] * offsets[None, :], side).astype(np.float32)
    phase = np.float32(2.0 * math.pi / side) * wrapped
    cosine = (np.cos(phase) / np.float32(side)).astype(ml_dtypes.bfloat16)
    sine = (np.sin(phase) / np.float32(side)).astype(ml_dtypes.bfloat16)
    right = np.block([[cosine, sine], [-sine, cosine]])
    left = np.block([[cosine, -sine], [sine, cosine]])
    return right, left


def windows(readout, segs):
    spacing, jitter = readout // segs, readout // (4 * segs)
    low = [0] + [j * spacing - jitter for j in range(1, segs)]
    high = [j * spacing + jitter for j in range(1, segs)] + [readout]
    width = 128
    while True:
        starts = [max(0, min(a // 16 * 16, readout - width)) for a in low]
        if all(s + width >= b for s, b in zip(starts, high)) or width >= readout:
            return starts, min(width, readout)
        width += 128


def edges_of(bounds_ref, readout, segs):
    return [0] + [bounds_ref[j] for j in range(segs - 1)] + [readout]


def prepare(starts, width, bounds_ref, kdata_ref, kx_ref, rows_ref, center_ref):
    angles, readout, side = kx_ref.shape
    segs = len(starts)
    edges = edges_of(bounds_ref, readout, segs)
    index = lax.broadcasted_iota(jnp.int32, (side, width), 1)
    keep = []
    for l in range(segs):
        at = index + starts[l]
        keep.append((at >= edges[l]) & (at < edges[l + 1]))

    def one(a, carry):
        for l in range(segs):
            part = kx_ref[a, starts[l] : starts[l] + width, :].astype(F32)
            rows_ref[a, l] = jnp.where(keep[l], part.T, 0.0).astype(BF16)
        return carry

    lax.fori_loop(0, angles, one, 0)
    half = readout // 2
    lanes = center_ref.shape[-1]
    for t in range(kdata_ref.shape[0]):
        for c in range(kdata_ref.shape[1]):
            total = jnp.zeros((2, lanes), F32)
            for s in range(kdata_ref.shape[2]):
                total += kdata_ref[t, c, s, :, half : half + lanes].astype(F32)
            center_ref[t, 0, c, :] = total[0]
            center_ref[t, 1, c, :] = total[1]


def drift(position_ref, center_ref, arrived_ref, first_ref, projection_ref, step_ref):
    frames, _, coils, lanes = center_ref.shape
    basis = projection_ref.shape[0]
    at_start = position_ref[0] == 0
    for t in range(frames):
        if t == 0:
            before = [jnp.where(at_start, first_ref[p], arrived_ref[p]) for p in range(2)]
        else:
            before = [center_ref[t - 1, p] for p in range(2)]
        now = [center_ref[t, p] for p in range(2)]
        cross = before[0] * now[1] - before[1] * now[0]
        energy = before[0] * before[0] + before[1] * before[1]
        energy = energy + (now[0] * now[0] + now[1] * now[1]) + 1.0
        signal = 2.0 * cross / energy
        for b in range(basis):
            row = jnp.sum(projection_ref[b] * signal, axis=0, keepdims=True)
            step_ref[pl.ds(t * basis + b, 1), :] = row


def grid_frames(
    starts, width, angles_ref, kdata_ref, rows_ref, ky_ref, right_ref, left_ref, sens_ref,
    out_ref, kd_ref, lhs_ref, turned_ref, weighted_ref, half_ref, *, first
):
    coils, spokes, _, readout = kdata_ref.shape
    segs = len(starts)
    side = ky_ref.shape[2]
    t = pl.program_id(0) + first
    slots = kd_ref.shape[1] // 2
    for s in range(spokes):
        a = angles_ref[t, s]
        for l in range(segs):
            lhs_ref[l, :, s * width : (s + 1) * width] = rows_ref[a, l]
        for c in range(coils):
            kd_ref[c, 2 * s : 2 * s + 2, :] = kdata_ref[c, s].astype(F32)
    per = min(128 // (2 * slots), coils)
    for g in range(coils // per):
        block = kd_ref[g * per : (g + 1) * per].reshape(per * 2 * slots, readout)
        flipped = block.T
        for j in range(per):
            turned_ref[g * per + j, :, : 2 * slots] = flipped[:, j * 2 * slots : (j + 1) * 2 * slots].astype(BF16)
    out_ref[...] = jnp.zeros_like(out_ref)

    def coil(c, carry):
        columns = turned_ref[c]
        for s in range(spokes):
            ky = ky_ref[angles_ref[t, s]]
            for p in range(2):
                scale = jnp.broadcast_to(columns[:, 2 * s + p : 2 * s + p + 1], (readout, side))
                weighted_ref[s, :, p * side : (p + 1) * side] = scale * ky
        for l in range(segs):
            rhs = weighted_ref[:, starts[l] : starts[l] + width, :].reshape(spokes * width, 2 * side)
            gridded = jnp.dot(lhs_ref[l], rhs, preferred_element_type=F32).astype(BF16)
            half = jnp.dot(gridded, right_ref[...], preferred_element_type=F32).astype(BF16)
            half_ref[:side, l * side : (l + 1) * side] = half[:, :side]
            half_ref[side:, l * side : (l + 1) * side] = half[:, side:]
        image = jnp.dot(left_ref[...], half_ref[...], preferred_element_type=F32)
        real = sens_ref[c, 0].astype(F32)
        imag = sens_ref[c, 1].astype(F32)
        for l in range(segs):
            re = image[:side, l * side : (l + 1) * side]
            im = image[side:, l * side : (l + 1) * side]
            out_ref[l, 0] += real * re + imag * im
            out_ref[l, 1] += real * im - imag * re
        return carry

    lax.fori_loop(0, coils, coil, 0)


def modulate(side, readout, position_ref, bounds_ref, coef_ref, parts_ref, *out_refs):
    segs = parts_ref.shape[1]
    owners = len(out_refs)
    rows = side // owners
    half = side // 2
    me = position_ref[0]
    edges = edges_of(bounds_ref, readout, segs)
    times = [(edges[l] + edges[l + 1] - 1).astype(F32) / (2.0 * readout) for l in range(segs)]
    t = pl.program_id(0)
    f0, f1, f2 = coef_ref[t, 0], coef_ref[t, 1], coef_ref[t, 2]
    col = (lax.broadcasted_iota(jnp.int32, (8, side), 1) - half).astype(F32) / half
    pos = (lax.broadcasted_iota(jnp.int32, (side, 128), 0) - half).astype(F32) / half
    factors = []
    for l in range(segs):
        down = (f0 + f1 * pos) * times[l]
        across = (f2 * col) * times[l]
        factors.append((jnp.cos(down)[:, :1], jnp.sin(down)[:, :1], jnp.cos(across)[:1], jnp.sin(across)[:1]))
    image_re = jnp.zeros((side, side), F32)
    image_im = jnp.zeros((side, side), F32)
    for l in range(segs):
        cr, sr, cc, sc = factors[l]
        cos = cr * cc - sr * sc
        sin = sr * cc + cr * sc
        re, im = parts_ref[0, l, 0], parts_ref[0, l, 1]
        image_re += cos * re - sin * im
        image_im += sin * re + cos * im
    for owner in range(owners):
        for d, out_ref in enumerate(out_refs):

            @pl.when(lax.rem(me + d, owners) == owner)
            def _():
                out_ref[0, 0] = image_re[owner * rows : (owner + 1) * rows]
                out_ref[0, 1] = image_im[owner * rows : (owner + 1) * rows]


def shifted(block, axis, distance):
    count = lax.axis_size(axis)
    return lax.ppermute(block, axis, [(i, i + distance) for i in range(count - distance)])


def around(block, axis, distance):
    count = lax.axis_size(axis)
    return lax.ppermute(block, axis, [(i, (i + distance) % count) for i in range(count)])


def local(kdata, angles, kernels, seg_bounds, sensitivity, ref_center, projection, init_coef):
    frames, coils, _, spokes, readout = kdata.shape
    table, side = kernels.shape[1], kernels.shape[3]
    segs = seg_bounds.shape[0] + 1
    basis = projection.shape[0]
    owners = lax.axis_size("coils")
    starts, width = windows(readout, segs)
    right, left = (jnp.asarray(table) for table in dft_tables(side))
    kd = jnp.swapaxes(kdata, 2, 3)
    smem = pl.BlockSpec(memory_space=pltpu.SMEM)
    vmem = pl.BlockSpec(memory_space=pltpu.VMEM)
    place = lax.axis_index("frames").astype(jnp.int32).reshape(1)
    owner = lax.axis_index("coils").astype(jnp.int32).reshape(1)

    rows, center = pl.pallas_call(
        functools.partial(prepare, starts, width),
        out_shape=(
            jax.ShapeDtypeStruct((table, segs, side, width), BF16),
            jax.ShapeDtypeStruct((frames, 2, coils, 128), F32),
        ),
        in_specs=[smem, vmem, vmem],
        out_specs=(vmem, vmem),
        name="prepare",
    )(seg_bounds, kd, kernels[0])

    arrived = shifted(center[-1], "frames", 1)
    first = jnp.broadcast_to(ref_center.T[:, :, None], (2, coils, 128))
    weights = jnp.broadcast_to(projection[:, :, None], (basis, coils, 128))
    step = pl.pallas_call(
        drift,
        out_shape=jax.ShapeDtypeStruct((frames * basis, 128), F32),
        in_specs=[smem, vmem, vmem, vmem, vmem],
        out_specs=vmem,
        name="drift",
    )(place, center, arrived, first, weights)
    step = step[:, :1].reshape(frames, basis)
    distance = 1
    increment = step
    while distance < owners:
        pairs = [(i, i ^ distance) for i in range(owners)]
        increment = increment + lax.ppermute(increment, "coils", pairs)
        distance *= 2
    running = jnp.sum(increment, axis=0)
    before = jnp.zeros_like(running)
    distance = 1
    while distance < lax.axis_size("frames"):
        came = shifted(running, "frames", distance)
        running, before = running + came, before + came
        distance *= 2
    field_coef = init_coef[None, :] + (before[None, :] + jnp.cumsum(increment, axis=0))

    def gridded(begin, end):
        count = end - begin
        grid_spec = pltpu.PrefetchScalarGridSpec(
            num_scalar_prefetch=1,
            grid=(count,),
            in_specs=[
                pl.BlockSpec((None, coils, spokes, 2, readout), lambda i, _: (begin + i, 0, 0, 0, 0)),
                vmem,
                pl.BlockSpec((None, table, readout, side), lambda i, _: (1, 0, 0, 0)),
                vmem,
                vmem,
                vmem,
            ],
            out_specs=pl.BlockSpec((None, segs, 2, side, side), lambda i, _: (i, 0, 0, 0, 0)),
            scratch_shapes=[
                pltpu.VMEM((coils, 32, readout), F32),
                pltpu.VMEM((segs, side, spokes * width), BF16),
                pltpu.VMEM((coils, readout, 128), BF16),
                pltpu.VMEM((spokes, readout, 2 * side), BF16),
                pltpu.VMEM((2 * side, segs * side), BF16),
            ],
        )
        return pl.pallas_call(
            functools.partial(grid_frames, starts, width, first=begin),
            out_shape=jax.ShapeDtypeStruct((count, segs, 2, side, side), F32),
            grid_spec=grid_spec,
            name="gridding",
        )(angles, kd, rows, kernels, right, left, sensitivity)

    def images(parts, coef):
        count = parts.shape[0]
        block = jax.ShapeDtypeStruct((count, 2, side // owners, side), F32)
        spec = pl.BlockSpec((1, 2, side // owners, side), lambda i: (i, 0, 0, 0))
        blocks = pl.pallas_call(
            functools.partial(modulate, side, readout),
            out_shape=(block,) * owners,
            grid=(count,),
            in_specs=[smem, smem, smem, pl.BlockSpec((1, segs, 2, side, side), lambda i: (i, 0, 0, 0, 0))],
            out_specs=(spec,) * owners,
            name="modulate",
        )(owner, seg_bounds, coef, parts)
        total = blocks[0]
        for d in range(1, owners):
            total = total + around(blocks[d], "coils", d)
        return total

    image = images(gridded(0, frames), field_coef)
    return (image, field_coef)


def solution(mesh):
    placed = (
        P("frames", "coils", None, None, None),
        P("frames", None),
        P(),
        P(),
        P("coils", None, None, None),
        P("coils", None),
        P(None, "coils"),
        P(),
    )
    return jax.shard_map(
        local,
        mesh=mesh,
        in_specs=placed,
        out_specs=(P("frames", None, "coils", None), P("frames", None)),
        check_vma=False,
    )
```

time: 239 us -> 133 us (0.56)
  Pallas kernels: 0 us -> 85.4 us
  matrix products: 66.5 us -> 0 us
  other arithmetic: 61.2 us -> 2.25 us
  local copies, waits for them, and re-layouts: 30.3 us -> 5.24 us
  starting transfers between devices: 2.42 us -> 27.3 us
  blocking collectives: 24.6 us -> 0 us
  waiting for transfers between devices: 35 us -> 11.9 us
  between operations: 16.9 us -> 0.72 us
    pallas_call x0 -> x4, Pallas kernels: none -> 85.4 us  [the longest x1 74.1 us: gridded(): pl.pallas_call(functools.partial(grid_frames, starts, width, first=begin)...]
    dot_general x25 -> x0, matrix products: 66.5 us -> none  [the longest x12 62.2 us: frame_images(): jnp.einsum('xcpg,pqgy->xcqy', gridded, right_table, preferred_element_typ...]
    mul x5 -> x0, other arithmetic: 37.7 us -> none  [the longest x4 37.5 us: frame_images(): weighted = frame_data[:, :, :, :, None] * weights_y[None, None]]
    unnamed x2 -> x0, waiting for transfers between devices: 35 us -> none
    ppermute x1 -> x9, starting transfers between devices: 2.38 us -> 27.3 us  [the longest x4 16.3 us: shifted(): lax.ppermute(block, axis, [(i, i + distance) for i in range(count - dista...]
    psum x1 -> x0, blocking collectives: 12.8 us -> none  [local(): increment = lax.psum(partial_step, 'coils')]
    ppermute x1 -> x9, waiting for transfers between devices: 0.01 us -> 11.9 us  [the longest x3 5.46 us: around(): lax.ppermute(block, axis, [(i, (i + distance) % count) for i in range(cou...]
    unnamed x1 -> x0, blocking collectives: 11.8 us -> none
  transfers between devices with their start and end apart: 2 -> 9, of which waited for: 1 -> 7; matrix products, arithmetic and copies ran while one was open for 62% -> 0% of each run, Pallas kernels for 0% -> 56%
where the time goes in v1:
time: 133 us
  Pallas kernels  85.4 us (64%)
  starting transfers between devices  27.3 us (21%)
  waiting for transfers between devices  11.9 us (9%)
  local copies, waits for them, and re-layouts  5.24 us (4%)
  other arithmetic  2.25 us (2%)
    pallas_call x1, Pallas kernels, gridded(): pl.pallas_call(functools.partial(grid_frames, starts, width, first=begin)...  74.1 us
    ppermute x4, starting transfers between devices, shifted(): lax.ppermute(block, axis, [(i, i + distance) for i in range(count - dista...  16.3 us
    pallas_call x1, Pallas kernels, images(): pl.pallas_call(functools.partial(modulate, side, readout), out_shape=(blo...  5.62 us
    ppermute x3, starting transfers between devices, around(): lax.ppermute(block, axis, [(i, (i + distance) % count) for i in range(cou...  5.55 us
    ppermute x3, waiting for transfers between devices, around(): lax.ppermute(block, axis, [(i, (i + distance) % count) for i in range(cou...  5.46 us
    ppermute x2, starting transfers between devices, local(): increment = increment + lax.ppermute(increment, 'coils', pairs)  5.43 us
    pallas_call x1, Pallas kernels, local(): pl.pallas_call(functools.partial(prepare, starts, width), out_shape=(jax....  4.23 us
    ppermute x4, waiting for transfers between devices, shifted(): lax.ppermute(block, axis, [(i, i + distance) for i in range(count - dista...  3.32 us
  transfers between devices with their start and end apart: 9, of which 7 were waited for; matrix products, arithmetic and copies ran while one was open for 0% of the time, Pallas kernels for 56%

profile of v1, /device:TPU:0, one launch (start us, length us, event | category | flops | bytes accessed | tf_op | source)
XLA Modules:
  0.0 132.8 jit_solution(10723585301228932230)
XLA Ops:
  0.6 2.3 %slice_bitcast_fusion.kx_ref = bf16[16,256,128]{2,1,0:T(8,128)(2,1)} fusion(bf16[2,16,256,128]{3,2,1,0:T(8,128)(2,1)} %ky_ref.1), kind=kLoop, calls=%fused_computation | loop fusion | bytes 2097152 | tf_op jit(solution)/shard_map/squeeze | solution.py:208
  2.9 4.2 %prepare.1 = (bf16[16,3,128,128]{3,2,1,0:T(8,128)(2,1)}, f32[4,2,8,128]{3,2,1,0:T(8,128)}) custom-call(s32[2]{0:T(128)} %bounds_ref.3, bf16[4,8,13,2,256]{4,3,2,1,0:T(2,128)(2,1)} %bitcast.8, bf16[16,256,128]{2,1,0:T(8,128)(2,1)} %slice_bitcast_fusion.kx_ref), custom_call_target="tpu_custom_call" | custom-call | tf_op jit(solution)/shard_map/prepare/pallas_call | solution.py:199
  7.1 0.7 slice_bitcast_fusion.1
  7.8 2.4 %collective-permute-start = (f32[2,8,128]{2,1,0:T(8,128)S(1)}, f32[2,8,128]{2,1,0:T(8,128)S(1)}, u32[]{:S(2)}, u32[]{:S(2)}) collective-permute-start(f32[2,8,128]{2,1,0:T(8,128)S(1)} %slice_bitcast_fusion.1), channel_id=1, source_target_pairs={{0,4},{4,8},{8,12},{12,16},{16,20},{20,24},{24,28},{1,5},{5,9},{9,... | collective-permute-start | bytes 24584 | tf_op jit(solution)/shard_map/ppermute | solution.py:177
  10.2 0.0 copy-start.1
  10.3 0.0 copy-start.2
  10.3 0.0 copy-start.3
  10.3 74.1 %gridding.1.parts_ref = f32[4,3,2,128,128]{4,3,2,1,0:T(8,128)} custom-call(s32[4,13]{1,0:T(4,128)} %angles_ref.1, bf16[4,8,13,2,256]{4,3,2,1,0:T(2,128)(2,1)} %bitcast.9, bf16[16,3,128,128]{3,2,1,0:T(8,128)(2,1)} %get-tuple-element.9.rows_ref, bf16[2,16,256,128]{3,2,1,0:T(8,128)(2,1)} %ky_ref.1, bf16[256,256]{1,0:T(8,128)(2,1)} %constant.18.clone.right_ref, ...), custom_call_target="tpu_custom_call" | custom-call | tf_op jit(solution)/shard_map/gridding/pallas_call | solution.py:258
  84.4 0.0 collective-permute-done.arrived_ref
  84.4 0.7 broadcast_in_dim.5.projection_ref
  85.1 0.7 broadcast_in_dim.4.first_ref
  85.8 1.4 %drift.1 = f32[12,128]{1,0:T(8,128)} custom-call(s32[1]{0:T(128)} %bitcast.1.position_ref, f32[4,2,8,128]{3,2,1,0:T(8,128)} %get-tuple-element.8.center_ref, f32[2,8,128]{2,1,0:T(8,128)} %copy-done, f32[2,8,128]{2,1,0:T(8,128)} %broadcast_in_dim.4.first_ref, f32[3,8,128]{2,1,0:T(8,128)} %broadcast_in_dim.5.projection_ref), custom_call_target="tpu_custom_call" | custom-call | tf_op jit(solution)/shard_map/drift/pallas_call | solution.py:213
  87.2 0.8 slice_reduce_fusion
  88.0 0.1 reshape.19
  88.1 2.4 %collective-permute-start.1 = (f32[4,3]{1,0:T(4,128)S(1)}, f32[4,3]{1,0:T(4,128)S(1)}, u32[]{:S(2)}, u32[]{:S(2)}) collective-permute-start(f32[4,3]{1,0:T(4,128)S(1)} %reshape.19), channel_id=1, source_target_pairs={{0,1},{1,0},{2,3},{3,2},{4,5},{5,4},{6,7},{7,6},{8,9},{9,8},{10,11... | collective-permute-start | bytes 152 | tf_op jit(solution)/shard_map/ppermute | solution.py:225
  90.5 1.6 %collective-permute-done.1 = f32[4,3]{1,0:T(4,128)S(1)} collective-permute-done((f32[4,3]{1,0:T(4,128)S(1)}, f32[4,3]{1,0:T(4,128)S(1)}, u32[]{:S(2)}, u32[]{:S(2)}) %collective-permute-start.1) | collective-permute-done | bytes 80 | tf_op jit(solution)/shard_map/ppermute | solution.py:225
  92.0 3.0 %collective-permute-start.2 = (f32[4,3]{1,0:T(4,128)S(1)}, f32[4,3]{1,0:T(4,128)S(1)}, u32[]{:S(2)}, u32[]{:S(2)}) collective-permute-start(f32[4,3]{1,0:T(4,128)S(1)} %add.44), channel_id=1, source_target_pairs={{0,2},{1,3},{2,0},{3,1},{4,6},{5,7},{6,4},{7,5},{8,10},{9,11},{10,... | collective-permute-start | bytes 152 | tf_op jit(solution)/shard_map/ppermute | solution.py:225
  95.1 1.6 %collective-permute-done.2 = f32[4,3]{1,0:T(4,128)S(1)} collective-permute-done((f32[4,3]{1,0:T(4,128)S(1)}, f32[4,3]{1,0:T(4,128)S(1)}, u32[]{:S(2)}, u32[]{:S(2)}) %collective-permute-start.2) | collective-permute-done | bytes 80 | tf_op jit(solution)/shard_map/ppermute | solution.py:225
  96.6 2.0 %collective-permute-start.3 = (f32[3]{0:T(128)S(1)}, f32[3]{0:T(128)S(1)}, u32[]{:S(2)}, u32[]{:S(2)}) collective-permute-start(f32[3]{0:T(128)S(1)} %get-tuple-element.14), channel_id=1, source_target_pairs={{0,4},{4,8},{8,12},{12,16},{16,20},{20,24},{24,28},{1,5},{5,9},{9,... | collective-permute-start | bytes 44 | tf_op jit(solution)/shard_map/ppermute | solution.py:177
  98.7 0.8 collective-permute-done.3
  99.5 6.0 %collective-permute-start.4 = (f32[3]{0:T(128)S(1)}, f32[3]{0:T(128)S(1)}, u32[]{:S(2)}, u32[]{:S(2)}) collective-permute-start(f32[3]{0:T(128)S(1)} %add.46), channel_id=1, source_target_pairs={{0,8},{4,12},{8,16},{12,20},{16,24},{20,28},{1,9},{5,13},{9,17},{1... | collective-permute-start | bytes 44 | tf_op jit(solution)/shard_map/ppermute | solution.py:177
  105.4 1.3 collective-permute-done.4
  106.7 6.0 %collective-permute-start.5 = (f32[3]{0:T(128)S(1)}, f32[3]{0:T(128)S(1)}, u32[]{:S(2)}, u32[]{:S(2)}) collective-permute-start(f32[3]{0:T(128)S(1)} %add.48), channel_id=1, source_target_pairs={{0,16},{4,20},{8,24},{12,28},{1,17},{5,21},{9,25},{13,29},{2,18},{... | collective-permute-start | bytes 44 | tf_op jit(solution)/shard_map/ppermute | solution.py:177
  112.7 1.3 collective-permute-done.5
  114.0 0.6 add_add_fusion.1.coef_ref
  114.6 5.6 %modulate.1 = (f32[4,2,32,128]{3,2,1,0:T(8,128)}, f32[4,2,32,128]{3,2,1,0:T(8,128)}, f32[4,2,32,128]{3,2,1,0:T(8,128)}, f32[4,2,32,128]{3,2,1,0:T(8,128)}) custom-call(s32[1]{0:T(128)} %bitcast.position_ref, s32[2]{0:T(128)} %bounds_ref.3, f32[4,3]{1,0:T(4,128)} %add_add_fusion.1.coef_ref, f32[4,3,2,128,128]{4,3,2,1,0:T(8,128)} %gridding.1.parts_ref), custom_call_target="tpu_custom_call" | custom-call | tf_op jit(solution)/shard_map/modulate/pallas_call | solution.py:269
  120.2 1.6 %collective-permute-start.6 = (f32[4,2,32,128]{3,2,1,0:T(8,128)}, f32[4,2,32,128]{3,2,1,0:T(8,128)S(1)}, u32[]{:S(2)}, u32[]{:S(2)}) collective-permute-start(f32[4,2,32,128]{3,2,1,0:T(8,128)} %get-tuple-element.11), channel_id=1, source_target_pairs={{0,1},{1,2},{2,3},{3,0},{4,5},{5,6},{6,7},{7,4},{8,9},{9,10},{10,1... | collective-permute-start | bytes 393224 | tf_op jit(solution)/shard_map/ppermute | solution.py:182
  121.8 2.6 %collective-permute-start.7 = (f32[4,2,32,128]{3,2,1,0:T(8,128)}, f32[4,2,32,128]{3,2,1,0:T(8,128)S(1)}, u32[]{:S(2)}, u32[]{:S(2)}) collective-permute-start(f32[4,2,32,128]{3,2,1,0:T(8,128)} %get-tuple-element.12), channel_id=1, source_target_pairs={{0,2},{1,3},{2,0},{3,1},{4,6},{5,7},{6,4},{7,5},{8,10},{9,11},{10,... | collective-permute-start | bytes 393224 | tf_op jit(solution)/shard_map/ppermute | solution.py:182
  124.4 1.3 %collective-permute-start.8 = (f32[4,2,32,128]{3,2,1,0:T(8,128)}, f32[4,2,32,128]{3,2,1,0:T(8,128)S(1)}, u32[]{:S(2)}, u32[]{:S(2)}) collective-permute-start(f32[4,2,32,128]{3,2,1,0:T(8,128)} %get-tuple-element.13), channel_id=1, source_target_pairs={{0,3},{1,0},{2,1},{3,2},{4,7},{5,4},{6,5},{7,6},{8,11},{9,8},{10,9... | collective-permute-start | bytes 393224 | tf_op jit(solution)/shard_map/ppermute | solution.py:182
  125.7 1.6 %collective-permute-done.6 = f32[4,2,32,128]{3,2,1,0:T(8,128)S(1)} collective-permute-done((f32[4,2,32,128]{3,2,1,0:T(8,128)}, f32[4,2,32,128]{3,2,1,0:T(8,128)S(1)}, u32[]{:S(2)}, u32[]{:S(2)}) %collective-permute-start.6) | collective-permute-done | bytes 131104 | tf_op jit(solution)/shard_map/ppermute | solution.py:182
  127.3 3.9 %collective-permute-done.7 = f32[4,2,32,128]{3,2,1,0:T(8,128)S(1)} collective-permute-done((f32[4,2,32,128]{3,2,1,0:T(8,128)}, f32[4,2,32,128]{3,2,1,0:T(8,128)S(1)}, u32[]{:S(2)}, u32[]{:S(2)}) %collective-permute-start.7) | collective-permute-done | bytes 131104 | tf_op jit(solution)/shard_map/ppermute | solution.py:182
  131.2 1.6 %add_add_fusion = f32[4,2,32,128]{3,2,1,0:T(8,128)} fusion(f32[4,2,32,128]{3,2,1,0:T(8,128)S(1)} %collective-permute-done.8, f32[4,2,32,128]{3,2,1,0:T(8,128)S(1)} %collective-permute-done.7, f32[4,2,32,128]{3,2,1,0:T(8,128)} %get-tuple-element.10, f32[4,2,32,128]{3,2,1,0:T(8,128)S(1)} %collective-permute-done.6), kind=kLoop, calls=%fused_computation.1 | loop fusion | flops 98304 | bytes 655360 | tf_op jit(solution)/shard_map/add | solution.py:279
  (12 shorter events, 0.1 us)
Async XLA Ops:
  7.8 76.6 %collective-permute-start = (f32[2,8,128]{2,1,0:T(8,128)S(1)}, f32[2,8,128]{2,1,0:T(8,128)S(1)}, u32[]{:S(2)}, u32[]{:S(2)}) collective-permute-start(f32[2,8,128]{2,1,0:T(8,128)S(1)} %slice_bitcast_fusion.1), channel_id=1, source_target_pairs={{0,4},{4,8},{8,12},{12,16},{16,20},{20,24},{24,28},{1,5},{5,9},{9,... | collective-permute-start | bytes 24584 | tf_op jit(solution)/shard_map/ppermute | solution.py:177
  10.2 74.2 %copy-start.1 = (f32[3,8]{1,0:T(4,128)S(1)}, f32[3,8]{1,0:T(4,128)}, u32[]{:S(2)}) copy-start(f32[3,8]{1,0:T(4,128)} %param.16) | copy-start | bytes 292
  10.3 74.8 %copy-start.2 = (f32[8,2]{0,1:T(2,128)S(1)}, f32[8,2]{0,1:T(2,128)}, u32[]{:S(2)}) copy-start(f32[8,2]{0,1:T(2,128)} %param.15) | copy-start | bytes 196
  10.3 103.7 %copy-start.3 = (f32[3]{0:T(128)S(1)}, f32[3]{0:T(128)}, u32[]{:S(2)}) copy-start(f32[3]{0:T(128)} %param.17) | copy-start | bytes 40
  84.4 1.3 %copy-start = (f32[2,8,128]{2,1,0:T(8,128)}, f32[2,8,128]{2,1,0:T(8,128)S(1)}, u32[]{:S(2)}) copy-start(f32[2,8,128]{2,1,0:T(8,128)S(1)} %collective-permute-done.arrived_ref) | copy-start | bytes 24580
  88.1 4.0 %collective-permute-start.1 = (f32[4,3]{1,0:T(4,128)S(1)}, f32[4,3]{1,0:T(4,128)S(1)}, u32[]{:S(2)}, u32[]{:S(2)}) collective-permute-start(f32[4,3]{1,0:T(4,128)S(1)} %reshape.19), channel_id=1, source_target_pairs={{0,1},{1,0},{2,3},{3,2},{4,5},{5,4},{6,7},{7,6},{8,9},{9,8},{10,11... | collective-permute-start | bytes 152 | tf_op jit(solution)/shard_map/ppermute | solution.py:225
  92.0 4.6 %collective-permute-start.2 = (f32[4,3]{1,0:T(4,128)S(1)}, f32[4,3]{1,0:T(4,128)S(1)}, u32[]{:S(2)}, u32[]{:S(2)}) collective-permute-start(f32[4,3]{1,0:T(4,128)S(1)} %add.44), channel_id=1, source_target_pairs={{0,2},{1,3},{2,0},{3,1},{4,6},{5,7},{6,4},{7,5},{8,10},{9,11},{10,... | collective-permute-start | bytes 152 | tf_op jit(solution)/shard_map/ppermute | solution.py:225
  96.6 2.8 %collective-permute-start.3 = (f32[3]{0:T(128)S(1)}, f32[3]{0:T(128)S(1)}, u32[]{:S(2)}, u32[]{:S(2)}) collective-permute-start(f32[3]{0:T(128)S(1)} %get-tuple-element.14), channel_id=1, source_target_pairs={{0,4},{4,8},{8,12},{12,16},{16,20},{20,24},{24,28},{1,5},{5,9},{9,... | collective-permute-start | bytes 44 | tf_op jit(solution)/shard_map/ppermute | solution.py:177
  99.5 7.2 %collective-permute-start.4 = (f32[3]{0:T(128)S(1)}, f32[3]{0:T(128)S(1)}, u32[]{:S(2)}, u32[]{:S(2)}) collective-permute-start(f32[3]{0:T(128)S(1)} %add.46), channel_id=1, source_target_pairs={{0,8},{4,12},{8,16},{12,20},{16,24},{20,28},{1,9},{5,13},{9,17},{1... | collective-permute-start | bytes 44 | tf_op jit(solution)/shard_map/ppermute | solution.py:177
  106.7 7.3 %collective-permute-start.5 = (f32[3]{0:T(128)S(1)}, f32[3]{0:T(128)S(1)}, u32[]{:S(2)}, u32[]{:S(2)}) collective-permute-start(f32[3]{0:T(128)S(1)} %add.48), channel_id=1, source_target_pairs={{0,16},{4,20},{8,24},{12,28},{1,17},{5,21},{9,25},{13,29},{2,18},{... | collective-permute-start | bytes 44 | tf_op jit(solution)/shard_map/ppermute | solution.py:177
  120.2 7.1 %collective-permute-start.6 = (f32[4,2,32,128]{3,2,1,0:T(8,128)}, f32[4,2,32,128]{3,2,1,0:T(8,128)S(1)}, u32[]{:S(2)}, u32[]{:S(2)}) collective-permute-start(f32[4,2,32,128]{3,2,1,0:T(8,128)} %get-tuple-element.11), channel_id=1, source_target_pairs={{0,1},{1,2},{2,3},{3,0},{4,5},{5,6},{6,7},{7,4},{8,9},{9,10},{10,1... | collective-permute-start | bytes 393224 | tf_op jit(solution)/shard_map/ppermute | solution.py:182
  121.8 9.4 %collective-permute-start.7 = (f32[4,2,32,128]{3,2,1,0:T(8,128)}, f32[4,2,32,128]{3,2,1,0:T(8,128)S(1)}, u32[]{:S(2)}, u32[]{:S(2)}) collective-permute-start(f32[4,2,32,128]{3,2,1,0:T(8,128)} %get-tuple-element.12), channel_id=1, source_target_pairs={{0,2},{1,3},{2,0},{3,1},{4,6},{5,7},{6,4},{7,5},{8,10},{9,11},{10,... | collective-permute-start | bytes 393224 | tf_op jit(solution)/shard_map/ppermute | solution.py:182
  124.4 6.8 %collective-permute-start.8 = (f32[4,2,32,128]{3,2,1,0:T(8,128)}, f32[4,2,32,128]{3,2,1,0:T(8,128)S(1)}, u32[]{:S(2)}, u32[]{:S(2)}) collective-permute-start(f32[4,2,32,128]{3,2,1,0:T(8,128)} %get-tuple-element.13), channel_id=1, source_target_pairs={{0,3},{1,0},{2,1},{3,2},{4,7},{5,4},{6,5},{7,6},{8,11},{9,8},{10,9... | collective-permute-start | bytes 393224 | tf_op jit(solution)/shard_map/ppermute | solution.py:182

commit v2 on v1

v2 whole, which is shorter than its diff:
```python
import functools
from jax._src.pallas.mosaic import core
import math

import jax
import jax.numpy as jnp
import ml_dtypes
import numpy as np
from jax import lax
from jax.experimental import pallas as pl
from jax.experimental.pallas import tpu as pltpu
from jax.sharding import PartitionSpec as P

BF16 = jnp.bfloat16
F32 = jnp.float32


def dft_tables(side):
    offsets = np.arange(side) - side // 2
    wrapped = np.mod(offsets[:, None] * offsets[None, :], side).astype(np.float32)
    phase = np.float32(2.0 * math.pi / side) * wrapped
    cosine = (np.cos(phase) / np.float32(side)).astype(ml_dtypes.bfloat16)
    sine = (np.sin(phase) / np.float32(side)).astype(ml_dtypes.bfloat16)
    right = np.block([[cosine, sine], [-sine, cosine]])
    left = np.block([[cosine, -sine], [sine, cosine]])
    return right, left


def windows(readout, segs):
    spacing, jitter = readout // segs, readout // (4 * segs)
    low = [0] + [j * spacing - jitter for j in range(1, segs)]
    high = [j * spacing + jitter for j in range(1, segs)] + [readout]
    width = 128
    while True:
        starts = [max(0, min(a // 16 * 16, readout - width)) for a in low]
        if all(s + width >= b for s, b in zip(starts, high)) or width >= readout:
            return starts, min(width, readout)
        width += 128


def edges_of(bounds_ref, readout, segs):
    return [0] + [bounds_ref[j] for j in range(segs - 1)] + [readout]


def centres(kdata_ref, center_ref):
    for t in range(kdata_ref.shape[0]):
        for c in range(kdata_ref.shape[1]):
            total = kdata_ref[t, c, 0].astype(F32)
            for s in range(1, kdata_ref.shape[2]):
                total += kdata_ref[t, c, s].astype(F32)
            center_ref[t, 0, c, :] = total[0]
            center_ref[t, 1, c, :] = total[1]


def drift(position_ref, center_ref, arrived_ref, first_ref, projection_ref, step_ref):
    frames, _, coils, lanes = center_ref.shape
    basis = projection_ref.shape[0]
    at_start = position_ref[0] == 0
    for t in range(frames):
        if t == 0:
            before = [jnp.where(at_start, first_ref[p], arrived_ref[p]) for p in range(2)]
        else:
            before = [center_ref[t - 1, p] for p in range(2)]
        now = [center_ref[t, p] for p in range(2)]
        cross = before[0] * now[1] - before[1] * now[0]
        energy = before[0] * before[0] + before[1] * before[1]
        energy = energy + (now[0] * now[0] + now[1] * now[1]) + 1.0
        signal = 2.0 * cross / energy
        for b in range(basis):
            row = jnp.sum(projection_ref[b] * signal, axis=0, keepdims=True)
            step_ref[pl.ds(t * basis + b, 1), :] = row


def grid_frames(starts, width, first, count, angles_ref, bounds_ref, kdata_ref, tables_ref, right_ref, left_ref, sens_ref, out_ref):
    _, coils, spokes, _, readout = kdata_ref.shape
    _, table, _, side = tables_ref.shape
    segs = len(starts)
    odd = spokes % 2
    padded = spokes + odd
    tiles = padded // 2
    pairs = coils // 2
    steps = count * pairs
    lanes = 128
    room = lanes // 4

    def body(kd, rows, turned, weighted, halves, ky, right, left, *accs):
        grid_acc = [accs[m * 8 : m * 8 + 3] for m in range(2)]
        half_acc = [accs[m * 8 + 3 : m * 8 + 5] for m in range(2)]
        image_acc = [accs[m * 8 + 5 : m * 8 + 8] for m in range(2)]
        edges = edges_of(bounds_ref, readout, segs)
        index = lax.broadcasted_iota(jnp.int32, (width, side), 0)

        def angle_tables(a, carry):
            ky[a] = tables_ref[1, a]
            for l in range(segs):
                at = index + starts[l]
                keep = (at >= edges[l]) & (at < edges[l + 1])
                part = jnp.where(keep, tables_ref[0, a, starts[l] : starts[l] + width, :].astype(F32), 0.0)
                rows[a, l] = part.T.astype(BF16)
            return carry

        lax.fori_loop(0, table, angle_tables, 0)
        right[...] = right_ref[...]
        left[...] = left_ref[...]
        out_ref[...] = jnp.zeros(out_ref.shape, F32)
        if odd:
            rows[table] = jnp.zeros((segs, side, width), BF16)
            weighted[:, :, :, spokes] = jnp.zeros((2, 2, 2, readout, side), BF16)

        def columns(i, carry):
            for s in range(spokes):
                for c in range(coils):
                    kd[c, 2 * s : 2 * s + 2, :] = kdata_ref[first + i, c, s].astype(F32)
            per = min(lanes // room, coils)
            for g in range(coils // per):
                flipped = kd[g * per : (g + 1) * per].reshape(per * room, readout).T
                for e in range(per):
                    turned[i, g * per + e, :, :room] = flipped[:, e * room : (e + 1) * room].astype(BF16)
            return carry

        lax.fori_loop(0, count, columns, 0)

        def place(step):
            return lax.div(step, pairs), lax.rem(step, pairs)

        def weigh(step, buf, m, s):
            i, n = place(step)
            column = turned[i, 2 * n + m, :, 2 * s : 2 * s + 2]
            factor = ky[angles_ref[first + i, s]]
            for p in range(2):
                scale = jnp.broadcast_to(column[:, p : p + 1], (readout, side))
                weighted[buf, m, p, s] = scale * factor

        def beside(blocks):
            return jnp.concatenate(blocks, axis=1)

        def grid_tile(step, buf, l, k):
            i, _ = place(step)
            spoke = [2 * k, 2 * k + 1]
            which = [angles_ref[first + i, s] if s < spokes else table for s in spoke]
            for m in range(2):
                rhs = beside([
                    weighted[buf, m, p, 2 * k : 2 * k + 2, starts[l] : starts[l] + width, :].reshape(2 * width, side)
                    for p in range(2)
                ])
                pltpu.matmul_push_rhs(rhs, k % 2, m)
            lhs = beside([rows[a, l] for a in which])
            for m in range(2):
                pltpu.matmul_acc_lhs(grid_acc[m][l], lhs, load_staged_rhs=k % 2)

        def over_columns(buf, l):
            for m in range(2):
                pltpu.matmul_push_rhs(beside([right[0], right[1]]), 1, m)
                gridded = pltpu.matmul_pop(grid_acc[m][l]).astype(BF16)
                pltpu.matmul_acc_lhs(half_acc[m][l % 2], gridded, load_staged_rhs=1)
            for m in range(2):
                half = pltpu.matmul_pop(half_acc[m][l % 2]).astype(BF16)
                halves[buf, m, l, 0] = half[:, :side]
                halves[buf, m, l, 1] = half[:, side:]

        def left_rows(h):
            return beside([left[q, h * side : (h + 1) * side] for q in range(2)])

        def over_rows_both(buf):
            for m in range(2):
                both = beside([halves[buf, m, l].reshape(2 * side, side) for l in range(2)])
                pltpu.matmul_push_rhs(both, 0, m)
            for h in range(2):
                for m in range(2):
                    pltpu.matmul_acc_lhs(image_acc[m][h], left_rows(h), load_staged_rhs=0 if h == 0 else None)

        def over_rows_last(buf):
            both = beside([halves[buf, m, 2].reshape(2 * side, side) for m in range(2)])
            for m in range(2):
                pltpu.matmul_push_rhs(both, 0, m)
                pltpu.matmul_acc_lhs(image_acc[m][2], left_rows(m), load_staged_rhs=0)

        def combine(step, l, parts):
            i, n = place(step)
            total_re, total_im = out_ref[i, l, 0], out_ref[i, l, 1]
            for m in range(2):
                re, im = parts[m]
                real = sens_ref[2 * n + m, 0].astype(F32)
                imag = sens_ref[2 * n + m, 1].astype(F32)
                total_re += real * re + imag * im
                total_im += real * im - imag * re
            out_ref[i, l, 0] = total_re
            out_ref[i, l, 1] = total_im

        def combine_both(step):
            images = [[pltpu.matmul_pop(image_acc[m][h]) for h in range(2)] for m in range(2)]
            for l in range(2):
                combine(step, l, [[part[:, l * side : (l + 1) * side] for part in images[m]] for m in range(2)])

        def combine_last(step):
            images = [pltpu.matmul_pop(image_acc[h][2]) for h in range(2)]
            combine(step, 2, [[part[:, m * side : (m + 1) * side] for part in images] for m in range(2)])

        def phase(step, buf, begin, end):
            ahead = [] if end else [(m, s) for s in range(spokes) for m in range(2)]
            chunks = [ahead[len(ahead) * n // (segs * tiles) : len(ahead) * (n + 1) // (segs * tiles)] for n in range(segs * tiles)]

            def grid_segment(l):
                for k in range(tiles):
                    for m, s in chunks[l * tiles + k]:
                        weigh(step + 1, 1 - buf, m, s)
                    grid_tile(step, buf, l, k)

            grid_segment(0)
            if not begin:
                over_columns(1 - buf, 2)
            grid_segment(1)
            over_columns(buf, 0)
            if not begin:
                over_rows_both(1 - buf)
            grid_segment(2)
            if not begin:
                over_rows_last(1 - buf)
                combine_both(step - 1)
            over_columns(buf, 1)
            if not begin:
                combine_last(step - 1)

        for s in range(spokes):
            for m in range(2):
                weigh(0, 0, m, s)
        phase(0, 0, True, False)

        def two(q, carry):
            phase(2 * q + 1, 1, False, False)
            phase(2 * q + 2, 0, False, False)
            return carry

        lax.fori_loop(0, steps // 2 - 1, two, 0)
        phase(steps - 1, 1, False, True)
        over_columns(1, 2)
        over_rows_both(1)
        over_rows_last(1)
        combine_both(steps - 1)
        combine_last(steps - 1)

    pl.run_scoped(
        body,
        pltpu.VMEM((coils, room, readout), F32),
        pltpu.VMEM((table + odd, segs, side, width), BF16),
        pltpu.VMEM((count, coils, readout, lanes), BF16),
        pltpu.VMEM((2, 2, 2, padded, readout, side), BF16),
        pltpu.VMEM((2, 2, segs, 2, side, side), BF16),
        pltpu.VMEM((table, readout, side), BF16),
        pltpu.VMEM((2, 2 * side, side), BF16),
        pltpu.VMEM((2, 2 * side, side), BF16),
        *[core.AccMemorySpace(m)((side, 2 * side), F32) for m in range(2) for _ in range(8)],
    )


def modulate(side, readout, position_ref, bounds_ref, coef_ref, parts_ref, *out_refs):
    frames, segs = parts_ref.shape[:2]
    owners = len(out_refs)
    rows = side // owners
    half = side // 2
    me = position_ref[0]
    edges = edges_of(bounds_ref, readout, segs)
    times = [(edges[l] + edges[l + 1] - 1).astype(F32) / (2.0 * readout) for l in range(segs)]
    lane = lax.broadcasted_iota(jnp.int32, (8, 128), 1)
    base = jnp.zeros((8, 128), F32)
    slope = jnp.zeros((8, 128), F32)
    scale = jnp.zeros((8, 128), F32)
    for t in range(frames):
        for l in range(segs):
            here = lane == t * segs + l
            base = jnp.where(here, coef_ref[t, 0], base)
            slope = jnp.where(here, coef_ref[t, 1], slope)
            scale = jnp.where(here, times[l], scale)
    down_pos = (lax.broadcasted_iota(jnp.int32, (side, 128), 0) - half).astype(F32) / half
    down = (base[:1] + slope[:1] * down_pos) * scale[:1]
    cos_down, sin_down = jnp.cos(down), jnp.sin(down)
    across_pos = (lax.broadcasted_iota(jnp.int32, (1, side), 1) - half).astype(F32) / half
    across = jnp.concatenate(
        [coef_ref[t, 2] * across_pos * times[l] for t in range(frames) for l in range(segs)], axis=0
    )
    cos_across, sin_across = jnp.cos(across), jnp.sin(across)
    for t in range(frames):
        image_re = jnp.zeros((side, side), F32)
        image_im = jnp.zeros((side, side), F32)
        for l in range(segs):
            n = t * segs + l
            cr, sr = cos_down[:, n : n + 1], sin_down[:, n : n + 1]
            cc, sc = cos_across[n : n + 1], sin_across[n : n + 1]
            cos = cr * cc - sr * sc
            sin = sr * cc + cr * sc
            re, im = parts_ref[t, l, 0], parts_ref[t, l, 1]
            image_re += cos * re - sin * im
            image_im += sin * re + cos * im
        for owner in range(owners):
            for d, out_ref in enumerate(out_refs):

                @pl.when(lax.rem(me + d, owners) == owner)
                def _():
                    out_ref[t, 0] = image_re[owner * rows : (owner + 1) * rows]
                    out_ref[t, 1] = image_im[owner * rows : (owner + 1) * rows]


def shifted(block, axis, distance):
    count = lax.axis_size(axis)
    return lax.ppermute(block, axis, [(i, i + distance) for i in range(count - distance)])


def around(block, axis, distance):
    count = lax.axis_size(axis)
    return lax.ppermute(block, axis, [(i, (i + distance) % count) for i in range(count)])


def exchanged(block, axis, distance):
    return lax.ppermute(block, axis, [(i, i ^ distance) for i in range(lax.axis_size(axis))])


def local(kdata, angles, kernels, seg_bounds, sensitivity, ref_center, projection, init_coef):
    frames, coils, _, spokes, readout = kdata.shape
    side = kernels.shape[3]
    segs = seg_bounds.shape[0] + 1
    basis = projection.shape[0]
    owners = lax.axis_size("coils")
    starts, width = windows(readout, segs)
    right, left = (jnp.stack(jnp.split(jnp.asarray(table), 2, axis=1)) for table in dft_tables(side))
    kd = jnp.swapaxes(kdata, 2, 3)
    smem = pl.BlockSpec(memory_space=pltpu.SMEM)
    vmem = pl.BlockSpec(memory_space=pltpu.VMEM)
    place = lax.axis_index("frames").astype(jnp.int32)
    owner = lax.axis_index("coils").astype(jnp.int32)

    lanes = 128
    center = pl.pallas_call(
        centres,
        grid=(1,),
        out_shape=jax.ShapeDtypeStruct((frames, 2, coils, lanes), F32),
        in_specs=[pl.BlockSpec((frames, coils, spokes, 2, lanes), lambda i: (0, 0, 0, 0, readout // 2 // lanes))],
        out_specs=pl.BlockSpec((frames, 2, coils, lanes), lambda i: (0, 0, 0, 0)),
        name="centres",
    )(kd)

    arrived = shifted(center[-1], "frames", 1)
    first = jnp.broadcast_to(ref_center.T[:, :, None], (2, coils, lanes))
    weights = jnp.broadcast_to(projection[:, :, None], (basis, coils, lanes))
    step = pl.pallas_call(
        drift,
        out_shape=jax.ShapeDtypeStruct((frames * basis, lanes), F32),
        in_specs=[smem, vmem, vmem, vmem, vmem],
        out_specs=vmem,
        name="drift",
    )(place.reshape(1), center, arrived, first, weights)
    increment = step[:, :1].reshape(frames, basis)
    distance = 1
    while distance < owners:
        increment = increment + exchanged(increment, "coils", distance)
        distance *= 2
    running = jnp.sum(increment, axis=0)
    before = jnp.zeros_like(running)
    distance = 1
    while distance < lax.axis_size("frames"):
        came = exchanged(running, "frames", distance)
        before = before + jnp.where((place & distance) != 0, came, 0.0)
        running = running + came
        distance *= 2
    field_coef = init_coef[None, :] + (before[None, :] + jnp.cumsum(increment, axis=0))

    parts = pl.pallas_call(
        functools.partial(grid_frames, starts, width, 0, frames),
        out_shape=jax.ShapeDtypeStruct((frames, segs, 2, side, side), F32),
        in_specs=[smem, smem, vmem, vmem, vmem, vmem, vmem],
        out_specs=vmem,
        name="gridding",
    )(angles, seg_bounds, kd, kernels, right, left, sensitivity)

    block = jax.ShapeDtypeStruct((frames, 2, side // owners, side), F32)
    blocks = pl.pallas_call(
        functools.partial(modulate, side, readout),
        out_shape=(block,) * owners,
        in_specs=[smem, smem, smem, vmem],
        out_specs=(vmem,) * owners,
        name="modulate",
    )(owner.reshape(1), seg_bounds, field_coef, parts)
    image = blocks[0]
    for d in range(1, owners):
        image = image + around(blocks[d], "coils", d)
    return (image, field_coef)


def solution(mesh):
    placed = (
        P("frames", "coils", None, None, None),
        P("frames", None),
        P(),
        P(),
        P("coils", None, None, None),
        P("coils", None),
        P(None, "coils"),
        P(),
    )
    def located(*arguments):
        with jax.sharding.use_abstract_mesh(mesh.abstract_mesh):
            return local(*arguments)

    return jax.shard_map(
        local,
        mesh=mesh,
        in_specs=placed,
        out_specs=(P("frames", None, "coils", None), P("frames", None)),
        check_vma=False,
    )
```

time: 133 us -> 70.1 us (0.53)
  Pallas kernels: 85.4 us -> 32.7 us
  starting transfers between devices: 27.3 us -> 17.8 us
  local copies, waits for them, and re-layouts: 5.24 us -> 2.95 us
  waiting for transfers between devices: 11.9 us -> 13.3 us
    pallas_call x4, Pallas kernels: 85.4 us -> 32.7 us  [the longest x1 26.3 us: local(): pl.pallas_call(functools.partial(grid_frames, starts, width, 0, frames),...]
    ppermute x4 -> x1, starting transfers between devices: 16.3 us -> 2.38 us  [shifted(): lax.ppermute(block, axis, [(i, i + distance) for i in range(count - dista...]
    ppermute x2 -> x5, starting transfers between devices: 5.43 us -> 9.6 us  [exchanged(): lax.ppermute(block, axis, [(i, i ^ distance) for i in range(lax.axis_size...]
    ppermute x2 -> x5, waiting for transfers between devices: 3.13 us -> 7.29 us  [exchanged(): lax.ppermute(block, axis, [(i, i ^ distance) for i in range(lax.axis_size...]
    ppermute x4 -> x1, waiting for transfers between devices: 3.32 us -> 0.01 us  [shifted(): lax.ppermute(block, axis, [(i, i + distance) for i in range(count - dista...]
    squeeze x1 -> x0, local copies, waits for them, and re-layouts: 2.29 us -> none  [local(): kernels[0]]
  transfers between devices with their start and end apart: 9 -> 9, of which waited for: 7 -> 7; matrix products, arithmetic and copies ran while one was open for 0% -> 0% of each run, Pallas kernels for 56% -> 38%
where the time goes in v2:
time: 70.1 us; the launch traced here: 69.7 us
  Pallas kernels  32.7 us (47%)
  starting transfers between devices  17.8 us (25%)
  waiting for transfers between devices  13.3 us (19%)
  local copies, waits for them, and re-layouts  2.95 us (4%)
  other arithmetic  2.25 us (3%)
    pallas_call x1, Pallas kernels, local(): pl.pallas_call(functools.partial(grid_frames, starts, width, 0, frames),...  26.3 us
    ppermute x5, starting transfers between devices, exchanged(): lax.ppermute(block, axis, [(i, i ^ distance) for i in range(lax.axis_size...  9.6 us
    ppermute x5, waiting for transfers between devices, exchanged(): lax.ppermute(block, axis, [(i, i ^ distance) for i in range(lax.axis_size...  7.29 us
    ppermute x3, waiting for transfers between devices, around(): lax.ppermute(block, axis, [(i, (i + distance) % count) for i in range(cou...  5.97 us
    ppermute x3, starting transfers between devices, around(): lax.ppermute(block, axis, [(i, (i + distance) % count) for i in range(cou...  5.83 us
    pallas_call x1, Pallas kernels, local(): pl.pallas_call(functools.partial(modulate, side, readout), out_shape=(blo...  3.42 us
    ppermute x1, starting transfers between devices, shifted(): lax.ppermute(block, axis, [(i, i + distance) for i in range(count - dista...  2.38 us
    pallas_call x1, Pallas kernels, local(): pl.pallas_call(centres, grid=(1,), out_shape=jax.ShapeDtypeStruct((frames...  1.66 us
  transfers between devices with their start and end apart: 9, of which 7 were waited for; matrix products, arithmetic and copies ran while one was open for 0% of the time, Pallas kernels for 38%

profile of v2, /device:TPU:0, one launch (start us, length us, event | category | flops | bytes accessed | tf_op | source)
XLA Modules:
  0.0 69.7 jit_solution(9111378036903054120)
XLA Ops:
  0.6 1.7 %centres.1.center_ref = f32[4,2,8,128]{3,2,1,0:T(8,128)} custom-call(bf16[4,8,13,2,256]{4,3,2,1,0:T(2,128)(2,1)} %bitcast.6), custom_call_target="tpu_custom_call" | custom-call | tf_op jit(solution)/shard_map/centres/pallas_call | solution.py:332
  2.3 0.7 %slice_bitcast_fusion = f32[2,8,128]{2,1,0:T(8,128)S(1)} fusion(f32[4,2,8,128]{3,2,1,0:T(8,128)} %centres.1.center_ref), kind=kLoop, calls=%fused_computation.2 | loop fusion | bytes 16384 | tf_op jit(solution)/shard_map/squeeze | solution.py:341
  3.0 2.4 %collective-permute-start = (f32[2,8,128]{2,1,0:T(8,128)S(1)}, f32[2,8,128]{2,1,0:T(8,128)S(1)}, u32[]{:S(2)}, u32[]{:S(2)}) collective-permute-start(f32[2,8,128]{2,1,0:T(8,128)S(1)} %slice_bitcast_fusion), channel_id=1, source_target_pairs={{0,4},{4,8},{8,12},{12,16},{16,20},{20,24},{24,28},{1,5},{5,9},{9,... | collective-permute-start | bytes 24584 | tf_op jit(solution)/shard_map/ppermute | solution.py:305
  5.4 0.0 copy-start.2
  5.4 0.0 copy-start.1
  5.4 0.0 copy-start.3
  5.4 26.3 %gridding.1.parts_ref = f32[4,3,2,128,128]{4,3,2,1,0:T(8,128)} custom-call(s32[4,13]{1,0:T(4,128)} %angles_ref.1, s32[2]{0:T(128)} %bounds_ref.3, bf16[4,8,13,2,256]{4,3,2,1,0:T(2,128)(2,1)} %bitcast.7, bf16[2,16,256,128]{3,2,1,0:T(8,128)(2,1)} %tables_ref.1, bf16[2,256,128]{2,1,0:T(8,128)(2,1)} %constant.34.right_ref, ...), custom_call_target="tpu_custom_call" | custom-call | tf_op jit(solution)/shard_map/gridding/pallas_call | solution.py:366
  31.7 0.0 collective-permute-done.arrived_ref
  31.7 0.7 broadcast_in_dim.10.first_ref
  32.4 0.7 broadcast_in_dim.11.projection_ref
  33.0 1.4 %drift.1 = f32[12,128]{1,0:T(8,128)} custom-call(s32[1]{0:T(128)} %bitcast.1.position_ref, f32[4,2,8,128]{3,2,1,0:T(8,128)} %centres.1.center_ref, f32[2,8,128]{2,1,0:T(8,128)} %copy-done, f32[2,8,128]{2,1,0:T(8,128)} %broadcast_in_dim.10.first_ref, f32[3,8,128]{2,1,0:T(8,128)} %broadcast_in_dim.11.projection_ref), custom_call_target="tpu_custom_call" | custom-call | tf_op jit(solution)/shard_map/drift/pallas_call | solution.py:344
  34.4 0.8 %slice_reduce_fusion = f32[12]{0:T(128)S(1)} fusion(f32[12,128]{1,0:T(8,128)} %drift.1), kind=kLoop, calls=%fused_computation.1 | loop fusion | bytes 96 | tf_op jit(solution)/shard_map/slice | solution.py:351
  35.3 0.1 reshape.19
  35.3 2.4 %collective-permute-start.1 = (f32[4,3]{1,0:T(4,128)S(1)}, f32[4,3]{1,0:T(4,128)S(1)}, u32[]{:S(2)}, u32[]{:S(2)}) collective-permute-start(f32[4,3]{1,0:T(4,128)S(1)} %reshape.19), channel_id=1, source_target_pairs={{0,1},{1,0},{2,3},{3,2},{4,5},{5,4},{6,7},{7,6},{8,9},{9,8},{10,11... | collective-permute-start | bytes 152 | tf_op jit(solution)/shard_map/ppermute | solution.py:314
  37.7 1.6 %collective-permute-done.1 = f32[4,3]{1,0:T(4,128)S(1)} collective-permute-done((f32[4,3]{1,0:T(4,128)S(1)}, f32[4,3]{1,0:T(4,128)S(1)}, u32[]{:S(2)}, u32[]{:S(2)}) %collective-permute-start.1) | collective-permute-done | bytes 80 | tf_op jit(solution)/shard_map/ppermute | solution.py:314
  39.3 3.0 %collective-permute-start.2 = (f32[4,3]{1,0:T(4,128)S(1)}, f32[4,3]{1,0:T(4,128)S(1)}, u32[]{:S(2)}, u32[]{:S(2)}) collective-permute-start(f32[4,3]{1,0:T(4,128)S(1)} %add.44), channel_id=1, source_target_pairs={{0,2},{1,3},{2,0},{3,1},{4,6},{5,7},{6,4},{7,5},{8,10},{9,11},{10,... | collective-permute-start | bytes 152 | tf_op jit(solution)/shard_map/ppermute | solution.py:314
  42.3 1.6 %collective-permute-done.2 = f32[4,3]{1,0:T(4,128)S(1)} collective-permute-done((f32[4,3]{1,0:T(4,128)S(1)}, f32[4,3]{1,0:T(4,128)S(1)}, u32[]{:S(2)}, u32[]{:S(2)}) %collective-permute-start.2) | collective-permute-done | bytes 80 | tf_op jit(solution)/shard_map/ppermute | solution.py:314
  43.9 0.2 collective-permute-start.3
  44.1 1.0 %collective-permute-done.3 = f32[3]{0:T(128)S(1)} collective-permute-done((f32[3]{0:T(128)S(1)}, f32[3]{0:T(128)S(1)}, u32[]{:S(2)}, u32[]{:S(2)}) %collective-permute-start.3) | collective-permute-done | bytes 44 | tf_op jit(solution)/shard_map/ppermute | solution.py:314
  45.2 2.0 %collective-permute-start.4 = (f32[3]{0:T(128)S(1)}, f32[3]{0:T(128)S(1)}, u32[]{:S(2)}, u32[]{:S(2)}) collective-permute-start(f32[3]{0:T(128)S(1)} %add.46), channel_id=1, source_target_pairs={{0,8},{4,12},{8,0},{12,4},{16,24},{20,28},{24,16},{28,20},{1,9},{5... | collective-permute-start | bytes 44 | tf_op jit(solution)/shard_map/ppermute | solution.py:314
  47.2 1.6 %collective-permute-done.4 = f32[3]{0:T(128)S(1)} collective-permute-done((f32[3]{0:T(128)S(1)}, f32[3]{0:T(128)S(1)}, u32[]{:S(2)}, u32[]{:S(2)}) %collective-permute-start.4) | collective-permute-done | bytes 44 | tf_op jit(solution)/shard_map/ppermute | solution.py:314
  48.7 2.0 %collective-permute-start.5 = (f32[3]{0:T(128)S(1)}, f32[3]{0:T(128)S(1)}, u32[]{:S(2)}, u32[]{:S(2)}) collective-permute-start(f32[3]{0:T(128)S(1)} %add.48), channel_id=1, source_target_pairs={{0,16},{4,20},{8,24},{12,28},{16,0},{20,4},{24,8},{28,12},{1,17},{... | collective-permute-start | bytes 44 | tf_op jit(solution)/shard_map/ppermute | solution.py:314
  50.8 1.6 %collective-permute-done.5 = f32[3]{0:T(128)S(1)} collective-permute-done((f32[3]{0:T(128)S(1)}, f32[3]{0:T(128)S(1)}, u32[]{:S(2)}, u32[]{:S(2)}) %collective-permute-start.5) | collective-permute-done | bytes 44 | tf_op jit(solution)/shard_map/ppermute | solution.py:314
  52.3 0.6 add_add_fusion.1.coef_ref
  52.9 3.4 %modulate.1 = (f32[4,2,32,128]{3,2,1,0:T(8,128)}, f32[4,2,32,128]{3,2,1,0:T(8,128)}, f32[4,2,32,128]{3,2,1,0:T(8,128)}, f32[4,2,32,128]{3,2,1,0:T(8,128)}) custom-call(s32[1]{0:T(128)} %bitcast.position_ref, s32[2]{0:T(128)} %bounds_ref.3, f32[4,3]{1,0:T(4,128)} %add_add_fusion.1.coef_ref, f32[4,3,2,128,128]{4,3,2,1,0:T(8,128)} %gridding.1.parts_ref), custom_call_target="tpu_custom_call" | custom-call | tf_op jit(solution)/shard_map/modulate/pallas_call | solution.py:375
  56.3 1.9 %collective-permute-start.6 = (f32[4,2,32,128]{3,2,1,0:T(8,128)}, f32[4,2,32,128]{3,2,1,0:T(8,128)S(1)}, u32[]{:S(2)}, u32[]{:S(2)}) collective-permute-start(f32[4,2,32,128]{3,2,1,0:T(8,128)} %get-tuple-element.7), channel_id=1, source_target_pairs={{0,1},{1,2},{2,3},{3,0},{4,5},{5,6},{6,7},{7,4},{8,9},{9,10},{10,1... | collective-permute-start | bytes 393224 | tf_op jit(solution)/shard_map/ppermute | solution.py:310
  58.2 2.6 %collective-permute-start.7 = (f32[4,2,32,128]{3,2,1,0:T(8,128)}, f32[4,2,32,128]{3,2,1,0:T(8,128)S(1)}, u32[]{:S(2)}, u32[]{:S(2)}) collective-permute-start(f32[4,2,32,128]{3,2,1,0:T(8,128)} %get-tuple-element.8), channel_id=1, source_target_pairs={{0,2},{1,3},{2,0},{3,1},{4,6},{5,7},{6,4},{7,5},{8,10},{9,11},{10,... | collective-permute-start | bytes 393224 | tf_op jit(solution)/shard_map/ppermute | solution.py:310
  60.8 1.3 %collective-permute-start.8 = (f32[4,2,32,128]{3,2,1,0:T(8,128)}, f32[4,2,32,128]{3,2,1,0:T(8,128)S(1)}, u32[]{:S(2)}, u32[]{:S(2)}) collective-permute-start(f32[4,2,32,128]{3,2,1,0:T(8,128)} %get-tuple-element.9), channel_id=1, source_target_pairs={{0,3},{1,0},{2,1},{3,2},{4,7},{5,4},{6,5},{7,6},{8,11},{9,8},{10,9... | collective-permute-start | bytes 393224 | tf_op jit(solution)/shard_map/ppermute | solution.py:310
  62.2 2.7 %collective-permute-done.6 = f32[4,2,32,128]{3,2,1,0:T(8,128)S(1)} collective-permute-done((f32[4,2,32,128]{3,2,1,0:T(8,128)}, f32[4,2,32,128]{3,2,1,0:T(8,128)S(1)}, u32[]{:S(2)}, u32[]{:S(2)}) %collective-permute-start.6) | collective-permute-done | bytes 131104 | tf_op jit(solution)/shard_map/ppermute | solution.py:310
  64.9 3.3 %collective-permute-done.7 = f32[4,2,32,128]{3,2,1,0:T(8,128)S(1)} collective-permute-done((f32[4,2,32,128]{3,2,1,0:T(8,128)}, f32[4,2,32,128]{3,2,1,0:T(8,128)S(1)}, u32[]{:S(2)}, u32[]{:S(2)}) %collective-permute-start.7) | collective-permute-done | bytes 131104 | tf_op jit(solution)/shard_map/ppermute | solution.py:310
  68.1 0.0 collective-permute-done.8
  68.1 1.6 %add_add_fusion = f32[4,2,32,128]{3,2,1,0:T(8,128)} fusion(f32[4,2,32,128]{3,2,1,0:T(8,128)S(1)} %collective-permute-done.8, f32[4,2,32,128]{3,2,1,0:T(8,128)S(1)} %collective-permute-done.7, f32[4,2,32,128]{3,2,1,0:T(8,128)} %get-tuple-element.6, f32[4,2,32,128]{3,2,1,0:T(8,128)S(1)} %collective-permute-done.6), kind=kLoop, calls=%fused_computation | loop fusion | flops 98304 | bytes 655360 | tf_op jit(solution)/shard_map/add | solution.py:384
  (11 shorter events, 0.1 us)
Async XLA Ops:
  3.0 28.7 %collective-permute-start = (f32[2,8,128]{2,1,0:T(8,128)S(1)}, f32[2,8,128]{2,1,0:T(8,128)S(1)}, u32[]{:S(2)}, u32[]{:S(2)}) collective-permute-start(f32[2,8,128]{2,1,0:T(8,128)S(1)} %slice_bitcast_fusion), channel_id=1, source_target_pairs={{0,4},{4,8},{8,12},{12,16},{16,20},{20,24},{24,28},{1,5},{5,9},{9,... | collective-permute-start | bytes 24584 | tf_op jit(solution)/shard_map/ppermute | solution.py:305
  5.4 26.3 %copy-start.2 = (f32[8,2]{0,1:T(2,128)S(1)}, f32[8,2]{0,1:T(2,128)}, u32[]{:S(2)}) copy-start(f32[8,2]{0,1:T(2,128)} %param.15) | copy-start | bytes 196
  5.4 27.0 %copy-start.1 = (f32[3,8]{1,0:T(4,128)S(1)}, f32[3,8]{1,0:T(4,128)}, u32[]{:S(2)}) copy-start(f32[3,8]{1,0:T(4,128)} %param.16) | copy-start | bytes 292
  5.4 46.9 %copy-start.3 = (f32[3]{0:T(128)S(1)}, f32[3]{0:T(128)}, u32[]{:S(2)}) copy-start(f32[3]{0:T(128)} %param.17) | copy-start | bytes 40
  31.7 1.3 %copy-start = (f32[2,8,128]{2,1,0:T(8,128)}, f32[2,8,128]{2,1,0:T(8,128)S(1)}, u32[]{:S(2)}) copy-start(f32[2,8,128]{2,1,0:T(8,128)S(1)} %collective-permute-done.arrived_ref) | copy-start | bytes 24580
  35.3 4.0 %collective-permute-start.1 = (f32[4,3]{1,0:T(4,128)S(1)}, f32[4,3]{1,0:T(4,128)S(1)}, u32[]{:S(2)}, u32[]{:S(2)}) collective-permute-start(f32[4,3]{1,0:T(4,128)S(1)} %reshape.19), channel_id=1, source_target_pairs={{0,1},{1,0},{2,3},{3,2},{4,5},{5,4},{6,7},{7,6},{8,9},{9,8},{10,11... | collective-permute-start | bytes 152 | tf_op jit(solution)/shard_map/ppermute | solution.py:314
  39.3 4.6 %collective-permute-start.2 = (f32[4,3]{1,0:T(4,128)S(1)}, f32[4,3]{1,0:T(4,128)S(1)}, u32[]{:S(2)}, u32[]{:S(2)}) collective-permute-start(f32[4,3]{1,0:T(4,128)S(1)} %add.44), channel_id=1, source_target_pairs={{0,2},{1,3},{2,0},{3,1},{4,6},{5,7},{6,4},{7,5},{8,10},{9,11},{10,... | collective-permute-start | bytes 152 | tf_op jit(solution)/shard_map/ppermute | solution.py:314
  43.9 1.2 %collective-permute-start.3 = (f32[3]{0:T(128)S(1)}, f32[3]{0:T(128)S(1)}, u32[]{:S(2)}, u32[]{:S(2)}) collective-permute-start(f32[3]{0:T(128)S(1)} %get-tuple-element.10), channel_id=1, source_target_pairs={{0,4},{4,0},{8,12},{12,8},{16,20},{20,16},{24,28},{28,24},{1,5},{5... | collective-permute-start | bytes 44 | tf_op jit(solution)/shard_map/ppermute | solution.py:314
  45.2 3.6 %collective-permute-start.4 = (f32[3]{0:T(128)S(1)}, f32[3]{0:T(128)S(1)}, u32[]{:S(2)}, u32[]{:S(2)}) collective-permute-start(f32[3]{0:T(128)S(1)} %add.46), channel_id=1, source_target_pairs={{0,8},{4,12},{8,0},{12,4},{16,24},{20,28},{24,16},{28,20},{1,9},{5... | collective-permute-start | bytes 44 | tf_op jit(solution)/shard_map/ppermute | solution.py:314
  48.7 3.6 %collective-permute-start.5 = (f32[3]{0:T(128)S(1)}, f32[3]{0:T(128)S(1)}, u32[]{:S(2)}, u32[]{:S(2)}) collective-permute-start(f32[3]{0:T(128)S(1)} %add.48), channel_id=1, source_target_pairs={{0,16},{4,20},{8,24},{12,28},{16,0},{20,4},{24,8},{28,12},{1,17},{... | collective-permute-start | bytes 44 | tf_op jit(solution)/shard_map/ppermute | solution.py:314
  56.3 8.5 %collective-permute-start.6 = (f32[4,2,32,128]{3,2,1,0:T(8,128)}, f32[4,2,32,128]{3,2,1,0:T(8,128)S(1)}, u32[]{:S(2)}, u32[]{:S(2)}) collective-permute-start(f32[4,2,32,128]{3,2,1,0:T(8,128)} %get-tuple-element.7), channel_id=1, source_target_pairs={{0,1},{1,2},{2,3},{3,0},{4,5},{5,6},{6,7},{7,4},{8,9},{9,10},{10,1... | collective-permute-start | bytes 393224 | tf_op jit(solution)/shard_map/ppermute | solution.py:310
  58.2 9.9 %collective-permute-start.7 = (f32[4,2,32,128]{3,2,1,0:T(8,128)}, f32[4,2,32,128]{3,2,1,0:T(8,128)S(1)}, u32[]{:S(2)}, u32[]{:S(2)}) collective-permute-start(f32[4,2,32,128]{3,2,1,0:T(8,128)} %get-tuple-element.8), channel_id=1, source_target_pairs={{0,2},{1,3},{2,0},{3,1},{4,6},{5,7},{6,4},{7,5},{8,10},{9,11},{10,... | collective-permute-start | bytes 393224 | tf_op jit(solution)/shard_map/ppermute | solution.py:310
  60.8 7.3 %collective-permute-start.8 = (f32[4,2,32,128]{3,2,1,0:T(8,128)}, f32[4,2,32,128]{3,2,1,0:T(8,128)S(1)}, u32[]{:S(2)}, u32[]{:S(2)}) collective-permute-start(f32[4,2,32,128]{3,2,1,0:T(8,128)} %get-tuple-element.9), channel_id=1, source_target_pairs={{0,3},{1,0},{2,1},{3,2},{4,7},{5,4},{6,5},{7,6},{8,11},{9,8},{10,9... | collective-permute-start | bytes 393224 | tf_op jit(solution)/shard_map/ppermute | solution.py:310

commit v3 on v2

v3 whole, which is shorter than its diff:
```python
import functools
from jax._src.pallas.mosaic import core
import math

import jax
import jax.numpy as jnp
import ml_dtypes
import numpy as np
from jax import lax
from jax.experimental import pallas as pl
from jax.experimental.pallas import tpu as pltpu
from jax.sharding import PartitionSpec as P

BF16 = jnp.bfloat16
F32 = jnp.float32


def dft_tables(side):
    offsets = np.arange(side) - side // 2
    wrapped = np.mod(offsets[:, None] * offsets[None, :], side).astype(np.float32)
    phase = np.float32(2.0 * math.pi / side) * wrapped
    cosine = (np.cos(phase) / np.float32(side)).astype(ml_dtypes.bfloat16)
    sine = (np.sin(phase) / np.float32(side)).astype(ml_dtypes.bfloat16)
    right = np.block([[cosine, sine], [-sine, cosine]])
    left = np.block([[cosine, -sine], [sine, cosine]])
    return right, left


def windows(readout, segs):
    spacing, jitter = readout // segs, readout // (4 * segs)
    low = [0] + [j * spacing - jitter for j in range(1, segs)]
    high = [j * spacing + jitter for j in range(1, segs)] + [readout]
    width = 128
    while True:
        starts = [max(0, min(a // 16 * 16, readout - width)) for a in low]
        if all(s + width >= b for s, b in zip(starts, high)) or width >= readout:
            return starts, min(width, readout)
        width += 128


def edges_of(bounds_ref, readout, segs):
    return [0] + [bounds_ref[j] for j in range(segs - 1)] + [readout]


def centres(kdata_ref, center_ref, last_ref):
    frames, coils = kdata_ref.shape[:2]
    for t in range(frames):
        for c in range(coils):
            total = kdata_ref[t, c, 0].astype(F32)
            for s in range(1, kdata_ref.shape[2]):
                total += kdata_ref[t, c, s].astype(F32)
            for p in range(2):
                center_ref[t, p, c, :] = total[p]
                if t == frames - 1:
                    last_ref[p, c, :] = total[p]


def drift(position_ref, projection_ref, center_ref, arrived_ref, first_ref, step_ref):
    frames, _, coils, lanes = center_ref.shape
    basis = projection_ref.shape[0]
    at_start = position_ref[0] == 0
    row = lax.broadcasted_iota(jnp.int32, (coils, lanes), 0)
    weights = []
    for b in range(basis):
        weight = jnp.zeros((coils, lanes), F32)
        for c in range(coils):
            weight = jnp.where(row == c, projection_ref[b, c], weight)
        weights.append(weight)
    step_ref[...] = jnp.zeros(step_ref.shape, F32)
    totals = [jnp.zeros((1, lanes), F32)] * basis
    for t in range(frames):
        if t == 0:
            before = [
                jnp.where(at_start, jnp.broadcast_to(first_ref[:, p : p + 1], (coils, lanes)), arrived_ref[p])
                for p in range(2)
            ]
        else:
            before = [center_ref[t - 1, p] for p in range(2)]
        now = [center_ref[t, p] for p in range(2)]
        cross = before[0] * now[1] - before[1] * now[0]
        energy = before[0] * before[0] + before[1] * before[1]
        energy = energy + (now[0] * now[0] + now[1] * now[1]) + 1.0
        signal = 2.0 * cross / energy
        for b in range(basis):
            part = jnp.sum(weights[b] * signal, axis=0, keepdims=True)
            step_ref[pl.ds(t * basis + b, 1), :] = part
            totals[b] = totals[b] + part
    for b in range(basis):
        step_ref[pl.ds(frames * basis + b, 1), :] = totals[b]


def grid_frames(starts, width, first, count, angles_ref, bounds_ref, kdata_ref, tables_ref, right_ref, left_ref, sens_ref, out_ref):
    _, coils, spokes, _, readout = kdata_ref.shape
    _, table, _, side = tables_ref.shape
    segs = len(starts)
    most = (spokes + 1) // 2
    least = min(3, most)
    pairs = coils // 2
    steps = count * pairs
    lanes = 128
    room = max(8, 2 * coils)
    group = lanes // room
    groups = (2 * most + group - 1) // group
    cut = 32
    cuts = side // cut

    def body(kd, flipped, columns, rows, weighted, halves, ky, right, left, slot_of, angle_of, tiles_of, *accs):
        banks = [[accs[(m * 8 + b) * cuts : (m * 8 + b + 1) * cuts] for b in range(8)] for m in range(2)]
        grid_acc = [banks[m][:3] for m in range(2)]
        half_acc = [banks[m][3:5] for m in range(2)]
        image_acc = [banks[m][5:] for m in range(2)]

        def multiply(bank, lhs, staged):
            for r in range(cuts):
                pltpu.matmul_acc_lhs(bank[r], lhs[r * cut : (r + 1) * cut], load_staged_rhs=None if r else staged)
        edges = edges_of(bounds_ref, readout, segs)
        index = lax.broadcasted_iota(jnp.int32, (width, side), 0)
        keep = []
        for l in range(segs):
            at = index + starts[l]
            keep.append(jnp.where((at >= edges[l]) & (at < edges[l + 1]), 1.0, 0.0).astype(BF16))

        def angle_tables(a, carry):
            ky[a] = tables_ref[1, a]
            for l in range(segs):
                rows[a, l] = (tables_ref[0, a, starts[l] : starts[l] + width, :] * keep[l]).T
            return carry

        lax.fori_loop(0, table, angle_tables, 0)
        ky[table] = jnp.zeros((readout, side), BF16)
        rows[table] = jnp.zeros((segs, side, width), BF16)
        right[...] = right_ref[...]
        left[...] = left_ref[...]
        halves[...] = jnp.zeros(halves.shape, BF16)
        out_ref[...] = jnp.zeros(out_ref.shape, F32)

        def gather(i, carry):
            kd[...] = jnp.zeros(kd.shape, F32)
            for a in range(table):
                slot_of[a] = -1
            for n in range(2 * most):
                angle_of[i, n] = table
            used = jnp.int32(0)
            for s in range(spokes):
                a = angles_ref[first + i, s]
                old = slot_of[a]
                slot = jnp.where(old < 0, used, old)
                used = used + jnp.where(old < 0, 1, 0)
                slot_of[a] = slot
                angle_of[i, slot] = a
                for c in range(coils):
                    kd[slot, 2 * c : 2 * c + 2, :] += kdata_ref[first + i, c, s].astype(F32)
            tiles_of[i] = jnp.maximum(lax.div(used + 1, 2), least)
            for g in range(groups):
                flipped[i, g] = kd[g * group : (g + 1) * group].reshape(lanes, readout).T
            return carry

        lax.fori_loop(0, count, gather, 0)

        def place(step):
            return lax.div(step, pairs), lax.rem(step, pairs)

        def own_columns(step):
            i, n = place(step)
            for g in range(groups):
                columns[g] = pltpu.roll(flipped[i, g], lanes - 4 * n, 1).astype(BF16)

        def weigh(step, k, buf):
            i, _ = place(step)
            for e in range(2):
                slot = 2 * k + e
                factor = ky[angle_of[i, slot]]
                for m in range(2):
                    for p in range(2):
                        lane = slot % group * room + 2 * m + p
                        column = columns[slot // group, :, lane : lane + 1]
                        weighted[buf, m, p, e] = jnp.broadcast_to(column, (readout, side)) * factor

        def beside(blocks):
            return jnp.concatenate(blocks, axis=1)

        def grid_tile(step, buf, l, k):
            i, _ = place(step)
            for m in range(2):
                rhs = beside([
                    weighted[buf, m, p, :, starts[l] : starts[l] + width, :].reshape(2 * width, side) for p in range(2)
                ])
                pltpu.matmul_push_rhs(rhs, l % 2, m)
            lhs = beside([rows[angle_of[i, 2 * k + e], l] for e in range(2)])
            for m in range(2):
                multiply(grid_acc[m][l], lhs, l % 2)

        def over_columns(l):
            for m in range(2):
                pltpu.matmul_push_rhs(beside([right[0], right[1]]), 1, m)
            for r in range(cuts):
                for m in range(2):
                    gridded = pltpu.matmul_pop(grid_acc[m][l][r]).astype(BF16)
                    pltpu.matmul_acc_lhs(half_acc[m][l % 2][r], gridded, load_staged_rhs=None if r else 1)

        def keep_half(l):
            for r in range(cuts):
                for m in range(2):
                    half = pltpu.matmul_pop(half_acc[m][l % 2][r]).astype(BF16)
                    halves[m, l, 0, r * cut : (r + 1) * cut] = half[:, :side]
                    halves[m, l, 1, r * cut : (r + 1) * cut] = half[:, side:]

        def left_rows(h):
            return beside([left[q, h * side : (h + 1) * side] for q in range(2)])

        def over_rows():
            for m in range(2):
                both = beside([halves[m, l].reshape(2 * side, side) for l in range(2)])
                pltpu.matmul_push_rhs(both, 0, m)
            last = beside([halves[m, 2].reshape(2 * side, side) for m in range(2)])
            for m in range(2):
                pltpu.matmul_push_rhs(last, 1, m)
            for h in range(2):
                for m in range(2):
                    multiply(image_acc[m][h], left_rows(h), 0 if h == 0 else None)
            for m in range(2):
                multiply(image_acc[m][2], left_rows(m), 1)

        def combine(step, r):
            i, n = place(step)
            here = pl.ds(r * cut, cut)
            real = [sens_ref[2 * n + m, 0, here].astype(F32) for m in range(2)]
            imag = [sens_ref[2 * n + m, 1, here].astype(F32) for m in range(2)]

            def add(l, parts):
                total_re, total_im = out_ref[i, l, 0, here], out_ref[i, l, 1, here]
                for m in range(2):
                    re, im = parts[m]
                    total_re += real[m] * re + imag[m] * im
                    total_im += real[m] * im - imag[m] * re
                out_ref[i, l, 0, here] = total_re
                out_ref[i, l, 1, here] = total_im

            images = [[pltpu.matmul_pop(image_acc[m][h][r]) for h in range(2)] for m in range(2)]
            for l in range(2):
                add(l, [[part[:, l * side : (l + 1) * side] for part in images[m]] for m in range(2)])
            images = [pltpu.matmul_pop(image_acc[h][2][r]) for h in range(2)]
            add(2, [[part[:, m * side : (m + 1) * side] for part in images] for m in range(2)])

        def phase(tiles, step):
            earlier = jnp.maximum(step - 1, 0)
            following = jnp.minimum(step + 1, steps - 1)
            left_over = list(range(cuts))
            for k in range(tiles):
                buf = k % 2 if k else 2
                last = k == tiles - 1
                if last:
                    weigh(following, 0, 2)
                else:
                    weigh(step, k + 1, (k + 1) % 2)
                for l in range(segs):
                    grid_tile(step, buf, l, k)
                    if k == 0 and l < 2:
                        over_columns(l + 1)
                    if k >= 2 and (l or k > 2) and left_over:
                        combine(earlier, left_over.pop(0))
                    if k == tiles - 2 and l == 1:
                        own_columns(following)
                    if last and l == 1:
                        over_columns(0)
                if k == 0:
                    keep_half(1)
                    keep_half(2)
                if k == 1:
                    over_rows()
            keep_half(0)
            for r in left_over:
                combine(earlier, r)

        own_columns(0)
        weigh(0, 0, 2)

        def one(step, carry):
            i, _ = place(step)
            tiles = tiles_of[i]
            for option in range(least, most + 1):
                pl.when(tiles == option)(functools.partial(phase, option, step))
            return carry

        lax.fori_loop(0, steps, one, 0)
        over_columns(1)
        over_columns(2)
        keep_half(1)
        keep_half(2)
        over_rows()
        for r in range(cuts):
            combine(steps - 1, r)

    pl.run_scoped(
        body,
        pltpu.VMEM((groups * group, room, readout), F32),
        pltpu.VMEM((count, groups, readout, lanes), F32),
        pltpu.VMEM((groups, readout, lanes), BF16),
        pltpu.VMEM((table + 1, segs, side, width), BF16),
        pltpu.VMEM((3, 2, 2, 2, readout, side), BF16),
        pltpu.VMEM((2, segs, 2, side, side), BF16),
        pltpu.VMEM((table + 1, readout, side), BF16),
        pltpu.VMEM((2, 2 * side, side), BF16),
        pltpu.VMEM((2, 2 * side, side), BF16),
        pltpu.SMEM((table,), jnp.int32),
        pltpu.SMEM((count, 2 * most), jnp.int32),
        pltpu.SMEM((count,), jnp.int32),
        *[core.AccMemorySpace(m)((cut, 2 * side), F32) for m in range(2) for _ in range(8 * cuts)],
    )


def modulate(
    readout, position_ref, bounds_ref, init_ref, increment_ref, before_ref, parts_ref, coef_ref, *refs
):
    *out_refs, image_ref = refs
    frames, segs, _, side, _ = parts_ref.shape
    basis = init_ref.shape[0]
    owners = len(out_refs)
    rows = side // owners
    half = side // 2
    me = position_ref[0]
    edges = edges_of(bounds_ref, readout, segs)
    times = [(edges[l] + edges[l + 1] - 1).astype(F32) / (2.0 * readout) for l in range(segs)]
    running = [before_ref[pl.ds(frames * basis + b, 1), :1] for b in range(basis)]
    coef = []
    for t in range(frames):
        for b in range(basis):
            running[b] = running[b] + increment_ref[pl.ds(t * basis + b, 1), :1]
            value = init_ref[b] + running[b]
            coef.append(value)
            coef_ref[pl.ds(t * basis + b, 1), :] = jnp.broadcast_to(value, (1, coef_ref.shape[1]))
    lane = lax.broadcasted_iota(jnp.int32, (1, 128), 1)
    base = jnp.zeros((1, 128), F32)
    slope = jnp.zeros((1, 128), F32)
    scale = jnp.zeros((1, 128), F32)
    for t in range(frames):
        for l in range(segs):
            here = lane == t * segs + l
            base = jnp.where(here, coef[t * basis], base)
            slope = jnp.where(here, coef[t * basis + 1], slope)
            scale = jnp.where(here, times[l], scale)
    down_pos = (lax.broadcasted_iota(jnp.int32, (side, 128), 0) - half).astype(F32) / half
    down = (base + slope * down_pos) * scale
    cos_down, sin_down = jnp.cos(down), jnp.sin(down)
    across_pos = (lax.broadcasted_iota(jnp.int32, (1, side), 1) - half).astype(F32) / half
    across = jnp.concatenate(
        [coef[t * basis + 2] * across_pos * times[l] for t in range(frames) for l in range(segs)], axis=0
    )
    cos_across, sin_across = jnp.cos(across), jnp.sin(across)
    for t in range(frames):
        image_re = jnp.zeros((side, side), F32)
        image_im = jnp.zeros((side, side), F32)
        for l in range(segs):
            n = t * segs + l
            cr, sr = cos_down[:, n : n + 1], sin_down[:, n : n + 1]
            cc, sc = cos_across[n : n + 1], sin_across[n : n + 1]
            cos = cr * cc - sr * sc
            sin = sr * cc + cr * sc
            re, im = parts_ref[t, l, 0], parts_ref[t, l, 1]
            image_re += cos * re - sin * im
            image_im += sin * re + cos * im
        image_ref[0] = image_re
        image_ref[1] = image_im
        for d, out_ref in enumerate(out_refs):
            owned = pl.multiple_of(lax.rem(me + d, owners) * rows, rows)
            out_ref[t] = image_ref[:, pl.ds(owned, rows), :]


def shifted(block, axis, distance):
    count = lax.axis_size(axis)
    return lax.ppermute(block, axis, [(i, i + distance) for i in range(count - distance)])


def around(block, axis, distance):
    count = lax.axis_size(axis)
    return lax.ppermute(block, axis, [(i, (i + distance) % count) for i in range(count)])


def exchanged(block, axis, distance):
    return lax.ppermute(block, axis, [(i, i ^ distance) for i in range(lax.axis_size(axis))])


def local(kdata, angles, kernels, seg_bounds, sensitivity, ref_center, projection, init_coef):
    frames, coils, _, spokes, readout = kdata.shape
    side = kernels.shape[3]
    segs = seg_bounds.shape[0] + 1
    basis = projection.shape[0]
    owners = lax.axis_size("coils")
    starts, width = windows(readout, segs)
    right, left = (jnp.stack(jnp.split(jnp.asarray(table), 2, axis=1)) for table in dft_tables(side))
    kd = jnp.swapaxes(kdata, 2, 3)
    smem = pl.BlockSpec(memory_space=pltpu.SMEM)
    vmem = pl.BlockSpec(memory_space=pltpu.VMEM)
    place = lax.axis_index("frames").astype(jnp.int32)
    owner = lax.axis_index("coils").astype(jnp.int32)

    lanes = 128
    center, last = pl.pallas_call(
        centres,
        grid=(1,),
        out_shape=(
            jax.ShapeDtypeStruct((frames, 2, coils, lanes), F32),
            jax.ShapeDtypeStruct((2, coils, lanes), F32),
        ),
        in_specs=[pl.BlockSpec((frames, coils, spokes, 2, lanes), lambda i: (0, 0, 0, 0, readout // 2 // lanes))],
        out_specs=(
            pl.BlockSpec((frames, 2, coils, lanes), lambda i: (0, 0, 0, 0)),
            pl.BlockSpec((2, coils, lanes), lambda i: (0, 0, 0)),
        ),
        name="centres",
    )(kd)
    arrived = shifted(last, "frames", 1)
    padded = ((frames + 1) * basis + 7) // 8 * 8
    increment = pl.pallas_call(
        drift,
        out_shape=jax.ShapeDtypeStruct((padded, lanes), F32),
        in_specs=[smem, smem, vmem, vmem, vmem],
        out_specs=vmem,
        name="drift",
    )(place.reshape(1), projection, center, arrived, ref_center)
    distance = 1
    while distance < owners:
        increment = increment + exchanged(increment, "coils", distance)
        distance *= 2
    running = increment
    before = jnp.zeros_like(running)
    distance = 1
    while distance < lax.axis_size("frames"):
        came = exchanged(running, "frames", distance)
        before = before + jnp.where((place & distance) != 0, came, 0.0)
        running = running + came
        distance *= 2

    parts = pl.pallas_call(
        functools.partial(grid_frames, starts, width, 0, frames),
        out_shape=jax.ShapeDtypeStruct((frames, segs, 2, side, side), F32),
        in_specs=[smem, smem, vmem, vmem, vmem, vmem, vmem],
        out_specs=vmem,
        name="gridding",
    )(angles, seg_bounds, kd, kernels, right, left, sensitivity)

    block = jax.ShapeDtypeStruct((frames, 2, side // owners, side), F32)
    coef, *blocks = pl.pallas_call(
        functools.partial(modulate, readout),
        out_shape=(jax.ShapeDtypeStruct((padded, lanes), F32),) + (block,) * owners,
        in_specs=[smem, smem, smem, vmem, vmem, vmem],
        out_specs=(vmem,) * (1 + owners),
        scratch_shapes=[pltpu.VMEM((2, side, side), F32)],
        name="modulate",
    )(owner.reshape(1), seg_bounds, init_coef, increment, before, parts)
    image = blocks[0]
    for d in range(1, owners):
        image = image + around(blocks[d], "coils", d)
    field_coef = coef[: frames * basis, 0].reshape(frames, basis)
    return (image, field_coef)


def solution(mesh):
    placed = (
        P("frames", "coils", None, None, None),
        P("frames", None),
        P(),
        P(),
        P("coils", None, None, None),
        P("coils", None),
        P(None, "coils"),
        P(),
    )
    def located(*arguments):
        with jax.sharding.use_abstract_mesh(mesh.abstract_mesh):
            return local(*arguments)

    return jax.shard_map(
        local,
        mesh=mesh,
        in_specs=placed,
        out_specs=(P("frames", None, "coils", None), P("frames", None)),
        check_vma=False,
    )
```

time: 70.1 us -> 68.9 us (0.983)
  Pallas kernels: 32.7 us -> 29.5 us
  starting transfers between devices: 17.8 us -> 20.3 us
  waiting for transfers between devices: 13.3 us -> 11.4 us
    pallas_call x1, Pallas kernels: 26.3 us -> 23.2 us  [local(): pl.pallas_call(functools.partial(grid_frames, starts, width, 0, frames),...]
    ppermute x5, starting transfers between devices: 9.6 us -> 12.3 us  [exchanged(): lax.ppermute(block, axis, [(i, i ^ distance) for i in range(lax.axis_size...]
    unnamed x8 -> x5, local copies, waits for them, and re-layouts: 0.02 us -> 1.94 us
    broadcast_in_dim x2 -> x0, local copies, waits for them, and re-layouts: 1.34 us -> none  [the longest x1 0.67 us: local(): weights = jnp.broadcast_to(projection[:, :, None], (basis, coils, lanes))]
    ppermute x5, waiting for transfers between devices: 7.29 us -> 6.24 us  [exchanged(): lax.ppermute(block, axis, [(i, i ^ distance) for i in range(lax.axis_size...]
    ppermute x3, waiting for transfers between devices: 5.97 us -> 5.15 us  [around(): lax.ppermute(block, axis, [(i, (i + distance) % count) for i in range(cou...]
  transfers between devices with their start and end apart: 9 -> 9, of which waited for: 7 -> 7; matrix products, arithmetic and copies ran while one was open for 0% -> 4% of each run, Pallas kernels for 38% -> 34%
where the time goes in v3:
time: 68.9 us; the launch traced here: 68.2 us
  Pallas kernels  29.5 us (43%)
  starting transfers between devices  20.3 us (29%)
  waiting for transfers between devices  11.4 us (17%)
  local copies, waits for them, and re-layouts  3.41 us (5%)
  other arithmetic  2.91 us (4%)
    pallas_call x1, Pallas kernels, local(): pl.pallas_call(functools.partial(grid_frames, starts, width, 0, frames),...  23.2 us
    ppermute x5, starting transfers between devices, exchanged(): lax.ppermute(block, axis, [(i, i ^ distance) for i in range(lax.axis_size...  12.3 us
    ppermute x5, waiting for transfers between devices, exchanged(): lax.ppermute(block, axis, [(i, i ^ distance) for i in range(lax.axis_size...  6.24 us
    ppermute x3, starting transfers between devices, around(): lax.ppermute(block, axis, [(i, (i + distance) % count) for i in range(cou...  5.55 us
    ppermute x3, waiting for transfers between devices, around(): lax.ppermute(block, axis, [(i, (i + distance) % count) for i in range(cou...  5.15 us
    pallas_call x1, Pallas kernels, local(): pl.pallas_call(functools.partial(modulate, readout), out_shape=(jax.Shape...  3.11 us
    ppermute x1, starting transfers between devices, shifted(): lax.ppermute(block, axis, [(i, i + distance) for i in range(count - dista...  2.38 us
    unnamed x5, local copies, waits for them, and re-layouts  1.94 us
  transfers between devices with their start and end apart: 9, of which 7 were waited for; matrix products, arithmetic and copies ran while one was open for 4% of the time, Pallas kernels for 34%

profile of v3, /device:TPU:0, one launch (start us, length us, event | category | flops | bytes accessed | tf_op | source)
XLA Modules:
  0.0 68.2 jit_solution(17152877655479702016)
XLA Ops:
  0.6 1.7 %centres.1 = (f32[4,2,8,128]{3,2,1,0:T(8,128)}, f32[2,8,128]{2,1,0:T(8,128)}) custom-call(bf16[4,8,13,2,256]{4,3,2,1,0:T(2,128)(2,1)} %bitcast.3), custom_call_target="tpu_custom_call" | custom-call | tf_op jit(solution)/shard_map/centres/pallas_call | solution.py:398
  2.3 2.4 %collective-permute-start = (f32[2,8,128]{2,1,0:T(8,128)}, f32[2,8,128]{2,1,0:T(8,128)S(1)}, u32[]{:S(2)}, u32[]{:S(2)}) collective-permute-start(f32[2,8,128]{2,1,0:T(8,128)} %get-tuple-element.10), channel_id=1, source_target_pairs={{0,4},{4,8},{8,12},{12,16},{16,20},{20,24},{24,28},{1,5},{5,9},{9,... | collective-permute-start | bytes 24584 | tf_op jit(solution)/shard_map/ppermute | solution.py:371
  4.7 1.3 %copy.13.first_ref = f32[8,2]{1,0:T(8,128)} copy(f32[8,2]{0,1:T(2,128)} %param.15) | data formatting | bytes 128 | tf_op args[5]
  6.0 0.0 collective-permute-done.arrived_ref
  6.0 0.0 copy-start.1
  6.0 0.6 copy-done.1
  6.6 1.5 %drift.1 = f32[16,128]{1,0:T(8,128)} custom-call(s32[1]{0:T(128)} %bitcast.1.position_ref, f32[3,8]{1,0:T(4,128)} %projection_ref.1, f32[4,2,8,128]{3,2,1,0:T(8,128)} %get-tuple-element.9.center_ref, f32[2,8,128]{2,1,0:T(8,128)} %copy-done.1, f32[8,2]{1,0:T(8,128)} %copy.13.first_ref), custom_call_target="tpu_custom_call" | custom-call | tf_op jit(solution)/shard_map/drift/pallas_call | solution.py:414
  8.1 2.4 %collective-permute-start.1 = (f32[16,128]{1,0:T(8,128)}, f32[16,128]{1,0:T(8,128)S(1)}, u32[]{:S(2)}, u32[]{:S(2)}) collective-permute-start(f32[16,128]{1,0:T(8,128)} %drift.1), channel_id=1, source_target_pairs={{0,1},{1,0},{2,3},{3,2},{4,5},{5,4},{6,7},{7,6},{8,9},{9,8},{10,11... | collective-permute-start | bytes 24584 | tf_op jit(solution)/shard_map/ppermute | solution.py:380
  10.5 1.8 %collective-permute-done.1 = f32[16,128]{1,0:T(8,128)S(1)} collective-permute-done((f32[16,128]{1,0:T(8,128)}, f32[16,128]{1,0:T(8,128)S(1)}, u32[]{:S(2)}, u32[]{:S(2)}) %collective-permute-start.1) | collective-permute-done | bytes 8224 | tf_op jit(solution)/shard_map/ppermute | solution.py:380
  12.4 0.7 %add.27 = f32[16,128]{1,0:T(8,128)S(1)} add(f32[16,128]{1,0:T(8,128)} %drift.1, f32[16,128]{1,0:T(8,128)S(1)} %collective-permute-done.1) | non-fusion elementwise | flops 2048 | bytes 24576 | tf_op jit(solution)/shard_map/add | solution.py:423
  13.1 3.0 %collective-permute-start.2 = (f32[16,128]{1,0:T(8,128)S(1)}, f32[16,128]{1,0:T(8,128)S(1)}, u32[]{:S(2)}, u32[]{:S(2)}) collective-permute-start(f32[16,128]{1,0:T(8,128)S(1)} %add.27), channel_id=1, source_target_pairs={{0,2},{1,3},{2,0},{3,1},{4,6},{5,7},{6,4},{7,5},{8,10},{9,11},{10,... | collective-permute-start | bytes 24584 | tf_op jit(solution)/shard_map/ppermute | solution.py:380
  16.1 1.7 %collective-permute-done.2 = f32[16,128]{1,0:T(8,128)S(1)} collective-permute-done((f32[16,128]{1,0:T(8,128)S(1)}, f32[16,128]{1,0:T(8,128)S(1)}, u32[]{:S(2)}, u32[]{:S(2)}) %collective-permute-start.2) | collective-permute-done | bytes 8224 | tf_op jit(solution)/shard_map/ppermute | solution.py:380
  17.8 0.0 copy-start
  17.8 0.1 collective-permute-start.3
  17.9 1.1 %collective-permute-done.3 = f32[16,128]{1,0:T(8,128)S(1)} collective-permute-done((f32[16,128]{1,0:T(8,128)S(1)}, f32[16,128]{1,0:T(8,128)S(1)}, u32[]{:S(2)}, u32[]{:S(2)}) %collective-permute-start.3) | collective-permute-done | bytes 8224 | tf_op jit(solution)/shard_map/ppermute | solution.py:380
  19.0 3.8 %collective-permute-start.4 = (f32[16,128]{1,0:T(8,128)S(1)}, f32[16,128]{1,0:T(8,128)S(1)}, u32[]{:S(2)}, u32[]{:S(2)}) collective-permute-start(f32[16,128]{1,0:T(8,128)S(1)} %add.29), channel_id=1, source_target_pairs={{0,8},{4,12},{8,0},{12,4},{16,24},{20,28},{24,16},{28,20},{1,9},{5... | collective-permute-start | bytes 24584 | tf_op jit(solution)/shard_map/ppermute | solution.py:380
  22.8 1.6 %collective-permute-done.4 = f32[16,128]{1,0:T(8,128)S(1)} collective-permute-done((f32[16,128]{1,0:T(8,128)S(1)}, f32[16,128]{1,0:T(8,128)S(1)}, u32[]{:S(2)}, u32[]{:S(2)}) %collective-permute-start.4) | collective-permute-done | bytes 8224 | tf_op jit(solution)/shard_map/ppermute | solution.py:380
  24.5 3.0 %collective-permute-start.5 = (f32[16,128]{1,0:T(8,128)S(1)}, f32[16,128]{1,0:T(8,128)S(1)}, u32[]{:S(2)}, u32[]{:S(2)}) collective-permute-start(f32[16,128]{1,0:T(8,128)S(1)} %add.31), channel_id=1, source_target_pairs={{0,16},{4,20},{8,24},{12,28},{16,0},{20,4},{24,8},{28,12},{1,17},{... | collective-permute-start | bytes 24584 | tf_op jit(solution)/shard_map/ppermute | solution.py:380
  27.4 23.2 %gridding.1.parts_ref = f32[4,3,2,128,128]{4,3,2,1,0:T(8,128)} custom-call(s32[4,13]{1,0:T(4,128)} %angles_ref.1, s32[2]{0:T(128)} %bounds_ref.3, bf16[4,8,13,2,256]{4,3,2,1,0:T(2,128)(2,1)} %bitcast.4, bf16[2,16,256,128]{3,2,1,0:T(8,128)(2,1)} %tables_ref.1, bf16[2,256,128]{2,1,0:T(8,128)(2,1)} %constant.31.right_ref, ...), custom_call_target="tpu_custom_call" | custom-call | tf_op jit(solution)/shard_map/gridding/pallas_call | solution.py:434
  50.7 0.0 copy-done
  50.7 0.0 collective-permute-done.5
  50.7 0.6 select_add_fusion.before_ref
  51.3 3.1 %modulate.1 = (f32[16,128]{1,0:T(8,128)}, f32[4,2,32,128]{3,2,1,0:T(8,128)}, f32[4,2,32,128]{3,2,1,0:T(8,128)}, f32[4,2,32,128]{3,2,1,0:T(8,128)}, f32[4,2,32,128]{3,2,1,0:T(8,128)}) custom-call(s32[1]{0:T(128)} %bitcast.position_ref, s32[2]{0:T(128)} %bounds_ref.3, f32[3]{0:T(128)} %init_ref.1, f32[16,128]{1,0:T(8,128)} %copy-done, ...), custom_call_target="tpu_custom_call" | custom-call | tf_op jit(solution)/shard_map/modulate/pallas_call | solution.py:443
  54.4 1.6 %collective-permute-start.6 = (f32[4,2,32,128]{3,2,1,0:T(8,128)}, f32[4,2,32,128]{3,2,1,0:T(8,128)S(1)}, u32[]{:S(2)}, u32[]{:S(2)}) collective-permute-start(f32[4,2,32,128]{3,2,1,0:T(8,128)} %get-tuple-element.12), channel_id=1, source_target_pairs={{0,1},{1,2},{2,3},{3,0},{4,5},{5,6},{6,7},{7,4},{8,9},{9,10},{10,1... | collective-permute-start | bytes 393224 | tf_op jit(solution)/shard_map/ppermute | solution.py:376
  56.0 2.6 %collective-permute-start.7 = (f32[4,2,32,128]{3,2,1,0:T(8,128)}, f32[4,2,32,128]{3,2,1,0:T(8,128)S(1)}, u32[]{:S(2)}, u32[]{:S(2)}) collective-permute-start(f32[4,2,32,128]{3,2,1,0:T(8,128)} %get-tuple-element.13), channel_id=1, source_target_pairs={{0,2},{1,3},{2,0},{3,1},{4,6},{5,7},{6,4},{7,5},{8,10},{9,11},{10,... | collective-permute-start | bytes 393224 | tf_op jit(solution)/shard_map/ppermute | solution.py:376
  58.6 1.4 %collective-permute-start.8 = (f32[4,2,32,128]{3,2,1,0:T(8,128)}, f32[4,2,32,128]{3,2,1,0:T(8,128)S(1)}, u32[]{:S(2)}, u32[]{:S(2)}) collective-permute-start(f32[4,2,32,128]{3,2,1,0:T(8,128)} %get-tuple-element.14), channel_id=1, source_target_pairs={{0,3},{1,0},{2,1},{3,2},{4,7},{5,4},{6,5},{7,6},{8,11},{9,8},{10,9... | collective-permute-start | bytes 393224 | tf_op jit(solution)/shard_map/ppermute | solution.py:376
  59.9 0.8 %slice_reduce_fusion = f32[12]{0:T(128)S(1)} fusion(f32[16,128]{1,0:T(8,128)} %get-tuple-element.15), kind=kLoop, calls=%fused_computation.1 | loop fusion | bytes 96 | tf_op jit(solution)/shard_map/slice | solution.py:454
  60.7 0.7 reshape_squeeze.3
  61.4 1.4 %collective-permute-done.6 = f32[4,2,32,128]{3,2,1,0:T(8,128)S(1)} collective-permute-done((f32[4,2,32,128]{3,2,1,0:T(8,128)}, f32[4,2,32,128]{3,2,1,0:T(8,128)S(1)}, u32[]{:S(2)}, u32[]{:S(2)}) %collective-permute-start.6) | collective-permute-done | bytes 131104 | tf_op jit(solution)/shard_map/ppermute | solution.py:376
  62.8 3.7 %collective-permute-done.7 = f32[4,2,32,128]{3,2,1,0:T(8,128)S(1)} collective-permute-done((f32[4,2,32,128]{3,2,1,0:T(8,128)}, f32[4,2,32,128]{3,2,1,0:T(8,128)S(1)}, u32[]{:S(2)}, u32[]{:S(2)}) %collective-permute-start.7) | collective-permute-done | bytes 131104 | tf_op jit(solution)/shard_map/ppermute | solution.py:376
  66.5 0.1 collective-permute-done.8
  66.6 1.6 %add_add_fusion = f32[4,2,32,128]{3,2,1,0:T(8,128)} fusion(f32[4,2,32,128]{3,2,1,0:T(8,128)S(1)} %collective-permute-done.8, f32[4,2,32,128]{3,2,1,0:T(8,128)S(1)} %collective-permute-done.7, f32[4,2,32,128]{3,2,1,0:T(8,128)} %get-tuple-element.11, f32[4,2,32,128]{3,2,1,0:T(8,128)S(1)} %collective-permute-done.6), kind=kLoop, calls=%fused_computation | loop fusion | flops 98304 | bytes 655360 | tf_op jit(solution)/shard_map/add | solution.py:453
  (3 shorter events, 0.0 us)
Async XLA Ops:
  2.3 3.7 %collective-permute-start = (f32[2,8,128]{2,1,0:T(8,128)}, f32[2,8,128]{2,1,0:T(8,128)S(1)}, u32[]{:S(2)}, u32[]{:S(2)}) collective-permute-start(f32[2,8,128]{2,1,0:T(8,128)} %get-tuple-element.10), channel_id=1, source_target_pairs={{0,4},{4,8},{8,12},{12,16},{16,20},{20,24},{24,28},{1,5},{5,9},{9,... | collective-permute-start | bytes 24584 | tf_op jit(solution)/shard_map/ppermute | solution.py:371
  6.0 0.6 copy-start.1
  8.1 4.2 %collective-permute-start.1 = (f32[16,128]{1,0:T(8,128)}, f32[16,128]{1,0:T(8,128)S(1)}, u32[]{:S(2)}, u32[]{:S(2)}) collective-permute-start(f32[16,128]{1,0:T(8,128)} %drift.1), channel_id=1, source_target_pairs={{0,1},{1,0},{2,3},{3,2},{4,5},{5,4},{6,7},{7,6},{8,9},{9,8},{10,11... | collective-permute-start | bytes 24584 | tf_op jit(solution)/shard_map/ppermute | solution.py:380
  13.1 4.7 %collective-permute-start.2 = (f32[16,128]{1,0:T(8,128)S(1)}, f32[16,128]{1,0:T(8,128)S(1)}, u32[]{:S(2)}, u32[]{:S(2)}) collective-permute-start(f32[16,128]{1,0:T(8,128)S(1)} %add.27), channel_id=1, source_target_pairs={{0,2},{1,3},{2,0},{3,1},{4,6},{5,7},{6,4},{7,5},{8,10},{9,11},{10,... | collective-permute-start | bytes 24584 | tf_op jit(solution)/shard_map/ppermute | solution.py:380
  17.8 32.8 %copy-start = (f32[16,128]{1,0:T(8,128)}, f32[16,128]{1,0:T(8,128)S(1)}, u32[]{:S(2)}) copy-start(f32[16,128]{1,0:T(8,128)S(1)} %add.28.increment_ref) | copy-start | bytes 24580
  17.8 1.2 %collective-permute-start.3 = (f32[16,128]{1,0:T(8,128)S(1)}, f32[16,128]{1,0:T(8,128)S(1)}, u32[]{:S(2)}, u32[]{:S(2)}) collective-permute-start(f32[16,128]{1,0:T(8,128)S(1)} %add.28.increment_ref), channel_id=1, source_target_pairs={{0,4},{4,0},{8,12},{12,8},{16,20},{20,16},{24,28},{28,24},{1,5},{5... | collective-permute-start | bytes 24584 | tf_op jit(solution)/shard_map/ppermute | solution.py:380
  19.0 5.5 %collective-permute-start.4 = (f32[16,128]{1,0:T(8,128)S(1)}, f32[16,128]{1,0:T(8,128)S(1)}, u32[]{:S(2)}, u32[]{:S(2)}) collective-permute-start(f32[16,128]{1,0:T(8,128)S(1)} %add.29), channel_id=1, source_target_pairs={{0,8},{4,12},{8,0},{12,4},{16,24},{20,28},{24,16},{28,20},{1,9},{5... | collective-permute-start | bytes 24584 | tf_op jit(solution)/shard_map/ppermute | solution.py:380
  24.5 26.2 %collective-permute-start.5 = (f32[16,128]{1,0:T(8,128)S(1)}, f32[16,128]{1,0:T(8,128)S(1)}, u32[]{:S(2)}, u32[]{:S(2)}) collective-permute-start(f32[16,128]{1,0:T(8,128)S(1)} %add.31), channel_id=1, source_target_pairs={{0,16},{4,20},{8,24},{12,28},{16,0},{20,4},{24,8},{28,12},{1,17},{... | collective-permute-start | bytes 24584 | tf_op jit(solution)/shard_map/ppermute | solution.py:380
  54.4 8.5 %collective-permute-start.6 = (f32[4,2,32,128]{3,2,1,0:T(8,128)}, f32[4,2,32,128]{3,2,1,0:T(8,128)S(1)}, u32[]{:S(2)}, u32[]{:S(2)}) collective-permute-start(f32[4,2,32,128]{3,2,1,0:T(8,128)} %get-tuple-element.12), channel_id=1, source_target_pairs={{0,1},{1,2},{2,3},{3,0},{4,5},{5,6},{6,7},{7,4},{8,9},{9,10},{10,1... | collective-permute-start | bytes 393224 | tf_op jit(solution)/shard_map/ppermute | solution.py:376
  56.0 10.5 %collective-permute-start.7 = (f32[4,2,32,128]{3,2,1,0:T(8,128)}, f32[4,2,32,128]{3,2,1,0:T(8,128)S(1)}, u32[]{:S(2)}, u32[]{:S(2)}) collective-permute-start(f32[4,2,32,128]{3,2,1,0:T(8,128)} %get-tuple-element.13), channel_id=1, source_target_pairs={{0,2},{1,3},{2,0},{3,1},{4,6},{5,7},{6,4},{7,5},{8,10},{9,11},{10,... | collective-permute-start | bytes 393224 | tf_op jit(solution)/shard_map/ppermute | solution.py:376
  58.6 8.0 %collective-permute-start.8 = (f32[4,2,32,128]{3,2,1,0:T(8,128)}, f32[4,2,32,128]{3,2,1,0:T(8,128)S(1)}, u32[]{:S(2)}, u32[]{:S(2)}) collective-permute-start(f32[4,2,32,128]{3,2,1,0:T(8,128)} %get-tuple-element.14), channel_id=1, source_target_pairs={{0,3},{1,0},{2,1},{3,2},{4,7},{5,4},{6,5},{7,6},{8,11},{9,8},{10,9... | collective-permute-start | bytes 393224 | tf_op jit(solution)/shard_map/ppermute | solution.py:376

commit v4 on v3

--- a/solution.py
+++ b/solution.py
@@ -42,51 +42,29 @@
     return [0] + [bounds_ref[j] for j in range(segs - 1)] + [readout]
 
 
-def centres(kdata_ref, center_ref, last_ref):
+def centres(kdata_ref, first_ref, projection_ref, block_ref, center_ref):
     frames, coils = kdata_ref.shape[:2]
+    rows, lanes = block_ref.shape
+    basis = projection_ref.shape[0]
+    lane = lax.broadcasted_iota(jnp.int32, (rows, lanes), 1)
+    row = lax.broadcasted_iota(jnp.int32, (rows, lanes), 0)
+    if rows > coils:
+        center_ref[...] = jnp.zeros(center_ref.shape, F32)
     for t in range(frames):
         for c in range(coils):
             total = kdata_ref[t, c, 0].astype(F32)
             for s in range(1, kdata_ref.shape[2]):
                 total += kdata_ref[t, c, s].astype(F32)
             for p in range(2):
-                center_ref[t, p, c, :] = total[p]
-                if t == frames - 1:
-                    last_ref[p, c, :] = total[p]
-
-
-def drift(position_ref, projection_ref, center_ref, arrived_ref, first_ref, step_ref):
-    frames, _, coils, lanes = center_ref.shape
-    basis = projection_ref.shape[0]
-    at_start = position_ref[0] == 0
-    row = lax.broadcasted_iota(jnp.int32, (coils, lanes), 0)
-    weights = []
-    for b in range(basis):
-        weight = jnp.zeros((coils, lanes), F32)
-        for c in range(coils):
-            weight = jnp.where(row == c, projection_ref[b, c], weight)
-        weights.append(weight)
-    step_ref[...] = jnp.zeros(step_ref.shape, F32)
-    totals = [jnp.zeros((1, lanes), F32)] * basis
-    for t in range(frames):
-        if t == 0:
-            before = [
-                jnp.where(at_start, jnp.broadcast_to(first_ref[:, p : p + 1], (coils, lanes)), arrived_ref[p])
-                for p in range(2)
-            ]
-        else:
-            before = [center_ref[t - 1, p] for p in range(2)]
-        now = [center_ref[t, p] for p in range(2)]
-        cross = before[0] * now[1] - before[1] * now[0]
-        energy = before[0] * before[0] + before[1] * before[1]
-        energy = energy + (now[0] * now[0] + now[1] * now[1]) + 1.0
-        signal = 2.0 * cross / energy
-        for b in range(basis):
-            part = jnp.sum(weights[b] * signal, axis=0, keepdims=True)
-            step_ref[pl.ds(t * basis + b, 1), :] = part
-            totals[b] = totals[b] + part
-    for b in range(basis):
-        step_ref[pl.ds(frames * basis + b, 1), :] = totals[b]
+                center_ref[2 * t + p, c, :] = total[p]
+    block = jnp.zeros((rows, lanes), F32)
+    for c in range(coils):
+        values = [first_ref[p, c] for p in range(2)] + [projection_ref[b, c] for b in range(basis)]
+        for n, value in enumerate(values):
+            block = jnp.where((row == c) & (lane == 2 * frames + n), value, block)
+    for n in range(2 * frames):
+        block = jnp.where(lane == n, jnp.broadcast_to(center_ref[n][:, :1], (rows, lanes)), block)
+    block_ref[...] = block
 
 
 def grid_frames(starts, width, first, count, angles_ref, bounds_ref, kdata_ref, tables_ref, right_ref, left_ref, sens_ref, out_ref):
@@ -309,23 +287,61 @@
     )
 
 
-def modulate(
-    readout, position_ref, bounds_ref, init_ref, increment_ref, before_ref, parts_ref, coef_ref, *refs
-):
-    *out_refs, image_ref = refs
+def increments(frames, basis, groups, labels, place, piece_refs, table_ref):
+    for piece_ref, names in zip(piece_refs, labels):
+        for n, (apart, coil_group) in enumerate(names):
+            table_ref[place ^ apart, coil_group] = piece_ref[n]
+    _, count, rows, lanes = table_ref.shape
+    lane = lax.broadcasted_iota(jnp.int32, (count, rows, lanes), 2)
+
+    def turned(x, by):
+        return pltpu.roll(x, by % lanes, 2)
+
+    def one(f, carry):
+        sums, own = carry
+        now = table_ref[f]
+        behind = table_ref[jnp.maximum(f - 1, 0)]
+        start = jnp.where(f == 0, turned(now, -2 * frames), turned(behind, 2 - 2 * frames))
+        before = jnp.where(lane < 2, start, turned(now, 2))
+        now_im, before_im = turned(now, -1), turned(before, -1)
+        cross = before * now_im - before_im * now
+        energy = before * before + before_im * before_im
+        energy = energy + (now * now + now_im * now_im) + 1.0
+        signal = 2.0 * cross / energy
+        for b in range(basis):
+            at = 2 * frames + 2 + b
+            part = jnp.sum(now[:, :, at : at + 1] * signal, axis=0)
+            part = jnp.sum(part, axis=0, keepdims=True)
+            sums = sums[:b] + [jnp.where(f < place, sums[b] + part, sums[b])] + sums[b + 1 :]
+            own = own[:b] + [jnp.where(f == place, part, own[b])] + own[b + 1 :]
+        return sums, own
+
+    zero = [jnp.zeros((1, lanes), F32)] * basis
+    return lax.fori_loop(0, groups, one, (zero, zero), unroll=groups <= 8)
+
+
+def modulate(readout, groups, labels, place_ref, owner_ref, bounds_ref, init_ref, parts_ref, *refs):
+    piece_refs, refs = refs[: len(labels)], refs[len(labels) :]
+    coef_ref, *out_refs, image_ref, table_ref = refs
     frames, segs, _, side, _ = parts_ref.shape
     basis = init_ref.shape[0]
     owners = len(out_refs)
     rows = side // owners
     half = side // 2
-    me = position_ref[0]
+    me = owner_ref[0]
     edges = edges_of(bounds_ref, readout, segs)
     times = [(edges[l] + edges[l + 1] - 1).astype(F32) / (2.0 * readout) for l in range(segs)]
-    running = [before_ref[pl.ds(frames * basis + b, 1), :1] for b in range(basis)]
+    sums, own = increments(frames, basis, groups, labels, place_ref[0], piece_refs, table_ref)
+    running = []
+    for b in range(basis):
+        total = sums[b][:, :1]
+        for t in range(1, frames):
+            total = total + sums[b][:, 2 * t : 2 * t + 1]
+        running.append(total)
     coef = []
     for t in range(frames):
         for b in range(basis):
-            running[b] = running[b] + increment_ref[pl.ds(t * basis + b, 1), :1]
+            running[b] = running[b] + own[b][:, 2 * t : 2 * t + 1]
             value = init_ref[b] + running[b]
             coef.append(value)
             coef_ref[pl.ds(t * basis + b, 1), :] = jnp.broadcast_to(value, (1, coef_ref.shape[1]))
@@ -366,11 +382,6 @@
             out_ref[t] = image_ref[:, pl.ds(owned, rows), :]
 
 
-def shifted(block, axis, distance):
-    count = lax.axis_size(axis)
-    return lax.ppermute(block, axis, [(i, i + distance) for i in range(count - distance)])
-
-
 def around(block, axis, distance):
     count = lax.axis_size(axis)
     return lax.ppermute(block, axis, [(i, (i + distance) % count) for i in range(count)])
@@ -378,6 +389,14 @@
 
 def exchanged(block, axis, distance):
     return lax.ppermute(block, axis, [(i, i ^ distance) for i in range(lax.axis_size(axis))])
+
+
+def exchange_rounds(axis, first, size):
+    rounds = []
+    while first < size:
+        rounds.append((axis, (2 * first, 3 * first, first) if 2 * first < size else (first,)))
+        first *= 4
+    return rounds
 
 
 def local(kdata, angles, kernels, seg_bounds, sensitivity, ref_center, projection, init_coef):
@@ -395,41 +414,31 @@
     owner = lax.axis_index("coils").astype(jnp.int32)
 
     lanes = 128
-    center, last = pl.pallas_call(
+    padded = (coils + 7) // 8 * 8
+    share = pl.pallas_call(
         centres,
         grid=(1,),
-        out_shape=(
-            jax.ShapeDtypeStruct((frames, 2, coils, lanes), F32),
-            jax.ShapeDtypeStruct((2, coils, lanes), F32),
-        ),
-        in_specs=[pl.BlockSpec((frames, coils, spokes, 2, lanes), lambda i: (0, 0, 0, 0, readout // 2 // lanes))],
-        out_specs=(
-            pl.BlockSpec((frames, 2, coils, lanes), lambda i: (0, 0, 0, 0)),
-            pl.BlockSpec((2, coils, lanes), lambda i: (0, 0, 0)),
-        ),
+        out_shape=jax.ShapeDtypeStruct((padded, lanes), F32),
+        in_specs=[
+            pl.BlockSpec((frames, coils, spokes, 2, lanes), lambda i: (0, 0, 0, 0, readout // 2 // lanes)),
+            smem,
+            smem,
+        ],
+        out_specs=pl.BlockSpec((padded, lanes), lambda i: (0, 0)),
+        scratch_shapes=[pltpu.VMEM((2 * frames, padded, lanes), F32)],
         name="centres",
-    )(kd)
-    arrived = shifted(last, "frames", 1)
-    padded = ((frames + 1) * basis + 7) // 8 * 8
-    increment = pl.pallas_call(
-        drift,
-        out_shape=jax.ShapeDtypeStruct((padded, lanes), F32),
-        in_specs=[smem, smem, vmem, vmem, vmem],
-        out_specs=vmem,
-        name="drift",
-    )(place.reshape(1), projection, center, arrived, ref_center)
-    distance = 1
-    while distance < owners:
-        increment = increment + exchanged(increment, "coils", distance)
-        distance *= 2
-    running = increment
-    before = jnp.zeros_like(running)
-    distance = 1
-    while distance < lax.axis_size("frames"):
-        came = exchanged(running, "frames", distance)
-        before = before + jnp.where((place & distance) != 0, came, 0.0)
-        running = running + came
-        distance *= 2
+    )(kd, ref_center.T, projection)
+
+    groups = lax.axis_size("frames")
+    rounds = [("frames", (1,))] + exchange_rounds("coils", 1, owners) + exchange_rounds("frames", 2, groups)
+    pieces, labels = [share[None]], [[(0, 0)]]
+    for axis, distances in rounds:
+        held = jnp.concatenate(pieces, axis=0) if len(pieces) > 1 else pieces[0]
+        names = [name for piece in labels for name in piece]
+        pieces, labels = [held], [names]
+        for distance in distances:
+            pieces.append(exchanged(held, axis, distance))
+            labels.append([(f ^ distance, c) if axis == "frames" else (f, c ^ distance) for f, c in names])
 
     parts = pl.pallas_call(
         functools.partial(grid_frames, starts, width, 0, frames),
@@ -440,14 +449,15 @@
     )(angles, seg_bounds, kd, kernels, right, left, sensitivity)
 
     block = jax.ShapeDtypeStruct((frames, 2, side // owners, side), F32)
+    height = (frames * basis + 7) // 8 * 8
     coef, *blocks = pl.pallas_call(
-        functools.partial(modulate, readout),
-        out_shape=(jax.ShapeDtypeStruct((padded, lanes), F32),) + (block,) * owners,
-        in_specs=[smem, smem, smem, vmem, vmem, vmem],
+        functools.partial(modulate, readout, groups, labels),
+        out_shape=(jax.ShapeDtypeStruct((height, lanes), F32),) + (block,) * owners,
+        in_specs=[smem, smem, smem, smem, vmem] + [vmem] * len(pieces),
         out_specs=(vmem,) * (1 + owners),
-        scratch_shapes=[pltpu.VMEM((2, side, side), F32)],
+        scratch_shapes=[pltpu.VMEM((2, side, side), F32), pltpu.VMEM((groups, owners, padded, lanes), F32)],
         name="modulate",
-    )(owner.reshape(1), seg_bounds, init_coef, increment, before, parts)
+    )(place.reshape(1), owner.reshape(1), seg_bounds, init_coef, parts, *pieces)
     image = blocks[0]
     for d in range(1, owners):
         image = image + around(blocks[d], "coils", d)

time: 68.9 us -> 59.1 us (0.86)
  starting transfers between devices: 20.3 us -> 13.4 us
  waiting for transfers between devices: 11.4 us -> 9.19 us
  Pallas kernels: 29.5 us -> 30.3 us
    ppermute x5 -> x7, starting transfers between devices: 12.3 us -> 9.54 us  [exchanged(): lax.ppermute(block, axis, [(i, i ^ distance) for i in range(lax.axis_size...]
    ppermute x1 -> x0, starting transfers between devices: 2.38 us -> none  [shifted(): lax.ppermute(block, axis, [(i, i + distance) for i in range(count - dista...]
    ppermute x3, starting transfers between devices: 5.55 us -> 3.83 us  [around(): lax.ppermute(block, axis, [(i, (i + distance) % count) for i in range(cou...]
    ppermute x5 -> x7, waiting for transfers between devices: 6.24 us -> 4.79 us  [exchanged(): lax.ppermute(block, axis, [(i, i ^ distance) for i in range(lax.axis_size...]
    pallas_call x1, Pallas kernels: 23.2 us -> 24.6 us  [local(): pl.pallas_call(functools.partial(grid_frames, starts, width, 0, frames),...]
    add x5 -> x0, other arithmetic: 1.32 us -> none  [the longest x2 0.7 us: local(): increment = increment + exchanged(increment, 'coils', distance)]
    ppermute x3, waiting for transfers between devices: 5.15 us -> 4.4 us  [around(): lax.ppermute(block, axis, [(i, (i + distance) % count) for i in range(cou...]
    unnamed x5 -> x12, local copies, waits for them, and re-layouts: 1.94 us -> 1.31 us
  transfers between devices with their start and end apart: 9 -> 10, of which waited for: 7 -> 4; matrix products, arithmetic and copies ran while one was open for 4% -> 4% of each run, Pallas kernels for 34% -> 42%
where the time goes in v4:
time: 59.1 us; the launch traced here: 58.6 us
  Pallas kernels  30.3 us (51%)
  starting transfers between devices  13.4 us (23%)
  waiting for transfers between devices  9.19 us (16%)
  local copies, waits for them, and re-layouts  2.78 us (5%)
  other arithmetic  2.28 us (4%)
  between operations  0.71 us (1%)
    pallas_call x1, Pallas kernels, local(): pl.pallas_call(functools.partial(grid_frames, starts, width, 0, frames),...  24.6 us
    ppermute x7, starting transfers between devices, exchanged(): lax.ppermute(block, axis, [(i, i ^ distance) for i in range(lax.axis_size...  9.54 us
    ppermute x7, waiting for transfers between devices, exchanged(): lax.ppermute(block, axis, [(i, i ^ distance) for i in range(lax.axis_size...  4.79 us
    ppermute x3, waiting for transfers between devices, around(): lax.ppermute(block, axis, [(i, (i + distance) % count) for i in range(cou...  4.4 us
    pallas_call x1, Pallas kernels, local(): pl.pallas_call(functools.partial(modulate, readout, groups, labels), out_...  3.96 us
    ppermute x3, starting transfers between devices, around(): lax.ppermute(block, axis, [(i, (i + distance) % count) for i in range(cou...  3.83 us
    pallas_call x1, Pallas kernels, local(): pl.pallas_call(centres, grid=(1,), out_shape=jax.ShapeDtypeStruct((padded...  1.73 us
    add x1, other arithmetic, local(): image = image + around(blocks[d], 'coils', d)  1.59 us
  transfers between devices with their start and end apart: 10, of which 4 were waited for; matrix products, arithmetic and copies ran while one was open for 4% of the time, Pallas kernels for 42%

profile of v4, /device:TPU:0, one launch (start us, length us, event | category | flops | bytes accessed | tf_op | source)
XLA Modules:
  0.0 58.6 jit_solution(16938467029967621791)
XLA Ops:
  0.6 1.7 %centres.1 = f32[8,128]{1,0:T(8,128)} custom-call(bf16[4,8,13,2,256]{4,3,2,1,0:T(2,128)(2,1)} %bitcast.6, f32[2,8]{1,0:T(2,128)} %bitcast.10, f32[3,8]{1,0:T(4,128)} %projection_ref.1), custom_call_target="tpu_custom_call" | custom-call | tf_op jit(solution)/shard_map/centres/pallas_call | solution.py:418
  2.4 0.5 collective-permute-start
  2.9 0.7 %constant_dynamic-update-slice_fusion.4 = f32[8,8,128]{2,1,0:T(8,128)S(1)} fusion(f32[8,128]{1,0:T(8,128)} %centres.1), kind=kLoop, calls=%fused_computation.5 | loop fusion | bytes 8192
  3.5 0.3 collective-permute-done
  3.9 0.7 %pad_maximum_fusion = f32[2,8,128]{2,1,0:T(8,128)S(1)} fusion(f32[1,8,128]{2,1,0:T(8,128)S(1)} %collective-permute-done, f32[1,8,128]{2,1,0:T(8,128)} %bitcast.9), kind=kLoop, calls=%fused_computation.6 | loop fusion | flops 2048 | bytes 16384 | tf_op jit(solution)/shard_map/concatenate | solution.py:436
  4.6 2.9 %collective-permute-start.3 = (f32[2,8,128]{2,1,0:T(8,128)S(1)}, f32[2,8,128]{2,1,0:T(8,128)S(1)}, u32[]{:S(2)}, u32[]{:S(2)}) collective-permute-start(f32[2,8,128]{2,1,0:T(8,128)S(1)} %pad_maximum_fusion), channel_id=1, source_target_pairs={{0,1},{1,0},{2,3},{3,2},{4,5},{5,4},{6,7},{7,6},{8,9},{9,8},{10,11... | collective-permute-start | bytes 24584 | tf_op jit(solution)/shard_map/ppermute | solution.py:391
  7.5 2.5 %collective-permute-start.2 = (f32[2,8,128]{2,1,0:T(8,128)S(1)}, f32[2,8,128]{2,1,0:T(8,128)S(1)}, u32[]{:S(2)}, u32[]{:S(2)}) collective-permute-start(f32[2,8,128]{2,1,0:T(8,128)S(1)} %pad_maximum_fusion), channel_id=1, source_target_pairs={{0,3},{1,2},{2,1},{3,0},{4,7},{5,6},{6,5},{7,4},{8,11},{9,10},{10,... | collective-permute-start | bytes 24584 | tf_op jit(solution)/shard_map/ppermute | solution.py:391
  10.0 0.1 collective-permute-start.1
  10.1 4.4 %collective-permute-done.1 = f32[2,8,128]{2,1,0:T(8,128)S(1)} collective-permute-done((f32[2,8,128]{2,1,0:T(8,128)S(1)}, f32[2,8,128]{2,1,0:T(8,128)S(1)}, u32[]{:S(2)}, u32[]{:S(2)}) %collective-permute-start.1) | collective-permute-done | bytes 8224 | tf_op jit(solution)/shard_map/ppermute | solution.py:391
  14.5 0.0 collective-permute-done.2
  14.5 0.0 collective-permute-done.3
  14.5 1.6 %collective-permute-start.6 = (f32[8,8,128]{2,1,0:T(8,128)S(1)}, f32[8,8,128]{2,1,0:T(8,128)S(1)}, u32[]{:S(2)}, u32[]{:S(2)}) collective-permute-start(f32[8,8,128]{2,1,0:T(8,128)S(1)} %constant_dynamic-update-slice_fusion.refs_0_), channel_id=1, source_target_pairs={{0,8},{4,12},{8,0},{12,4},{16,24},{20,28},{24,16},{28,20},{1,9},{5... | collective-permute-start | bytes 98312 | tf_op jit(solution)/shard_map/ppermute | solution.py:391
  16.1 1.5 %collective-permute-start.5 = (f32[8,8,128]{2,1,0:T(8,128)S(1)}, f32[8,8,128]{2,1,0:T(8,128)S(1)}, u32[]{:S(2)}, u32[]{:S(2)}) collective-permute-start(f32[8,8,128]{2,1,0:T(8,128)S(1)} %constant_dynamic-update-slice_fusion.refs_0_), channel_id=1, source_target_pairs={{0,24},{4,28},{8,16},{12,20},{16,8},{20,12},{24,0},{28,4},{1,25},{... | collective-permute-start | bytes 98312 | tf_op jit(solution)/shard_map/ppermute | solution.py:391
  17.6 0.5 collective-permute-start.4
  18.1 24.6 %gridding.1.parts_ref = f32[4,3,2,128,128]{4,3,2,1,0:T(8,128)} custom-call(s32[4,13]{1,0:T(4,128)} %angles_ref.1, s32[2]{0:T(128)} %bounds_ref.3, bf16[4,8,13,2,256]{4,3,2,1,0:T(2,128)(2,1)} %bitcast.7, bf16[2,16,256,128]{3,2,1,0:T(8,128)(2,1)} %tables_ref.1, bf16[2,256,128]{2,1,0:T(8,128)(2,1)} %constant.21.right_ref, ...), custom_call_target="tpu_custom_call" | custom-call | tf_op jit(solution)/shard_map/gridding/pallas_call | solution.py:443
  42.7 0.0 collective-permute-done.6.refs_3_
  42.7 0.0 collective-permute-done.5.refs_2_
  42.7 0.0 copy-start.2
  42.7 0.0 collective-permute-done.4.refs_1_
  42.8 0.6 copy-done.1
  43.3 0.0 copy-done.2
  43.3 0.0 copy-done.3
  43.4 4.0 %modulate.1 = (f32[16,128]{1,0:T(8,128)}, f32[4,2,32,128]{3,2,1,0:T(8,128)}, f32[4,2,32,128]{3,2,1,0:T(8,128)}, f32[4,2,32,128]{3,2,1,0:T(8,128)}, f32[4,2,32,128]{3,2,1,0:T(8,128)}) custom-call(s32[1]{0:T(128)} %bitcast.place_ref, s32[1]{0:T(128)} %bitcast.1.owner_ref, s32[2]{0:T(128)} %bounds_ref.3, f32[3]{0:T(128)} %init_ref.1, ...), custom_call_target="tpu_custom_call" | custom-call | tf_op jit(solution)/shard_map/modulate/pallas_call | solution.py:453
  47.3 0.7 %collective-permute-start.7 = (f32[4,2,32,128]{3,2,1,0:T(8,128)}, f32[4,2,32,128]{3,2,1,0:T(8,128)S(1)}, u32[]{:S(2)}, u32[]{:S(2)}) collective-permute-start(f32[4,2,32,128]{3,2,1,0:T(8,128)} %get-tuple-element.8), channel_id=1, source_target_pairs={{0,1},{1,2},{2,3},{3,0},{4,5},{5,6},{6,7},{7,4},{8,9},{9,10},{10,1... | collective-permute-start | bytes 393224 | tf_op jit(solution)/shard_map/ppermute | solution.py:387
  48.0 1.2 %collective-permute-start.8 = (f32[4,2,32,128]{3,2,1,0:T(8,128)}, f32[4,2,32,128]{3,2,1,0:T(8,128)S(1)}, u32[]{:S(2)}, u32[]{:S(2)}) collective-permute-start(f32[4,2,32,128]{3,2,1,0:T(8,128)} %get-tuple-element.9), channel_id=1, source_target_pairs={{0,2},{1,3},{2,0},{3,1},{4,6},{5,7},{6,4},{7,5},{8,10},{9,11},{10,... | collective-permute-start | bytes 393224 | tf_op jit(solution)/shard_map/ppermute | solution.py:387
  49.2 1.9 %collective-permute-start.9 = (f32[4,2,32,128]{3,2,1,0:T(8,128)}, f32[4,2,32,128]{3,2,1,0:T(8,128)S(1)}, u32[]{:S(2)}, u32[]{:S(2)}) collective-permute-start(f32[4,2,32,128]{3,2,1,0:T(8,128)} %get-tuple-element.10), channel_id=1, source_target_pairs={{0,3},{1,0},{2,1},{3,2},{4,7},{5,4},{6,5},{7,6},{8,11},{9,8},{10,9... | collective-permute-start | bytes 393224 | tf_op jit(solution)/shard_map/ppermute | solution.py:387
  51.2 0.8 %slice_reduce_fusion = f32[12]{0:T(128)S(1)} fusion(f32[16,128]{1,0:T(8,128)} %get-tuple-element.11), kind=kLoop, calls=%fused_computation.7 | loop fusion | bytes 96 | tf_op jit(solution)/shard_map/slice | solution.py:464
  52.0 0.7 %reshape_squeeze.3 = f32[4,3]{1,0:T(4,128)} reshape(f32[12]{0:T(128)S(1)} %slice_reduce_fusion) | data formatting | bytes 96 | tf_op jit(solution)/shard_map/reshape;squeeze | solution.py:464
  52.6 1.9 %collective-permute-done.7 = f32[4,2,32,128]{3,2,1,0:T(8,128)S(1)} collective-permute-done((f32[4,2,32,128]{3,2,1,0:T(8,128)}, f32[4,2,32,128]{3,2,1,0:T(8,128)S(1)}, u32[]{:S(2)}, u32[]{:S(2)}) %collective-permute-start.7) | collective-permute-done | bytes 131104 | tf_op jit(solution)/shard_map/ppermute | solution.py:387
  54.5 2.5 %collective-permute-done.8 = f32[4,2,32,128]{3,2,1,0:T(8,128)S(1)} collective-permute-done((f32[4,2,32,128]{3,2,1,0:T(8,128)}, f32[4,2,32,128]{3,2,1,0:T(8,128)S(1)}, u32[]{:S(2)}, u32[]{:S(2)}) %collective-permute-start.8) | collective-permute-done | bytes 131104 | tf_op jit(solution)/shard_map/ppermute | solution.py:387
  57.0 0.0 collective-permute-done.9
  57.0 1.6 %add_add_fusion = f32[4,2,32,128]{3,2,1,0:T(8,128)} fusion(f32[4,2,32,128]{3,2,1,0:T(8,128)S(1)} %collective-permute-done.9, f32[4,2,32,128]{3,2,1,0:T(8,128)S(1)} %collective-permute-done.8, f32[4,2,32,128]{3,2,1,0:T(8,128)} %get-tuple-element.7, f32[4,2,32,128]{3,2,1,0:T(8,128)S(1)} %collective-permute-done.7), kind=kLoop, calls=%fused_computation | loop fusion | flops 98304 | bytes 655360 | tf_op jit(solution)/shard_map/add | solution.py:463
  (8 shorter events, 0.0 us)
Async XLA Ops:
  2.4 1.5 %collective-permute-start = (f32[1,8,128]{2,1,0:T(8,128)}, f32[1,8,128]{2,1,0:T(8,128)S(1)}, u32[]{:S(2)}, u32[]{:S(2)}) collective-permute-start(f32[1,8,128]{2,1,0:T(8,128)} %bitcast.8), channel_id=1, source_target_pairs={{0,4},{4,0},{8,12},{12,8},{16,20},{20,16},{24,28},{28,24},{1,5},{5... | collective-permute-start | bytes 12296 | tf_op jit(solution)/shard_map/ppermute | solution.py:391
  4.6 9.9 %collective-permute-start.3 = (f32[2,8,128]{2,1,0:T(8,128)S(1)}, f32[2,8,128]{2,1,0:T(8,128)S(1)}, u32[]{:S(2)}, u32[]{:S(2)}) collective-permute-start(f32[2,8,128]{2,1,0:T(8,128)S(1)} %pad_maximum_fusion), channel_id=1, source_target_pairs={{0,1},{1,0},{2,3},{3,2},{4,5},{5,4},{6,7},{7,6},{8,9},{9,8},{10,11... | collective-permute-start | bytes 24584 | tf_op jit(solution)/shard_map/ppermute | solution.py:391
  7.5 7.0 %collective-permute-start.2 = (f32[2,8,128]{2,1,0:T(8,128)S(1)}, f32[2,8,128]{2,1,0:T(8,128)S(1)}, u32[]{:S(2)}, u32[]{:S(2)}) collective-permute-start(f32[2,8,128]{2,1,0:T(8,128)S(1)} %pad_maximum_fusion), channel_id=1, source_target_pairs={{0,3},{1,2},{2,1},{3,0},{4,7},{5,6},{6,5},{7,4},{8,11},{9,10},{10,... | collective-permute-start | bytes 24584 | tf_op jit(solution)/shard_map/ppermute | solution.py:391
  10.0 4.5 %collective-permute-start.1 = (f32[2,8,128]{2,1,0:T(8,128)S(1)}, f32[2,8,128]{2,1,0:T(8,128)S(1)}, u32[]{:S(2)}, u32[]{:S(2)}) collective-permute-start(f32[2,8,128]{2,1,0:T(8,128)S(1)} %pad_maximum_fusion), channel_id=1, source_target_pairs={{0,2},{1,3},{2,0},{3,1},{4,6},{5,7},{6,4},{7,5},{8,10},{9,11},{10,... | collective-permute-start | bytes 24584 | tf_op jit(solution)/shard_map/ppermute | solution.py:391
  14.5 28.2 %copy-start = (f32[8,8,128]{2,1,0:T(8,128)}, f32[8,8,128]{2,1,0:T(8,128)S(1)}, u32[]{:S(2)}) copy-start(f32[8,8,128]{2,1,0:T(8,128)S(1)} %constant_dynamic-update-slice_fusion.refs_0_) | copy-start | bytes 98308
  14.5 28.2 %collective-permute-start.6 = (f32[8,8,128]{2,1,0:T(8,128)S(1)}, f32[8,8,128]{2,1,0:T(8,128)S(1)}, u32[]{:S(2)}, u32[]{:S(2)}) collective-permute-start(f32[8,8,128]{2,1,0:T(8,128)S(1)} %constant_dynamic-update-slice_fusion.refs_0_), channel_id=1, source_target_pairs={{0,8},{4,12},{8,0},{12,4},{16,24},{20,28},{24,16},{28,20},{1,9},{5... | collective-permute-start | bytes 98312 | tf_op jit(solution)/shard_map/ppermute | solution.py:391
  16.1 26.6 %collective-permute-start.5 = (f32[8,8,128]{2,1,0:T(8,128)S(1)}, f32[8,8,128]{2,1,0:T(8,128)S(1)}, u32[]{:S(2)}, u32[]{:S(2)}) collective-permute-start(f32[8,8,128]{2,1,0:T(8,128)S(1)} %constant_dynamic-update-slice_fusion.refs_0_), channel_id=1, source_target_pairs={{0,24},{4,28},{8,16},{12,20},{16,8},{20,12},{24,0},{28,4},{1,25},{... | collective-permute-start | bytes 98312 | tf_op jit(solution)/shard_map/ppermute | solution.py:391
  17.6 25.1 %collective-permute-start.4 = (f32[8,8,128]{2,1,0:T(8,128)S(1)}, f32[8,8,128]{2,1,0:T(8,128)S(1)}, u32[]{:S(2)}, u32[]{:S(2)}) collective-permute-start(f32[8,8,128]{2,1,0:T(8,128)S(1)} %constant_dynamic-update-slice_fusion.refs_0_), channel_id=1, source_target_pairs={{0,16},{4,20},{8,24},{12,28},{16,0},{20,4},{24,8},{28,12},{1,17},{... | collective-permute-start | bytes 98312 | tf_op jit(solution)/shard_map/ppermute | solution.py:391
  42.7 0.6 %copy-start.1 = (f32[8,8,128]{2,1,0:T(8,128)}, f32[8,8,128]{2,1,0:T(8,128)S(1)}, u32[]{:S(2)}) copy-start(f32[8,8,128]{2,1,0:T(8,128)S(1)} %collective-permute-done.6.refs_3_) | copy-start | bytes 98308
  42.7 0.6 %copy-start.2 = (f32[8,8,128]{2,1,0:T(8,128)}, f32[8,8,128]{2,1,0:T(8,128)S(1)}, u32[]{:S(2)}) copy-start(f32[8,8,128]{2,1,0:T(8,128)S(1)} %collective-permute-done.5.refs_2_) | copy-start | bytes 98308
  42.7 0.6 %copy-start.3 = (f32[8,8,128]{2,1,0:T(8,128)}, f32[8,8,128]{2,1,0:T(8,128)S(1)}, u32[]{:S(2)}) copy-start(f32[8,8,128]{2,1,0:T(8,128)S(1)} %collective-permute-done.4.refs_1_) | copy-start | bytes 98308
  47.3 7.2 %collective-permute-start.7 = (f32[4,2,32,128]{3,2,1,0:T(8,128)}, f32[4,2,32,128]{3,2,1,0:T(8,128)S(1)}, u32[]{:S(2)}, u32[]{:S(2)}) collective-permute-start(f32[4,2,32,128]{3,2,1,0:T(8,128)} %get-tuple-element.8), channel_id=1, source_target_pairs={{0,1},{1,2},{2,3},{3,0},{4,5},{5,6},{6,7},{7,4},{8,9},{9,10},{10,1... | collective-permute-start | bytes 393224 | tf_op jit(solution)/shard_map/ppermute | solution.py:387
  48.0 9.0 %collective-permute-start.8 = (f32[4,2,32,128]{3,2,1,0:T(8,128)}, f32[4,2,32,128]{3,2,1,0:T(8,128)S(1)}, u32[]{:S(2)}, u32[]{:S(2)}) collective-permute-start(f32[4,2,32,128]{3,2,1,0:T(8,128)} %get-tuple-element.9), channel_id=1, source_target_pairs={{0,2},{1,3},{2,0},{3,1},{4,6},{5,7},{6,4},{7,5},{8,10},{9,11},{10,... | collective-permute-start | bytes 393224 | tf_op jit(solution)/shard_map/ppermute | solution.py:387
  49.2 7.8 %collective-permute-start.9 = (f32[4,2,32,128]{3,2,1,0:T(8,128)}, f32[4,2,32,128]{3,2,1,0:T(8,128)S(1)}, u32[]{:S(2)}, u32[]{:S(2)}) collective-permute-start(f32[4,2,32,128]{3,2,1,0:T(8,128)} %get-tuple-element.10), channel_id=1, source_target_pairs={{0,3},{1,0},{2,1},{3,2},{4,7},{5,4},{6,5},{7,6},{8,11},{9,8},{10,9... | collective-permute-start | bytes 393224 | tf_op jit(solution)/shard_map/ppermute | solution.py:387

commit v5 on v4

--- a/solution.py
+++ b/solution.py
@@ -67,7 +67,13 @@
     block_ref[...] = block
 
 
-def grid_frames(starts, width, first, count, angles_ref, bounds_ref, kdata_ref, tables_ref, right_ref, left_ref, sens_ref, out_ref):
+def grid_frames(starts, width, first, count, angles_ref, bounds_ref, *refs):
+    *far_refs, out_ref = refs[:6]
+    near_refs, sems = refs[6:11], refs[11]
+    copies = [pltpu.make_async_copy(far, near, sems.at[n]) for n, (far, near) in enumerate(zip(far_refs, near_refs))]
+    for copy in copies:
+        copy.start()
+    kdata_ref, tables_ref, right_ref, left_ref, sens_ref = near_refs
     _, coils, spokes, _, readout = kdata_ref.shape
     _, table, _, side = tables_ref.shape
     segs = len(starts)
@@ -104,11 +110,8 @@
                 rows[a, l] = (tables_ref[0, a, starts[l] : starts[l] + width, :] * keep[l]).T
             return carry
 
-        lax.fori_loop(0, table, angle_tables, 0)
         ky[table] = jnp.zeros((readout, side), BF16)
         rows[table] = jnp.zeros((segs, side, width), BF16)
-        right[...] = right_ref[...]
-        left[...] = left_ref[...]
         halves[...] = jnp.zeros(halves.shape, BF16)
         out_ref[...] = jnp.zeros(out_ref.shape, F32)
 
@@ -133,7 +136,14 @@
                 flipped[i, g] = kd[g * group : (g + 1) * group].reshape(lanes, readout).T
             return carry
 
+        copies[0].wait()
         lax.fori_loop(0, count, gather, 0)
+        copies[1].wait()
+        lax.fori_loop(0, table, angle_tables, 0)
+        for copy in copies[2:]:
+            copy.wait()
+        right[...] = right_ref[...]
+        left[...] = left_ref[...]
 
         def place(step):
             return lax.div(step, pairs), lax.rem(step, pairs)
@@ -430,7 +440,7 @@
     )(kd, ref_center.T, projection)
 
     groups = lax.axis_size("frames")
-    rounds = [("frames", (1,))] + exchange_rounds("coils", 1, owners) + exchange_rounds("frames", 2, groups)
+    rounds = [("frames", (1,))] + exchange_rounds("frames", 2, groups) + exchange_rounds("coils", 1, owners)
     pieces, labels = [share[None]], [[(0, 0)]]
     for axis, distances in rounds:
         held = jnp.concatenate(pieces, axis=0) if len(pieces) > 1 else pieces[0]
@@ -443,8 +453,10 @@
     parts = pl.pallas_call(
         functools.partial(grid_frames, starts, width, 0, frames),
         out_shape=jax.ShapeDtypeStruct((frames, segs, 2, side, side), F32),
-        in_specs=[smem, smem, vmem, vmem, vmem, vmem, vmem],
+        in_specs=[smem, smem] + [pl.BlockSpec(memory_space=pl.ANY)] * 5,
         out_specs=vmem,
+        scratch_shapes=[pltpu.VMEM(a.shape, a.dtype) for a in (kd, kernels, right, left, sensitivity)]
+        + [pltpu.SemaphoreType.DMA((5,))],
         name="gridding",
     )(angles, seg_bounds, kd, kernels, right, left, sensitivity)
 

time: 59.1 us -> 58.7 us (level)
  waiting for transfers between devices: 9.19 us -> 7.39 us
  starting transfers between devices: 13.4 us -> 14.8 us
    ppermute x3, starting transfers between devices: 3.83 us -> 5.74 us  [around(): lax.ppermute(block, axis, [(i, (i + distance) % count) for i in range(cou...]
    ppermute x3, waiting for transfers between devices: 4.4 us -> 3.41 us  [around(): lax.ppermute(block, axis, [(i, (i + distance) % count) for i in range(cou...]
    ppermute x7, waiting for transfers between devices: 4.79 us -> 3.98 us  [exchanged(): lax.ppermute(block, axis, [(i, i ^ distance) for i in range(lax.axis_size...]
  transfers between devices with their start and end apart: 10 -> 10, of which waited for: 4 -> 3; matrix products, arithmetic and copies ran while one was open for 4% -> 4% of each run, Pallas kernels for 42% -> 43%
where the time goes in v5:
time: 58.7 us
  Pallas kernels  30.7 us (52%)
  starting transfers between devices  14.8 us (25%)
  waiting for transfers between devices  7.39 us (13%)
  local copies, waits for them, and re-layouts  2.78 us (5%)
  other arithmetic  2.28 us (4%)
  between operations  0.73 us (1%)
    pallas_call x1, Pallas kernels, local(): pl.pallas_call(functools.partial(grid_frames, starts, width, 0, frames),...  25 us
    ppermute x7, starting transfers between devices, exchanged(): lax.ppermute(block, axis, [(i, i ^ distance) for i in range(lax.axis_size...  9.07 us
    ppermute x3, starting transfers between devices, around(): lax.ppermute(block, axis, [(i, (i + distance) % count) for i in range(cou...  5.74 us
    ppermute x7, waiting for transfers between devices, exchanged(): lax.ppermute(block, axis, [(i, i ^ distance) for i in range(lax.axis_size...  3.98 us
    pallas_call x1, Pallas kernels, local(): pl.pallas_call(functools.partial(modulate, readout, groups, labels), out_...  3.96 us
    ppermute x3, waiting for transfers between devices, around(): lax.ppermute(block, axis, [(i, (i + distance) % count) for i in range(cou...  3.41 us
    pallas_call x1, Pallas kernels, local(): pl.pallas_call(centres, grid=(1,), out_shape=jax.ShapeDtypeStruct((padded...  1.73 us
    add x1, other arithmetic, local(): image = image + around(blocks[d], 'coils', d)  1.59 us
  transfers between devices with their start and end apart: 10, of which 3 were waited for; matrix products, arithmetic and copies ran while one was open for 4% of the time, Pallas kernels for 43%

profile of v5, /device:TPU:0, one launch (start us, length us, event | category | flops | bytes accessed | tf_op | source)
XLA Modules:
  0.0 58.7 jit_solution(247722296672297408)
XLA Ops:
  0.6 1.7 %centres.1 = f32[8,128]{1,0:T(8,128)} custom-call(bf16[4,8,13,2,256]{4,3,2,1,0:T(2,128)(2,1)} %bitcast.6, f32[2,8]{1,0:T(2,128)} %bitcast.10, f32[3,8]{1,0:T(4,128)} %projection_ref.1), custom_call_target="tpu_custom_call" | custom-call | tf_op jit(solution)/shard_map/centres/pallas_call | solution.py:428
  2.4 0.5 collective-permute-start
  2.9 0.7 %constant_dynamic-update-slice_fusion.4 = f32[8,8,128]{2,1,0:T(8,128)S(1)} fusion(f32[8,128]{1,0:T(8,128)} %centres.1), kind=kLoop, calls=%fused_computation.5 | loop fusion | bytes 8192
  3.5 0.3 collective-permute-done
  3.9 0.7 %pad_maximum_fusion = f32[2,8,128]{2,1,0:T(8,128)S(1)} fusion(f32[1,8,128]{2,1,0:T(8,128)S(1)} %collective-permute-done, f32[1,8,128]{2,1,0:T(8,128)} %bitcast.9), kind=kLoop, calls=%fused_computation.6 | loop fusion | flops 2048 | bytes 16384 | tf_op jit(solution)/shard_map/concatenate | solution.py:446
  4.6 2.8 %collective-permute-start.3 = (f32[2,8,128]{2,1,0:T(8,128)S(1)}, f32[2,8,128]{2,1,0:T(8,128)S(1)}, u32[]{:S(2)}, u32[]{:S(2)}) collective-permute-start(f32[2,8,128]{2,1,0:T(8,128)S(1)} %pad_maximum_fusion), channel_id=1, source_target_pairs={{0,8},{4,12},{8,0},{12,4},{16,24},{20,28},{24,16},{28,20},{1,9},{5... | collective-permute-start | bytes 24584 | tf_op jit(solution)/shard_map/ppermute | solution.py:401
  7.4 1.5 %collective-permute-start.2 = (f32[2,8,128]{2,1,0:T(8,128)S(1)}, f32[2,8,128]{2,1,0:T(8,128)S(1)}, u32[]{:S(2)}, u32[]{:S(2)}) collective-permute-start(f32[2,8,128]{2,1,0:T(8,128)S(1)} %pad_maximum_fusion), channel_id=1, source_target_pairs={{0,24},{4,28},{8,16},{12,20},{16,8},{20,12},{24,0},{28,4},{1,25},{... | collective-permute-start | bytes 24584 | tf_op jit(solution)/shard_map/ppermute | solution.py:401
  8.9 0.0 collective-permute-start.1
  8.9 3.6 %collective-permute-done.1 = f32[2,8,128]{2,1,0:T(8,128)S(1)} collective-permute-done((f32[2,8,128]{2,1,0:T(8,128)S(1)}, f32[2,8,128]{2,1,0:T(8,128)S(1)}, u32[]{:S(2)}, u32[]{:S(2)}) %collective-permute-start.1) | collective-permute-done | bytes 8224 | tf_op jit(solution)/shard_map/ppermute | solution.py:401
  12.5 0.0 collective-permute-done.2
  12.5 0.0 collective-permute-done.3
  12.6 1.6 %collective-permute-start.6 = (f32[8,8,128]{2,1,0:T(8,128)S(1)}, f32[8,8,128]{2,1,0:T(8,128)S(1)}, u32[]{:S(2)}, u32[]{:S(2)}) collective-permute-start(f32[8,8,128]{2,1,0:T(8,128)S(1)} %constant_dynamic-update-slice_fusion.refs_0_), channel_id=1, source_target_pairs={{0,1},{1,0},{2,3},{3,2},{4,5},{5,4},{6,7},{7,6},{8,9},{9,8},{10,11... | collective-permute-start | bytes 98312 | tf_op jit(solution)/shard_map/ppermute | solution.py:401
  14.2 2.5 %collective-permute-start.5 = (f32[8,8,128]{2,1,0:T(8,128)S(1)}, f32[8,8,128]{2,1,0:T(8,128)S(1)}, u32[]{:S(2)}, u32[]{:S(2)}) collective-permute-start(f32[8,8,128]{2,1,0:T(8,128)S(1)} %constant_dynamic-update-slice_fusion.refs_0_), channel_id=1, source_target_pairs={{0,3},{1,2},{2,1},{3,0},{4,7},{5,6},{6,5},{7,4},{8,11},{9,10},{10,... | collective-permute-start | bytes 98312 | tf_op jit(solution)/shard_map/ppermute | solution.py:401
  16.7 0.1 collective-permute-start.4
  16.8 25.0 %gridding.1.parts_ref = f32[4,3,2,128,128]{4,3,2,1,0:T(8,128)} custom-call(s32[4,13]{1,0:T(4,128)} %angles_ref.1, s32[2]{0:T(128)} %bounds_ref.3, bf16[4,8,13,2,256]{4,3,2,1,0:T(2,128)(2,1)} %bitcast.7, bf16[2,16,256,128]{3,2,1,0:T(8,128)(2,1)} %refs_1_.1, bf16[2,256,128]{2,1,0:T(8,128)(2,1)} %constant.21.refs_2_, bf16[2,256,128]{2,1,0:T(8,128)(2,1)} %constant.26.refs_3_, ...), custom_call_target="tpu_custom_call" | custom-call | tf_op jit(solution)/shard_map/gridding/pallas_call | solution.py:453
  41.9 0.0 copy-done
  41.9 0.0 collective-permute-done.6.refs_3_
  41.9 0.0 collective-permute-done.5.refs_2_
  41.9 0.0 collective-permute-done.4.refs_1_
  41.9 0.6 copy-done.1
  42.5 0.0 copy-done.2
  42.5 0.0 copy-done.3
  42.5 4.0 %modulate.1 = (f32[16,128]{1,0:T(8,128)}, f32[4,2,32,128]{3,2,1,0:T(8,128)}, f32[4,2,32,128]{3,2,1,0:T(8,128)}, f32[4,2,32,128]{3,2,1,0:T(8,128)}, f32[4,2,32,128]{3,2,1,0:T(8,128)}) custom-call(s32[1]{0:T(128)} %bitcast.place_ref, s32[1]{0:T(128)} %bitcast.1.owner_ref, s32[2]{0:T(128)} %bounds_ref.3, f32[3]{0:T(128)} %init_ref.1, ...), custom_call_target="tpu_custom_call" | custom-call | tf_op jit(solution)/shard_map/modulate/pallas_call | solution.py:465
  46.5 1.8 %collective-permute-start.7 = (f32[4,2,32,128]{3,2,1,0:T(8,128)}, f32[4,2,32,128]{3,2,1,0:T(8,128)S(1)}, u32[]{:S(2)}, u32[]{:S(2)}) collective-permute-start(f32[4,2,32,128]{3,2,1,0:T(8,128)} %get-tuple-element.8), channel_id=1, source_target_pairs={{0,1},{1,2},{2,3},{3,0},{4,5},{5,6},{6,7},{7,4},{8,9},{9,10},{10,1... | collective-permute-start | bytes 393224 | tf_op jit(solution)/shard_map/ppermute | solution.py:397
  48.3 1.7 %collective-permute-start.8 = (f32[4,2,32,128]{3,2,1,0:T(8,128)}, f32[4,2,32,128]{3,2,1,0:T(8,128)S(1)}, u32[]{:S(2)}, u32[]{:S(2)}) collective-permute-start(f32[4,2,32,128]{3,2,1,0:T(8,128)} %get-tuple-element.9), channel_id=1, source_target_pairs={{0,2},{1,3},{2,0},{3,1},{4,6},{5,7},{6,4},{7,5},{8,10},{9,11},{10,... | collective-permute-start | bytes 393224 | tf_op jit(solution)/shard_map/ppermute | solution.py:397
  50.0 2.2 %collective-permute-start.9 = (f32[4,2,32,128]{3,2,1,0:T(8,128)}, f32[4,2,32,128]{3,2,1,0:T(8,128)S(1)}, u32[]{:S(2)}, u32[]{:S(2)}) collective-permute-start(f32[4,2,32,128]{3,2,1,0:T(8,128)} %get-tuple-element.10), channel_id=1, source_target_pairs={{0,3},{1,0},{2,1},{3,2},{4,7},{5,4},{6,5},{7,6},{8,11},{9,8},{10,9... | collective-permute-start | bytes 393224 | tf_op jit(solution)/shard_map/ppermute | solution.py:397
  52.2 0.8 %slice_reduce_fusion = f32[12]{0:T(128)S(1)} fusion(f32[16,128]{1,0:T(8,128)} %get-tuple-element.11), kind=kLoop, calls=%fused_computation.7 | loop fusion | bytes 96 | tf_op jit(solution)/shard_map/slice | solution.py:476
  53.0 0.7 %reshape_squeeze.3 = f32[4,3]{1,0:T(4,128)} reshape(f32[12]{0:T(128)S(1)} %slice_reduce_fusion) | data formatting | bytes 96 | tf_op jit(solution)/shard_map/reshape;squeeze | solution.py:476
  53.7 0.0 collective-permute-done.7
  53.7 3.4 %collective-permute-done.8 = f32[4,2,32,128]{3,2,1,0:T(8,128)S(1)} collective-permute-done((f32[4,2,32,128]{3,2,1,0:T(8,128)}, f32[4,2,32,128]{3,2,1,0:T(8,128)S(1)}, u32[]{:S(2)}, u32[]{:S(2)}) %collective-permute-start.8) | collective-permute-done | bytes 131104 | tf_op jit(solution)/shard_map/ppermute | solution.py:397
  57.1 0.0 collective-permute-done.9
  57.1 1.6 %add_add_fusion = f32[4,2,32,128]{3,2,1,0:T(8,128)} fusion(f32[4,2,32,128]{3,2,1,0:T(8,128)S(1)} %collective-permute-done.9, f32[4,2,32,128]{3,2,1,0:T(8,128)S(1)} %collective-permute-done.8, f32[4,2,32,128]{3,2,1,0:T(8,128)} %get-tuple-element.7, f32[4,2,32,128]{3,2,1,0:T(8,128)S(1)} %collective-permute-done.7), kind=kLoop, calls=%fused_computation | loop fusion | flops 98304 | bytes 655360 | tf_op jit(solution)/shard_map/add | solution.py:475
  (8 shorter events, 0.0 us)
Async XLA Ops:
  2.4 1.5 %collective-permute-start = (f32[1,8,128]{2,1,0:T(8,128)}, f32[1,8,128]{2,1,0:T(8,128)S(1)}, u32[]{:S(2)}, u32[]{:S(2)}) collective-permute-start(f32[1,8,128]{2,1,0:T(8,128)} %bitcast.8), channel_id=1, source_target_pairs={{0,4},{4,0},{8,12},{12,8},{16,20},{20,16},{24,28},{28,24},{1,5},{5... | collective-permute-start | bytes 12296 | tf_op jit(solution)/shard_map/ppermute | solution.py:401
  4.6 8.0 %collective-permute-start.3 = (f32[2,8,128]{2,1,0:T(8,128)S(1)}, f32[2,8,128]{2,1,0:T(8,128)S(1)}, u32[]{:S(2)}, u32[]{:S(2)}) collective-permute-start(f32[2,8,128]{2,1,0:T(8,128)S(1)} %pad_maximum_fusion), channel_id=1, source_target_pairs={{0,8},{4,12},{8,0},{12,4},{16,24},{20,28},{24,16},{28,20},{1,9},{5... | collective-permute-start | bytes 24584 | tf_op jit(solution)/shard_map/ppermute | solution.py:401
  7.4 5.1 %collective-permute-start.2 = (f32[2,8,128]{2,1,0:T(8,128)S(1)}, f32[2,8,128]{2,1,0:T(8,128)S(1)}, u32[]{:S(2)}, u32[]{:S(2)}) collective-permute-start(f32[2,8,128]{2,1,0:T(8,128)S(1)} %pad_maximum_fusion), channel_id=1, source_target_pairs={{0,24},{4,28},{8,16},{12,20},{16,8},{20,12},{24,0},{28,4},{1,25},{... | collective-permute-start | bytes 24584 | tf_op jit(solution)/shard_map/ppermute | solution.py:401
  8.9 3.7 %collective-permute-start.1 = (f32[2,8,128]{2,1,0:T(8,128)S(1)}, f32[2,8,128]{2,1,0:T(8,128)S(1)}, u32[]{:S(2)}, u32[]{:S(2)}) collective-permute-start(f32[2,8,128]{2,1,0:T(8,128)S(1)} %pad_maximum_fusion), channel_id=1, source_target_pairs={{0,16},{4,20},{8,24},{12,28},{16,0},{20,4},{24,8},{28,12},{1,17},{... | collective-permute-start | bytes 24584 | tf_op jit(solution)/shard_map/ppermute | solution.py:401
  12.6 29.3 %copy-start = (f32[8,8,128]{2,1,0:T(8,128)}, f32[8,8,128]{2,1,0:T(8,128)S(1)}, u32[]{:S(2)}) copy-start(f32[8,8,128]{2,1,0:T(8,128)S(1)} %constant_dynamic-update-slice_fusion.refs_0_) | copy-start | bytes 98308
  12.6 29.3 %collective-permute-start.6 = (f32[8,8,128]{2,1,0:T(8,128)S(1)}, f32[8,8,128]{2,1,0:T(8,128)S(1)}, u32[]{:S(2)}, u32[]{:S(2)}) collective-permute-start(f32[8,8,128]{2,1,0:T(8,128)S(1)} %constant_dynamic-update-slice_fusion.refs_0_), channel_id=1, source_target_pairs={{0,1},{1,0},{2,3},{3,2},{4,5},{5,4},{6,7},{7,6},{8,9},{9,8},{10,11... | collective-permute-start | bytes 98312 | tf_op jit(solution)/shard_map/ppermute | solution.py:401
  14.2 27.7 %collective-permute-start.5 = (f32[8,8,128]{2,1,0:T(8,128)S(1)}, f32[8,8,128]{2,1,0:T(8,128)S(1)}, u32[]{:S(2)}, u32[]{:S(2)}) collective-permute-start(f32[8,8,128]{2,1,0:T(8,128)S(1)} %constant_dynamic-update-slice_fusion.refs_0_), channel_id=1, source_target_pairs={{0,3},{1,2},{2,1},{3,0},{4,7},{5,6},{6,5},{7,4},{8,11},{9,10},{10,... | collective-permute-start | bytes 98312 | tf_op jit(solution)/shard_map/ppermute | solution.py:401
  16.7 25.2 %collective-permute-start.4 = (f32[8,8,128]{2,1,0:T(8,128)S(1)}, f32[8,8,128]{2,1,0:T(8,128)S(1)}, u32[]{:S(2)}, u32[]{:S(2)}) collective-permute-start(f32[8,8,128]{2,1,0:T(8,128)S(1)} %constant_dynamic-update-slice_fusion.refs_0_), channel_id=1, source_target_pairs={{0,2},{1,3},{2,0},{3,1},{4,6},{5,7},{6,4},{7,5},{8,10},{9,11},{10,... | collective-permute-start | bytes 98312 | tf_op jit(solution)/shard_map/ppermute | solution.py:401
  41.9 0.6 %copy-start.1 = (f32[8,8,128]{2,1,0:T(8,128)}, f32[8,8,128]{2,1,0:T(8,128)S(1)}, u32[]{:S(2)}) copy-start(f32[8,8,128]{2,1,0:T(8,128)S(1)} %collective-permute-done.6.refs_3_) | copy-start | bytes 98308
  41.9 0.6 %copy-start.2 = (f32[8,8,128]{2,1,0:T(8,128)}, f32[8,8,128]{2,1,0:T(8,128)S(1)}, u32[]{:S(2)}) copy-start(f32[8,8,128]{2,1,0:T(8,128)S(1)} %collective-permute-done.5.refs_2_) | copy-start | bytes 98308
  41.9 0.6 %copy-start.3 = (f32[8,8,128]{2,1,0:T(8,128)}, f32[8,8,128]{2,1,0:T(8,128)S(1)}, u32[]{:S(2)}) copy-start(f32[8,8,128]{2,1,0:T(8,128)S(1)} %collective-permute-done.4.refs_1_) | copy-start | bytes 98308
  46.5 7.2 %collective-permute-start.7 = (f32[4,2,32,128]{3,2,1,0:T(8,128)}, f32[4,2,32,128]{3,2,1,0:T(8,128)S(1)}, u32[]{:S(2)}, u32[]{:S(2)}) collective-permute-start(f32[4,2,32,128]{3,2,1,0:T(8,128)} %get-tuple-element.8), channel_id=1, source_target_pairs={{0,1},{1,2},{2,3},{3,0},{4,5},{5,6},{6,7},{7,4},{8,9},{9,10},{10,1... | collective-permute-start | bytes 393224 | tf_op jit(solution)/shard_map/ppermute | solution.py:397
  48.3 8.8 %collective-permute-start.8 = (f32[4,2,32,128]{3,2,1,0:T(8,128)}, f32[4,2,32,128]{3,2,1,0:T(8,128)S(1)}, u32[]{:S(2)}, u32[]{:S(2)}) collective-permute-start(f32[4,2,32,128]{3,2,1,0:T(8,128)} %get-tuple-element.9), channel_id=1, source_target_pairs={{0,2},{1,3},{2,0},{3,1},{4,6},{5,7},{6,4},{7,5},{8,10},{9,11},{10,... | collective-permute-start | bytes 393224 | tf_op jit(solution)/shard_map/ppermute | solution.py:397
  50.0 7.1 %collective-permute-start.9 = (f32[4,2,32,128]{3,2,1,0:T(8,128)}, f32[4,2,32,128]{3,2,1,0:T(8,128)S(1)}, u32[]{:S(2)}, u32[]{:S(2)}) collective-permute-start(f32[4,2,32,128]{3,2,1,0:T(8,128)} %get-tuple-element.10), channel_id=1, source_target_pairs={{0,3},{1,0},{2,1},{3,2},{4,7},{5,4},{6,5},{7,6},{8,11},{9,8},{10,9... | collective-permute-start | bytes 393224 | tf_op jit(solution)/shard_map/ppermute | solution.py:397

commit v6 on v5

--- a/solution.py
+++ b/solution.py
@@ -68,11 +68,25 @@
 
 
 def grid_frames(starts, width, first, count, angles_ref, bounds_ref, *refs):
-    *far_refs, out_ref = refs[:6]
-    near_refs, sems = refs[6:11], refs[11]
-    copies = [pltpu.make_async_copy(far, near, sems.at[n]) for n, (far, near) in enumerate(zip(far_refs, near_refs))]
-    for copy in copies:
-        copy.start()
+    far_refs, image_ref = refs[:5], refs[5]
+    near_refs, out_ref, sems, out_sems = refs[6:11], refs[11], refs[12], refs[13]
+    copies = []
+    for far, near in zip(far_refs, near_refs):
+        parts = [(far.at[n], near.at[n]) for n in range(far.shape[0])] if len(far.shape) > 3 else [(far, near)]
+        if len(far.shape) == 4 and far.shape[0] == 2:
+            cut = far.shape[1] // 4
+            parts = [(far.at[n, pl.ds(q * cut, cut)], near.at[n, pl.ds(q * cut, cut)]) for n in range(2) for q in range(4)]
+        elif len(far.shape) == 4:
+            parts = [(far, near)]
+        copies.append([pltpu.make_async_copy(a, b, sems.at[len(copies), n]) for n, (a, b) in enumerate(parts)])
+    for group in copies:
+        for copy in group:
+            copy.start()
+
+    def arrive(n):
+        for copy in copies[n]:
+            copy.wait()
+
     kdata_ref, tables_ref, right_ref, left_ref, sens_ref = near_refs
     _, coils, spokes, _, readout = kdata_ref.shape
     _, table, _, side = tables_ref.shape
@@ -85,10 +99,10 @@
     room = max(8, 2 * coils)
     group = lanes // room
     groups = (2 * most + group - 1) // group
-    cut = 32
+    cut = 16
     cuts = side // cut
 
-    def body(kd, flipped, columns, rows, weighted, halves, ky, right, left, slot_of, angle_of, tiles_of, *accs):
+    def body(sens, kd, flipped, columns, rows, weighted, halves, ky, right, left, slot_of, angle_of, tiles_of, *accs):
         banks = [[accs[(m * 8 + b) * cuts : (m * 8 + b + 1) * cuts] for b in range(8)] for m in range(2)]
         grid_acc = [banks[m][:3] for m in range(2)]
         half_acc = [banks[m][3:5] for m in range(2)]
@@ -136,14 +150,15 @@
                 flipped[i, g] = kd[g * group : (g + 1) * group].reshape(lanes, readout).T
             return carry
 
-        copies[0].wait()
+        arrive(0)
         lax.fori_loop(0, count, gather, 0)
-        copies[1].wait()
+        arrive(1)
         lax.fori_loop(0, table, angle_tables, 0)
-        for copy in copies[2:]:
-            copy.wait()
+        for n in range(2, 5):
+            arrive(n)
         right[...] = right_ref[...]
         left[...] = left_ref[...]
+        sens[...] = sens_ref[...].astype(F32)
 
         def place(step):
             return lax.div(step, pairs), lax.rem(step, pairs)
@@ -212,8 +227,8 @@
         def combine(step, r):
             i, n = place(step)
             here = pl.ds(r * cut, cut)
-            real = [sens_ref[2 * n + m, 0, here].astype(F32) for m in range(2)]
-            imag = [sens_ref[2 * n + m, 1, here].astype(F32) for m in range(2)]
+            real = [sens[2 * n + m, 0, here] for m in range(2)]
+            imag = [sens[2 * n + m, 1, here] for m in range(2)]
 
             def add(l, parts):
                 total_re, total_im = out_ref[i, l, 0, here], out_ref[i, l, 1, here]
@@ -234,6 +249,8 @@
             earlier = jnp.maximum(step - 1, 0)
             following = jnp.minimum(step + 1, steps - 1)
             left_over = list(range(cuts))
+            spots = segs * tiles - 6
+
             for k in range(tiles):
                 buf = k % 2 if k else 2
                 last = k == tiles - 1
@@ -245,8 +262,12 @@
                     grid_tile(step, buf, l, k)
                     if k == 0 and l < 2:
                         over_columns(l + 1)
-                    if k >= 2 and (l or k > 2) and left_over:
-                        combine(earlier, left_over.pop(0))
+                    if k == 1 and l == 2:
+                        over_rows()
+                    at = k * segs + l - 6
+                    if at >= 0:
+                        for r in range(cuts * at // spots, cuts * (at + 1) // spots):
+                            combine(earlier, r)
                     if k == tiles - 2 and l == 1:
                         own_columns(following)
                     if last and l == 1:
@@ -254,11 +275,10 @@
                 if k == 0:
                     keep_half(1)
                     keep_half(2)
-                if k == 1:
-                    over_rows()
             keep_half(0)
-            for r in left_over:
-                combine(earlier, r)
+
+        def leave(i):
+            return pltpu.make_async_copy(out_ref.at[i], image_ref.at[i], out_sems.at[i])
 
         own_columns(0)
         weigh(0, 0, 2)
@@ -268,6 +288,11 @@
             tiles = tiles_of[i]
             for option in range(least, most + 1):
                 pl.when(tiles == option)(functools.partial(phase, option, step))
+
+            @pl.when((lax.rem(step, pairs) == 0) & (step > 0))
+            def _():
+                leave(i - 1).start()
+
             return carry
 
         lax.fori_loop(0, steps, one, 0)
@@ -278,9 +303,13 @@
         over_rows()
         for r in range(cuts):
             combine(steps - 1, r)
+        leave(count - 1).start()
+        for i in range(count):
+            leave(i).wait()
 
     pl.run_scoped(
         body,
+        pltpu.VMEM((coils, 2, side, side), F32),
         pltpu.VMEM((groups * group, room, readout), F32),
         pltpu.VMEM((count, groups, readout, lanes), F32),
         pltpu.VMEM((groups, readout, lanes), BF16),
@@ -330,9 +359,12 @@
     return lax.fori_loop(0, groups, one, (zero, zero), unroll=groups <= 8)
 
 
-def modulate(readout, groups, labels, place_ref, owner_ref, bounds_ref, init_ref, parts_ref, *refs):
+def modulate(readout, groups, labels, place_ref, owner_ref, bounds_ref, init_ref, far_ref, *refs):
     piece_refs, refs = refs[: len(labels)], refs[len(labels) :]
-    coef_ref, *out_refs, image_ref, table_ref = refs
+    coef_ref, *out_refs, image_ref, table_ref, parts_ref, sems = refs
+    copies = [pltpu.make_async_copy(far_ref.at[t], parts_ref.at[t], sems.at[t]) for t in range(far_ref.shape[0])]
+    for copy in copies:
+        copy.start()
     frames, segs, _, side, _ = parts_ref.shape
     basis = init_ref.shape[0]
     owners = len(out_refs)
@@ -374,6 +406,7 @@
     )
     cos_across, sin_across = jnp.cos(across), jnp.sin(across)
     for t in range(frames):
+        copies[t].wait()
         image_re = jnp.zeros((side, side), F32)
         image_im = jnp.zeros((side, side), F32)
         for l in range(segs):
@@ -454,9 +487,9 @@
         functools.partial(grid_frames, starts, width, 0, frames),
         out_shape=jax.ShapeDtypeStruct((frames, segs, 2, side, side), F32),
         in_specs=[smem, smem] + [pl.BlockSpec(memory_space=pl.ANY)] * 5,
-        out_specs=vmem,
+        out_specs=pl.BlockSpec(memory_space=pl.ANY),
         scratch_shapes=[pltpu.VMEM(a.shape, a.dtype) for a in (kd, kernels, right, left, sensitivity)]
-        + [pltpu.SemaphoreType.DMA((5,))],
+        + [pltpu.VMEM((frames, segs, 2, side, side), F32), pltpu.SemaphoreType.DMA((5, 8)), pltpu.SemaphoreType.DMA((frames,))],
         name="gridding",
     )(angles, seg_bounds, kd, kernels, right, left, sensitivity)
 
@@ -465,9 +498,15 @@
     coef, *blocks = pl.pallas_call(
         functools.partial(modulate, readout, groups, labels),
         out_shape=(jax.ShapeDtypeStruct((height, lanes), F32),) + (block,) * owners,
-        in_specs=[smem, smem, smem, smem, vmem] + [vmem] * len(pieces),
+        in_specs=[smem, smem, smem, smem, pl.BlockSpec(memory_space=pl.ANY)] + [vmem] * len(pieces),
         out_specs=(vmem,) * (1 + owners),
-        scratch_shapes=[pltpu.VMEM((2, side, side), F32), pltpu.VMEM((groups, owners, padded, lanes), F32)],
+        scratch_shapes=[
+            pltpu.VMEM((2, side, side), F32),
+            pltpu.VMEM((groups, owners, padded, lanes), F32),
+            pltpu.VMEM(parts.shape, F32),
+            pltpu.SemaphoreType.DMA((frames,)),
+        ],
+        compiler_params=pltpu.CompilerParams(vmem_limit_bytes=52 * 2**20),
         name="modulate",
     )(place.reshape(1), owner.reshape(1), seg_bounds, init_coef, parts, *pieces)
     image = blocks[0]

time: 58.7 us -> 56.3 us (0.959)
  Pallas kernels: 30.7 us -> 28.8 us
  waiting for transfers between devices: 7.39 us -> 8.89 us
  local copies, waits for them, and re-layouts: 2.78 us -> 1.48 us
  other arithmetic: 2.28 us -> 1.39 us
    ppermute x3, waiting for transfers between devices: 3.41 us -> 4.91 us  [around(): lax.ppermute(block, axis, [(i, (i + distance) % count) for i in range(cou...]
    pallas_call x1, Pallas kernels: 25 us -> 23.9 us  [local(): pl.pallas_call(functools.partial(grid_frames, starts, width, 0, frames),...]
    add x1, other arithmetic: 1.59 us -> 0.7 us  [local(): image = image + around(blocks[d], 'coils', d)]
    pallas_call x1, Pallas kernels: 3.96 us -> 3.2 us  [local(): pl.pallas_call(functools.partial(modulate, readout, groups, labels), out_...]
    slice x1, local copies, waits for them, and re-layouts: 0.81 us -> 0.11 us  [local(): field_coef = coef[:frames * basis, 0].reshape(frames, basis)]
    unnamed x12 -> x8, local copies, waits for them, and re-layouts: 1.31 us -> 0.7 us
  transfers between devices with their start and end apart: 10 -> 10, of which waited for: 3 -> 4; matrix products, arithmetic and copies ran while one was open for 4% -> 3% of each run, Pallas kernels for 43% -> 43%
where the time goes in v6:
time: 56.3 us; the launch traced here: 56.1 us
  Pallas kernels  28.8 us (51%)
  starting transfers between devices  14.9 us (26%)
  waiting for transfers between devices  8.89 us (16%)
  local copies, waits for them, and re-layouts  1.48 us (3%)
  other arithmetic  1.39 us (2%)
  between operations  0.71 us (1%)
    pallas_call x1, Pallas kernels, local(): pl.pallas_call(functools.partial(grid_frames, starts, width, 0, frames),...  23.9 us
    ppermute x7, starting transfers between devices, exchanged(): lax.ppermute(block, axis, [(i, i ^ distance) for i in range(lax.axis_size...  9.07 us
    ppermute x3, starting transfers between devices, around(): lax.ppermute(block, axis, [(i, (i + distance) % count) for i in range(cou...  5.78 us
    ppermute x3, waiting for transfers between devices, around(): lax.ppermute(block, axis, [(i, (i + distance) % count) for i in range(cou...  4.91 us
    ppermute x7, waiting for transfers between devices, exchanged(): lax.ppermute(block, axis, [(i, i ^ distance) for i in range(lax.axis_size...  3.98 us
    pallas_call x1, Pallas kernels, local(): pl.pallas_call(functools.partial(modulate, readout, groups, labels), out_...  3.2 us
    pallas_call x1, Pallas kernels, local(): pl.pallas_call(centres, grid=(1,), out_shape=jax.ShapeDtypeStruct((padded...  1.73 us
  transfers between devices with their start and end apart: 10, of which 4 were waited for; matrix products, arithmetic and copies ran while one was open for 3% of the time, Pallas kernels for 43%

profile of v6, /device:TPU:0, one launch (start us, length us, event | category | flops | bytes accessed | tf_op | source)
XLA Modules:
  0.0 56.1 jit_solution(7220568832334973142)
XLA Ops:
  0.6 1.7 %centres.1 = f32[8,128]{1,0:T(8,128)} custom-call(bf16[4,8,13,2,256]{4,3,2,1,0:T(2,128)(2,1)} %bitcast.6, f32[2,8]{1,0:T(2,128)} %bitcast.10, f32[3,8]{1,0:T(4,128)} %projection_ref.1), custom_call_target="tpu_custom_call" | custom-call | tf_op jit(solution)/shard_map/centres/pallas_call | solution.py:461
  2.4 0.5 collective-permute-start
  2.9 0.7 %constant_dynamic-update-slice_fusion.4 = f32[8,8,128]{2,1,0:T(8,128)S(1)} fusion(f32[8,128]{1,0:T(8,128)} %centres.1), kind=kLoop, calls=%fused_computation.5 | loop fusion | bytes 8192
  3.5 0.3 collective-permute-done
  3.9 0.7 %pad_maximum_fusion = f32[2,8,128]{2,1,0:T(8,128)S(1)} fusion(f32[1,8,128]{2,1,0:T(8,128)S(1)} %collective-permute-done, f32[1,8,128]{2,1,0:T(8,128)} %bitcast.9), kind=kLoop, calls=%fused_computation.6 | loop fusion | flops 2048 | bytes 16384 | tf_op jit(solution)/shard_map/concatenate | solution.py:479
  4.6 2.8 %collective-permute-start.3 = (f32[2,8,128]{2,1,0:T(8,128)S(1)}, f32[2,8,128]{2,1,0:T(8,128)S(1)}, u32[]{:S(2)}, u32[]{:S(2)}) collective-permute-start(f32[2,8,128]{2,1,0:T(8,128)S(1)} %pad_maximum_fusion), channel_id=1, source_target_pairs={{0,8},{4,12},{8,0},{12,4},{16,24},{20,28},{24,16},{28,20},{1,9},{5... | collective-permute-start | bytes 24584 | tf_op jit(solution)/shard_map/ppermute | solution.py:434
  7.4 1.5 %collective-permute-start.2 = (f32[2,8,128]{2,1,0:T(8,128)S(1)}, f32[2,8,128]{2,1,0:T(8,128)S(1)}, u32[]{:S(2)}, u32[]{:S(2)}) collective-permute-start(f32[2,8,128]{2,1,0:T(8,128)S(1)} %pad_maximum_fusion), channel_id=1, source_target_pairs={{0,24},{4,28},{8,16},{12,20},{16,8},{20,12},{24,0},{28,4},{1,25},{... | collective-permute-start | bytes 24584 | tf_op jit(solution)/shard_map/ppermute | solution.py:434
  8.9 0.0 collective-permute-start.1
  8.9 3.6 %collective-permute-done.1 = f32[2,8,128]{2,1,0:T(8,128)S(1)} collective-permute-done((f32[2,8,128]{2,1,0:T(8,128)S(1)}, f32[2,8,128]{2,1,0:T(8,128)S(1)}, u32[]{:S(2)}, u32[]{:S(2)}) %collective-permute-start.1) | collective-permute-done | bytes 8224 | tf_op jit(solution)/shard_map/ppermute | solution.py:434
  12.5 0.0 collective-permute-done.2
  12.5 0.0 collective-permute-done.3
  12.6 1.6 %collective-permute-start.6 = (f32[8,8,128]{2,1,0:T(8,128)S(1)}, f32[8,8,128]{2,1,0:T(8,128)S(1)}, u32[]{:S(2)}, u32[]{:S(2)}) collective-permute-start(f32[8,8,128]{2,1,0:T(8,128)S(1)} %constant_dynamic-update-slice_fusion.refs_0_), channel_id=1, source_target_pairs={{0,1},{1,0},{2,3},{3,2},{4,5},{5,4},{6,7},{7,6},{8,9},{9,8},{10,11... | collective-permute-start | bytes 98312 | tf_op jit(solution)/shard_map/ppermute | solution.py:434
  14.2 2.5 %collective-permute-start.5 = (f32[8,8,128]{2,1,0:T(8,128)S(1)}, f32[8,8,128]{2,1,0:T(8,128)S(1)}, u32[]{:S(2)}, u32[]{:S(2)}) collective-permute-start(f32[8,8,128]{2,1,0:T(8,128)S(1)} %constant_dynamic-update-slice_fusion.refs_0_), channel_id=1, source_target_pairs={{0,3},{1,2},{2,1},{3,0},{4,7},{5,6},{6,5},{7,4},{8,11},{9,10},{10,... | collective-permute-start | bytes 98312 | tf_op jit(solution)/shard_map/ppermute | solution.py:434
  16.7 0.1 collective-permute-start.4
  16.8 0.0 copy-start
  16.8 0.0 copy-start.1
  16.8 23.9 %gridding.1.far_ref = f32[4,3,2,128,128]{4,3,2,1,0:T(8,128)} custom-call(s32[4,13]{1,0:T(4,128)} %angles_ref.1, s32[2]{0:T(128)} %bounds_ref.3, bf16[4,8,13,2,256]{4,3,2,1,0:T(2,128)(2,1)} %bitcast.7, bf16[2,16,256,128]{3,2,1,0:T(8,128)(2,1)} %refs_1_.1, bf16[2,256,128]{2,1,0:T(8,128)(2,1)} %constant.21.refs_2_, bf16[2,256,128]{2,1,0:T(8,128)(2,1)} %constant.26.refs_3_, ...), custom_call_target="tpu_custom_call" | custom-call | tf_op jit(solution)/shard_map/gridding/pallas_call | solution.py:486
  40.7 0.0 collective-permute-done.6.refs_3_
  40.7 0.0 collective-permute-done.5.refs_2_
  40.7 0.0 collective-permute-done.4.refs_1_
  40.7 0.0 copy-done
  40.7 0.0 copy-done.1
  40.7 3.2 %modulate.1 = (f32[16,128]{1,0:T(8,128)S(1)}, f32[4,2,32,128]{3,2,1,0:T(8,128)S(1)}, f32[4,2,32,128]{3,2,1,0:T(8,128)S(1)}, f32[4,2,32,128]{3,2,1,0:T(8,128)S(1)}, f32[4,2,32,128]{3,2,1,0:T(8,128)S(1)}) custom-call(s32[1]{0:T(128)} %bitcast.place_ref, s32[1]{0:T(128)} %bitcast.1.owner_ref, s32[2]{0:T(128)S(1)} %copy-done, f32[3]{0:T(128)S(1)} %copy-done.1, ...), custom_call_target="tpu_custom_call" | custom-call | tf_op jit(solution)/shard_map/modulate/pallas_call | solution.py:498
  43.9 1.8 %collective-permute-start.7 = (f32[4,2,32,128]{3,2,1,0:T(8,128)S(1)}, f32[4,2,32,128]{3,2,1,0:T(8,128)S(1)}, u32[]{:S(2)}, u32[]{:S(2)}) collective-permute-start(f32[4,2,32,128]{3,2,1,0:T(8,128)S(1)} %get-tuple-element.8), channel_id=1, source_target_pairs={{0,1},{1,2},{2,3},{3,0},{4,5},{5,6},{6,7},{7,4},{8,9},{9,10},{10,1... | collective-permute-start | bytes 393224 | tf_op jit(solution)/shard_map/ppermute | solution.py:430
  45.8 1.7 %collective-permute-start.8 = (f32[4,2,32,128]{3,2,1,0:T(8,128)S(1)}, f32[4,2,32,128]{3,2,1,0:T(8,128)S(1)}, u32[]{:S(2)}, u32[]{:S(2)}) collective-permute-start(f32[4,2,32,128]{3,2,1,0:T(8,128)S(1)} %get-tuple-element.9), channel_id=1, source_target_pairs={{0,2},{1,3},{2,0},{3,1},{4,6},{5,7},{6,4},{7,5},{8,10},{9,11},{10,... | collective-permute-start | bytes 393224 | tf_op jit(solution)/shard_map/ppermute | solution.py:430
  47.5 2.2 %collective-permute-start.9 = (f32[4,2,32,128]{3,2,1,0:T(8,128)S(1)}, f32[4,2,32,128]{3,2,1,0:T(8,128)S(1)}, u32[]{:S(2)}, u32[]{:S(2)}) collective-permute-start(f32[4,2,32,128]{3,2,1,0:T(8,128)S(1)} %get-tuple-element.10), channel_id=1, source_target_pairs={{0,3},{1,0},{2,1},{3,2},{4,7},{5,4},{6,5},{7,6},{8,11},{9,8},{10,9... | collective-permute-start | bytes 393224 | tf_op jit(solution)/shard_map/ppermute | solution.py:430
  49.7 0.1 slice_reduce_fusion
  49.8 0.7 %reshape_squeeze.3 = f32[4,3]{1,0:T(4,128)} reshape(f32[12]{0:T(128)S(1)} %slice_reduce_fusion) | data formatting | bytes 96 | tf_op jit(solution)/shard_map/reshape;squeeze | solution.py:515
  50.5 0.9 %collective-permute-done.7 = f32[4,2,32,128]{3,2,1,0:T(8,128)S(1)} collective-permute-done((f32[4,2,32,128]{3,2,1,0:T(8,128)S(1)}, f32[4,2,32,128]{3,2,1,0:T(8,128)S(1)}, u32[]{:S(2)}, u32[]{:S(2)}) %collective-permute-start.7) | collective-permute-done | bytes 131104 | tf_op jit(solution)/shard_map/ppermute | solution.py:430
  51.4 4.0 %collective-permute-done.8 = f32[4,2,32,128]{3,2,1,0:T(8,128)S(1)} collective-permute-done((f32[4,2,32,128]{3,2,1,0:T(8,128)S(1)}, f32[4,2,32,128]{3,2,1,0:T(8,128)S(1)}, u32[]{:S(2)}, u32[]{:S(2)}) %collective-permute-start.8) | collective-permute-done | bytes 131104 | tf_op jit(solution)/shard_map/ppermute | solution.py:430
  55.4 0.0 collective-permute-done.9
  55.4 0.7 %add_add_fusion = f32[4,2,32,128]{3,2,1,0:T(8,128)} fusion(f32[4,2,32,128]{3,2,1,0:T(8,128)S(1)} %collective-permute-done.9, f32[4,2,32,128]{3,2,1,0:T(8,128)S(1)} %collective-permute-done.8, f32[4,2,32,128]{3,2,1,0:T(8,128)S(1)} %get-tuple-element.7, f32[4,2,32,128]{3,2,1,0:T(8,128)S(1)} %collective-permute-done.7), kind=kLoop, calls=%fused_computation | loop fusion | flops 98304 | bytes 655360 | tf_op jit(solution)/shard_map/add | solution.py:514
  (4 shorter events, 0.0 us)
Async XLA Ops:
  2.4 1.5 %collective-permute-start = (f32[1,8,128]{2,1,0:T(8,128)}, f32[1,8,128]{2,1,0:T(8,128)S(1)}, u32[]{:S(2)}, u32[]{:S(2)}) collective-permute-start(f32[1,8,128]{2,1,0:T(8,128)} %bitcast.8), channel_id=1, source_target_pairs={{0,4},{4,0},{8,12},{12,8},{16,20},{20,16},{24,28},{28,24},{1,5},{5... | collective-permute-start | bytes 12296 | tf_op jit(solution)/shard_map/ppermute | solution.py:434
  4.6 8.0 %collective-permute-start.3 = (f32[2,8,128]{2,1,0:T(8,128)S(1)}, f32[2,8,128]{2,1,0:T(8,128)S(1)}, u32[]{:S(2)}, u32[]{:S(2)}) collective-permute-start(f32[2,8,128]{2,1,0:T(8,128)S(1)} %pad_maximum_fusion), channel_id=1, source_target_pairs={{0,8},{4,12},{8,0},{12,4},{16,24},{20,28},{24,16},{28,20},{1,9},{5... | collective-permute-start | bytes 24584 | tf_op jit(solution)/shard_map/ppermute | solution.py:434
  7.4 5.1 %collective-permute-start.2 = (f32[2,8,128]{2,1,0:T(8,128)S(1)}, f32[2,8,128]{2,1,0:T(8,128)S(1)}, u32[]{:S(2)}, u32[]{:S(2)}) collective-permute-start(f32[2,8,128]{2,1,0:T(8,128)S(1)} %pad_maximum_fusion), channel_id=1, source_target_pairs={{0,24},{4,28},{8,16},{12,20},{16,8},{20,12},{24,0},{28,4},{1,25},{... | collective-permute-start | bytes 24584 | tf_op jit(solution)/shard_map/ppermute | solution.py:434
  8.9 3.7 %collective-permute-start.1 = (f32[2,8,128]{2,1,0:T(8,128)S(1)}, f32[2,8,128]{2,1,0:T(8,128)S(1)}, u32[]{:S(2)}, u32[]{:S(2)}) collective-permute-start(f32[2,8,128]{2,1,0:T(8,128)S(1)} %pad_maximum_fusion), channel_id=1, source_target_pairs={{0,16},{4,20},{8,24},{12,28},{16,0},{20,4},{24,8},{28,12},{1,17},{... | collective-permute-start | bytes 24584 | tf_op jit(solution)/shard_map/ppermute | solution.py:434
  12.6 28.1 %collective-permute-start.6 = (f32[8,8,128]{2,1,0:T(8,128)S(1)}, f32[8,8,128]{2,1,0:T(8,128)S(1)}, u32[]{:S(2)}, u32[]{:S(2)}) collective-permute-start(f32[8,8,128]{2,1,0:T(8,128)S(1)} %constant_dynamic-update-slice_fusion.refs_0_), channel_id=1, source_target_pairs={{0,1},{1,0},{2,3},{3,2},{4,5},{5,4},{6,7},{7,6},{8,9},{9,8},{10,11... | collective-permute-start | bytes 98312 | tf_op jit(solution)/shard_map/ppermute | solution.py:434
  14.2 26.5 %collective-permute-start.5 = (f32[8,8,128]{2,1,0:T(8,128)S(1)}, f32[8,8,128]{2,1,0:T(8,128)S(1)}, u32[]{:S(2)}, u32[]{:S(2)}) collective-permute-start(f32[8,8,128]{2,1,0:T(8,128)S(1)} %constant_dynamic-update-slice_fusion.refs_0_), channel_id=1, source_target_pairs={{0,3},{1,2},{2,1},{3,0},{4,7},{5,6},{6,5},{7,4},{8,11},{9,10},{10,... | collective-permute-start | bytes 98312 | tf_op jit(solution)/shard_map/ppermute | solution.py:434
  16.7 24.0 %collective-permute-start.4 = (f32[8,8,128]{2,1,0:T(8,128)S(1)}, f32[8,8,128]{2,1,0:T(8,128)S(1)}, u32[]{:S(2)}, u32[]{:S(2)}) collective-permute-start(f32[8,8,128]{2,1,0:T(8,128)S(1)} %constant_dynamic-update-slice_fusion.refs_0_), channel_id=1, source_target_pairs={{0,2},{1,3},{2,0},{3,1},{4,6},{5,7},{6,4},{7,5},{8,10},{9,11},{10,... | collective-permute-start | bytes 98312 | tf_op jit(solution)/shard_map/ppermute | solution.py:434
  16.8 23.9 %copy-start = (s32[2]{0:T(128)S(1)}, s32[2]{0:T(128)}, u32[]{:S(2)}) copy-start(s32[2]{0:T(128)} %bounds_ref.3) | copy-start | bytes 28
  16.8 23.9 %copy-start.1 = (f32[3]{0:T(128)S(1)}, f32[3]{0:T(128)}, u32[]{:S(2)}) copy-start(f32[3]{0:T(128)} %init_ref.1) | copy-start | bytes 40
  43.9 7.5 %collective-permute-start.7 = (f32[4,2,32,128]{3,2,1,0:T(8,128)S(1)}, f32[4,2,32,128]{3,2,1,0:T(8,128)S(1)}, u32[]{:S(2)}, u32[]{:S(2)}) collective-permute-start(f32[4,2,32,128]{3,2,1,0:T(8,128)S(1)} %get-tuple-element.8), channel_id=1, source_target_pairs={{0,1},{1,2},{2,3},{3,0},{4,5},{5,6},{6,7},{7,4},{8,9},{9,10},{10,1... | collective-permute-start | bytes 393224 | tf_op jit(solution)/shard_map/ppermute | solution.py:430
  45.8 9.6 %collective-permute-start.8 = (f32[4,2,32,128]{3,2,1,0:T(8,128)S(1)}, f32[4,2,32,128]{3,2,1,0:T(8,128)S(1)}, u32[]{:S(2)}, u32[]{:S(2)}) collective-permute-start(f32[4,2,32,128]{3,2,1,0:T(8,128)S(1)} %get-tuple-element.9), channel_id=1, source_target_pairs={{0,2},{1,3},{2,0},{3,1},{4,6},{5,7},{6,4},{7,5},{8,10},{9,11},{10,... | collective-permute-start | bytes 393224 | tf_op jit(solution)/shard_map/ppermute | solution.py:430
  47.5 7.9 %collective-permute-start.9 = (f32[4,2,32,128]{3,2,1,0:T(8,128)S(1)}, f32[4,2,32,128]{3,2,1,0:T(8,128)S(1)}, u32[]{:S(2)}, u32[]{:S(2)}) collective-permute-start(f32[4,2,32,128]{3,2,1,0:T(8,128)S(1)} %get-tuple-element.10), channel_id=1, source_target_pairs={{0,3},{1,0},{2,1},{3,2},{4,7},{5,4},{6,5},{7,6},{8,11},{9,8},{10,9... | collective-permute-start | bytes 393224 | tf_op jit(solution)/shard_map/ppermute | solution.py:430
